TPU v7x, 32 devices: a whole 2x2x4 slice. The times are simulated.
32 devices in a mesh: groups: 2 (over y), lon: 16 (over z, x, core).
Axes of the slice: x: 2, y: 2, z: 4, core: 2. Of those that a mesh axis runs over, the one named last changes fastest.
Arguments:
- tokens: bfloat16 [8, 24, 96, 512], P('groups', None, 'lon'), parts along dimension 0, may hold values from -6 to 6
- window_shift: int32 [2, 3], replicated, may hold values from 0 to 11, as said below
- fine_gain: float32 [512], replicated, may hold values from 0.25 to 1.75
- fine_qkv: bfloat16 [512, 1536], replicated
- fine_proj: bfloat16 [512, 512], replicated, may hold values from -0.25 to 0.25
- merge_gain: float32 [2048], replicated, may hold values from 0.25 to 1.75
- merge_weight: bfloat16 [2048, 512], replicated, may hold values from -0.125 to 0.125
- coarse_gain: float32 [512], replicated, may hold values from 0.25 to 1.75
- coarse_qkv: bfloat16 [512, 1536], replicated
- coarse_proj: bfloat16 [512, 512], replicated, may hold values from -0.25 to 0.25
- expand_weight: bfloat16 [512, 2048], replicated, may hold values from -0.25 to 0.25
- expand_gain: float32 [512], replicated, may hold values from 0.25 to 1.75
Outputs:
- forecast_state: bfloat16 [8, 24, 96, 512], P('groups', None, 'lon'), parts along dimension 0
There are 2 independent parts, one for each index of `groups`. A program takes and returns all parts, laid end to end along the dimension named above; an argument that names none is the same for every part. Nothing has to cross between parts.
Inputs may be any that keep to these rules, and one draw needn't show every extreme that they name: window_shift[k] holds offsets 0 to 1, 0 to 5 and 0 to 11 along level, latitude and longitude.
All inputs are finite; a program needn't handle non-finite values.
Results may differ from a plain program's by a relative error of at most 0.013.
Values may be sent and summed in bfloat16 or wider, within the bound.
No kernel may reach another device: no remote copies, remote signals or barrier semaphores. Data moves between devices by JAX's collectives and lax.ppermute only.
A program may use at most 128 MiB of HBM per device.

v0:
```python
import functools

import jax
import jax.numpy as jnp
from jax import lax
from jax.experimental import pallas as pl
from jax.experimental.pallas import tpu as pltpu
from jax.sharding import PartitionSpec as P

HEADS = 8
HC = 8
WIN_LEV = 2
WIN_LAT = 6
WIN_LON = 12
EPSILON = 1e-05
NEG = -1e30
F32 = jnp.float32
BF16 = jnp.bfloat16


def permuted(value, steps):
    count = lax.axis_size("lon")
    return lax.ppermute(value, "lon", [(s, (s + steps) % count) for s in range(count)])


def swapped(value):
    count = lax.axis_size("lon")
    return lax.ppermute(value, "lon", [(s, s ^ 1) for s in range(count)])


def layer_norm(x, gain):
    center = x - jnp.mean(x, axis=-1, keepdims=True)
    spread = jnp.mean(center * center, axis=-1, keepdims=True)
    return center * lax.rsqrt(spread + EPSILON) * gain


def dot(a, b):
    return jnp.dot(a, b, preferred_element_type=F32)


def dot_t(a, b):
    return lax.dot_general(a, b, (((1,), (1,)), ((), ())), preferred_element_type=F32)


def level_of(core, slot, a):
    if slot == 0:
        return 2 * core
    return jnp.where(core == 0, 1 + 2 * a, 3 - 2 * a)


def iota(shape, axis):
    return lax.broadcasted_iota(jnp.int32, shape, axis)


def take(ref, start, count, stride=1):
    at = pl.ds(start, count, stride=stride) if stride > 1 else pl.ds(start, count)
    return jnp.concatenate([ref[k, at, :] for k in range(ref.shape[0])], axis=1)


def put(ref, start, value, stride=1):
    at = pl.ds(start, value.shape[0], stride=stride) if stride > 1 else pl.ds(start, value.shape[0])
    for k in range(ref.shape[0]):
        ref[k, at, :] = value[:, k * 128 : (k + 1) * 128]


def chunked(count, width):
    return pltpu.VMEM((width // 128, count, 128), F32)


def split_kernel(shift_ref, tok_ref, keep_ref, send_ref, scr):
    core = lax.axis_index("lon") % 2
    levels, rows, cols, feats = tok_ref.shape
    a, b = shift_ref[0, 0], shift_ref[0, 1]
    for target, out_ref in ((core, keep_ref), (1 - core, send_ref)):
        for slot in range(2):
            level = level_of(target, slot, a)
            for placed in range(rows):
                source = placed - b
                source = jnp.where(source < 0, source + rows, source)
                put(scr, (placed * 2 + slot) * 8, tok_ref[level, source].astype(F32))
        for col in range(cols):
            out_ref[col] = take(scr, col, rows * 2, 8).astype(BF16)


def head_pair(q, keys, values, picks, bias, scale):
    size = q.shape[0]
    low = iota(q.shape, 1) < q.shape[1] // 2
    zero = jnp.zeros_like(q)
    q2 = jnp.concatenate([jnp.where(low, q, zero), jnp.where(low, zero, q)], axis=0)
    if picks is None:
        scores = dot_t(q2, keys[0])
    else:
        scores = jnp.where(picks, dot_t(q2, keys[0]), dot_t(q2, keys[1]))
    scores = scores + bias
    top = jnp.max(scores, axis=-1, keepdims=True)
    expo = jnp.exp((scores - top) * scale)
    total = jnp.sum(expo, axis=-1, keepdims=True)
    if picks is None:
        mixed = dot(expo.astype(BF16), values[0])
    else:
        none = jnp.zeros_like(expo)
        mixed = dot(jnp.where(picks, expo, none).astype(BF16), values[0]) + dot(
            jnp.where(picks, none, expo).astype(BF16), values[1]
        )
    mixed = mixed / total
    return jnp.where(low, mixed[:size], mixed[size:])


def fine_kernel(
    shift_ref, x_ref, r_ref, gain_ref, qkv_ref, proj_ref, mgain_ref, mw_ref,
    keep_ref, send_ref, coarse_ref,
    xs, rs, qkv, kvr, mix, fu, scr, bias,
):
    core = lax.axis_index("lon") % 2
    cols, depth, feats = x_ref.shape
    rows = depth // 2
    wins = rows // WIN_LAT
    size = WIN_LAT * 2 * cols
    a, b, c = shift_ref[0, 0], shift_ref[0, 1], shift_ref[0, 2]
    for col in range(cols):
        put(xs, col, x_ref[col].astype(F32), cols)
        put(rs, col, r_ref[col].astype(F32), cols)
    gain = gain_ref[...]
    for j in range(wins):
        at = pl.ds(j * size, size)
        normed = layer_norm(take(xs, j * size, size), gain).astype(BF16)
        qkv[at, :] = dot(normed, qkv_ref[...]).astype(BF16)
        normed = layer_norm(take(rs, j * size, size), gain).astype(BF16)
        kvr[at, :] = dot(normed, qkv_ref[:, feats:]).astype(BF16)

    def parts(shape, axis):
        index = iota(shape, axis) % size
        return index // (2 * cols), (index // cols) % 2, index % cols

    full = (2 * size, size)
    q_row, q_slot, q_col = parts(full, 0)
    k_row, k_slot, k_col = parts(full, 1)
    picks = (q_col + c >= cols) == (k_col + c >= cols)
    levels_ok = (q_slot == k_slot) | (a == 0) | (core == 1)
    rows_ok = (q_row < b) == (k_row < b)
    bias[0] = jnp.where(levels_ok & rows_ok, 0.0, NEG)
    bias[1] = jnp.where(levels_ok, 0.0, NEG)
    scale = (feats // HEADS) ** -0.5
    for j in range(wins):
        at = pl.ds(j * size, size)
        for pair in range(feats // 128):
            lanes = pl.ds(pair * 128, 128)
            k_lanes = pl.ds(feats + pair * 128, 128)
            v_lanes = pl.ds(2 * feats + pair * 128, 128)
            mix[at, lanes] = head_pair(
                qkv[at, lanes],
                (qkv[at, k_lanes], kvr[at, lanes]),
                (qkv[at, v_lanes], kvr[at, k_lanes]),
                picks,
                bias[min(j, 1)],
                scale,
            ).astype(BF16)
    half = rows // 2
    unit = 2 * cols
    for j in range(wins):
        at = pl.ds(j * size, size)
        fine = take(xs, j * size, size) + dot(mix[at, :], proj_ref[...])
        fine = fine.astype(BF16).astype(F32)
        for inner in range(WIN_LAT):
            source = j * WIN_LAT + inner - b
            source = jnp.where(source < 0, source + rows, source)
            start = (source % 2) * (half * unit) + (source // 2) * unit
            put(fu, pl.multiple_of(start, 8), fine[inner * unit : (inner + 1) * unit])
    own_cols = cols // 2
    for target, out_ref in ((core, keep_ref), (1 - core, send_ref)):
        for col in range(own_cols):
            put(scr, col, take(fu, target * own_cols + col, depth, cols), 8)
        packed = take(scr, 0, depth * 8).reshape(depth, 8, feats)
        out_ref[...] = packed[:, :own_cols, :].astype(BF16)
    pieces = []
    count = half * unit // 2
    for q in range(2):
        for p in range(2):
            pieces.append(take(fu, p * half * unit + q, count, 2))
    width = 4 * feats
    mean = sum(jnp.sum(piece, axis=-1, keepdims=True) for piece in pieces) / width
    pieces = [piece - mean for piece in pieces]
    spread = sum(jnp.sum(piece * piece, axis=-1, keepdims=True) for piece in pieces) / width
    scaling = lax.rsqrt(spread + EPSILON)
    total = jnp.zeros((count, mw_ref.shape[1]), F32)
    for k, piece in enumerate(pieces):
        merged = (piece * scaling * mgain_ref[k : k + 1, :]).astype(BF16)
        total = total + dot(merged, mw_ref[k * feats : (k + 1) * feats, :])
    coarse_ref[...] = total.astype(BF16)


def coarse_kernel(
    shift_ref, own_ref, l1_ref, r1_ref, l2_ref, r2_ref, gain_ref, qkv_ref, proj_ref,
    out_ref, keys, values, bias, mix, *, own_cols,
):
    place = lax.axis_index("lon")
    core = place % 2
    chips_wide = WIN_LON // own_cols
    side = (place // 2) % chips_wide
    size, feats = own_ref.shape
    a, b, c = shift_ref[1, 0], shift_ref[1, 1], shift_ref[1, 2]
    gain = gain_ref[...]
    refs = (own_ref, l1_ref, r1_ref, l2_ref, r2_ref)
    offsets = (0, -1, 1, -2, 2)
    queries = None
    for n, ref in enumerate(refs):
        at = pl.ds(n * size, size)
        normed = layer_norm(ref[...].astype(F32), gain).astype(BF16)
        if n == 0:
            queries = dot(normed, qkv_ref[:, :feats]).astype(BF16)
        keys[at, :] = dot(normed, qkv_ref[:, feats : 2 * feats]).astype(BF16)
        values[at, :] = dot(normed, qkv_ref[:, 2 * feats :]).astype(BF16)

    def ids(index, offset):
        row = index // (2 * own_cols)
        slot = (index // own_cols) % 2
        col = (side + offset + chips_wide) * own_cols + index % own_cols
        window = (col + c) // WIN_LON
        return ((row + b) // WIN_LAT) * 2 + jnp.where((a == 0) | (core == 1), 0, slot), window

    shape = (2 * size, size)
    q_id, q_win = ids(iota(shape, 0) % size, 0)
    for n, offset in enumerate(offsets):
        k_id, k_win = ids(iota(shape, 1), offset)
        bias[:, n * size : (n + 1) * size] = jnp.where((q_id == k_id) & (q_win == k_win), 0.0, NEG)
    scale = (feats // HC) ** -0.5
    for pair in range(feats // 128):
        lanes = pl.ds(pair * 128, 128)
        mix[:, lanes] = head_pair(
            queries[:, pair * 128 : (pair + 1) * 128],
            (keys[:, lanes],),
            (values[:, lanes],),
            None,
            bias[...],
            scale,
        ).astype(BF16)
    out = own_ref[...].astype(F32) + dot(mix[...], proj_ref[...])
    out_ref[...] = out.astype(BF16)


def expand_kernel(
    shift_ref, own_ref, other_ref, fkeep_ref, fother_ref, gain_ref, weight_ref,
    out_ref, cs, ex, *, own_cols,
):
    core = lax.axis_index("lon") % 2
    size, feats = own_ref.shape
    units = size // own_cols
    home = own_cols // 2
    a1, a2 = shift_ref[0, 0], shift_ref[1, 0]
    crossed = jnp.where(a1 == a2, 0, 1)
    put(cs.at[0], 0, own_ref[...].astype(F32))
    put(cs.at[1], 0, other_ref[...].astype(F32))
    blocks = []
    for which in range(2):
        for col in range(home):
            blocks.append(take(cs.at[which], core * home + col, units, own_cols))
    blocks = jnp.concatenate(blocks, axis=0).astype(BF16)
    gain = gain_ref[...]
    for q in range(2):
        for p in range(2):
            k = 2 * q + p
            piece = layer_norm(dot(blocks, weight_ref[:, k * feats : (k + 1) * feats]), gain)
            for which in range(2):
                for col in range(home):
                    first = (which * home + col) * units
                    put(ex.at[which], p * 8 + 2 * col + q, piece[first : first + units], 16)
    half = units // 2
    for which, (target, f_ref) in enumerate(((core, fkeep_ref), (1 - core, fother_ref))):
        for slot in range(2):
            level = level_of(target, slot, a1)
            source = which if slot == 0 else jnp.where(crossed == 1, 1 - which, which)
            for i in range(half):
                for p in range(2):
                    add = take(ex.at[source], (i * 2 + slot) * 16 + p * 8, 2 * home)
                    fine = f_ref[(p * half + i) * 2 + slot].astype(F32)
                    out_ref[level, 2 * i + p] = (fine + add).astype(BF16)


VMEM_SPEC = pl.BlockSpec(memory_space=pltpu.VMEM)
SMEM_SPEC = pl.BlockSpec(memory_space=pltpu.SMEM)


def call(kernel, name, outs, scratch, arrays, cost=None):
    return pl.pallas_call(
        kernel,
        name=name,
        out_shape=outs,
        in_specs=[SMEM_SPEC] + [VMEM_SPEC] * (len(arrays) - 1),
        out_specs=jax.tree.map(lambda _: VMEM_SPEC, outs),
        scratch_shapes=scratch,
        cost_estimate=cost,
    )(*arrays)


def local(
    tokens,
    window_shift,
    fine_gain,
    fine_qkv,
    fine_proj,
    merge_gain,
    merge_weight,
    coarse_gain,
    coarse_qkv,
    coarse_proj,
    expand_weight,
    expand_gain,
):
    levels, rows, dev_cols, feats = tokens.shape
    cols = 2 * dev_cols
    depth = 2 * rows
    assert levels == 4 and cols == WIN_LON and rows % (2 * WIN_LAT) == 0
    core = lax.axis_index("lon") % 2
    sds = jax.ShapeDtypeStruct
    half = sds((dev_cols, depth, feats), BF16)
    keep, send = call(
        split_kernel, "split", (half, half), [chunked(depth * 8, feats)],
        (window_shift, tokens),
    )
    other = swapped(send)
    grid = jnp.concatenate(
        [jnp.where(core == 0, keep, other), jnp.where(core == 0, other, keep)], axis=0
    )

    def branch(c):
        def run(grid):
            if c == 0:
                return grid
            left = permuted(grid[: cols - c], -2)
            right = permuted(grid[cols - c :], 2)
            return jnp.concatenate([left, right], axis=0)

        return run

    around = lax.switch(window_shift[0, 2], [branch(c) for c in range(WIN_LON)], grid)
    tokens_n = depth * cols
    size = WIN_LAT * 2 * cols
    coarse_n = tokens_n // 4
    channels = merge_weight.shape[1]
    fine_half = sds((depth, dev_cols, feats), BF16)
    fine_keep, fine_send, coarse = call(
        fine_kernel, "fine", (fine_half, fine_half, sds((coarse_n, channels), BF16)),
        [
            chunked(tokens_n, feats),
            chunked(tokens_n, feats),
            pltpu.VMEM((tokens_n, 3 * feats), BF16),
            pltpu.VMEM((tokens_n, 2 * feats), BF16),
            pltpu.VMEM((tokens_n, feats), BF16),
            chunked(tokens_n, feats),
            chunked(depth * 8, feats),
            pltpu.VMEM((2, 2 * size, size), F32),
        ],
        (
            window_shift, grid, around, fine_gain.reshape(1, feats), fine_qkv, fine_proj,
            merge_gain.reshape(4, feats), merge_weight,
        ),
    )
    fine_other = swapped(fine_send)
    coarse_cols = dev_cols
    slot = (jnp.arange(coarse_n, dtype=jnp.int32) // coarse_cols) % 2
    crossed = window_shift[0, 0] != window_shift[1, 0]
    coarse = jnp.where((slot[:, None] == 1) & crossed, swapped(coarse), coarse)
    l1, r1 = permuted(coarse, 2), permuted(coarse, -2)
    l2, r2 = permuted(coarse, 4), permuted(coarse, -4)
    coarse_out = call(
        functools.partial(coarse_kernel, own_cols=coarse_cols), "coarse",
        sds((coarse_n, channels), BF16),
        [
            pltpu.VMEM((5 * coarse_n, channels), BF16),
            pltpu.VMEM((5 * coarse_n, channels), BF16),
            pltpu.VMEM((2 * coarse_n, 5 * coarse_n), F32),
            pltpu.VMEM((coarse_n, channels), BF16),
        ],
        (
            window_shift, coarse, l1, r1, l2, r2, coarse_gain.reshape(1, channels), coarse_qkv,
            coarse_proj,
        ),
    )
    coarse_other = swapped(coarse_out)
    return call(
        functools.partial(expand_kernel, own_cols=coarse_cols), "expand",
        sds(tokens.shape, BF16),
        [
            pltpu.VMEM((2, channels // 128, coarse_n, 128), F32),
            pltpu.VMEM((2, feats // 128, depth // 2 * 16, 128), F32),
        ],
        (
            window_shift, coarse_out, coarse_other, fine_keep, fine_other,
            expand_gain.reshape(1, feats), expand_weight,
        ),
    )


def solution(mesh):
    placed = (P("groups", None, "lon", None), P(), P(), P(), P(), P(), P(), P(), P(), P(), P(), P())
    return jax.shard_map(
        local, mesh=mesh, in_specs=placed, out_specs=P("groups", None, "lon", None), check_vma=False
    )
```

profile of v0, /device:TPU:0, one launch (start us, length us, event | category | flops | bytes accessed | tf_op | source)
XLA Modules:
  0.0 68.8 jit_solution(3327412016454876070)
XLA Ops:
  0.0 2.2 %copy.13.tok_ref = bf16[4,24,6,512]{3,2,1,0:T(8,128)(2,1)} copy(bf16[4,24,6,512]{3,1,2,0:T(8,128)(2,1)} %param.24) | data formatting | bytes 1179648 | tf_op args[0]
  2.2 2.2 %split.1 = (bf16[6,48,512]{2,1,0:T(8,128)(2,1)}, bf16[6,48,512]{2,1,0:T(8,128)(2,1)}) custom-call(s32[2,3]{1,0:T(2,128)} %shift_ref.7, bf16[4,24,6,512]{3,2,1,0:T(8,128)(2,1)} %copy.13.tok_ref), custom_call_target="tpu_custom_call" | custom-call | tf_op jit(solution)/shard_map/split/pallas_call | solution.py:284
  4.4 0.5 collective-permute-start.22
  4.9 0.6 reshape.45.mgain_ref
  5.5 0.6 fusion.1
  6.8 1.0 %broadcast_select_fusion.1 = (bf16[6,48,512]{2,1,0:T(8,128)(2,1)S(1)}, bf16[6,48,512]{2,1,0:T(8,128)(2,1)S(1)}) fusion(bf16[6,48,512]{2,1,0:T(8,128)(2,1)} %get-tuple-element.90, bf16[6,48,512]{2,1,0:T(8,128)(2,1)S(1)} %collective-permute-done.22, pred[]{:T(512)S(6)} %eq.18), kind=kLoop, calls=%fused_computation.13 | loop fusion | flops 294912 | bytes 1179649 | tf_op jit(solution)/shard_map/jit(_where)/select_n | solution.py:322
  7.9 0.1 pad_maximum_fusion.11.x_ref
  7.9 18.7 %conditional.1 = (bf16[12,48,512]{2,1,0:T(8,128)(2,1)S(1)}) conditional(s32[]{:T(128)} %bitcast.1, bf16[12,48,512]{2,1,0:T(8,128)(2,1)S(1)} %pad_maximum_fusion.11.x_ref, (bf16[12,48,512]{2,1,0:T(8,128)(2,1)S(1)}, bf16[6,48,512]{2,1,0:T(8,128)(2,1)S(1)}) %tuple.41, (bf16[12,48,512]{2,1,0:T(8,128)(2,1)S(1)}, ...), branch_computations={%region_0.1_spmd, %region_1.2_spmd, %region_2.3_spmd, %region_3.4_... | conditional | flops 294912 | bytes 4718680 | solution.py:335
  8.0 2.5 %collective-permute-start.21 = (bf16[11,48,512]{2,1,0:T(8,128)(2,1)S(1)}, bf16[11,48,512]{2,1,0:T(8,128)(2,1)S(1)}, u32[]{:S(2)}, u32[]{:S(2)}) collective-permute-start(bf16[11,48,512]{2,1,0:T(8,128)(2,1)S(1)} %slice.65), channel_id=1, source_target_pairs={{0,2},{1,3},{2,4},{3,5},{4,6},{5,7},{6,8},{7,9},{8,10},{9,11},{10,... | collective-permute-start | bytes 1622024 | tf_op jit(solution)/shard_map/cond/branch_11_fun/ppermute | solution.py:23
  10.6 3.1 %collective-permute-start.20 = (bf16[1,48,512]{2,1,0:T(8,128)(2,1)S(1)}, bf16[1,48,512]{2,1,0:T(8,128)(2,1)S(1)}, u32[]{:S(2)}, u32[]{:S(2)}) collective-permute-start(bf16[1,48,512]{2,1,0:T(8,128)(2,1)S(1)} %slice.64), channel_id=1, source_target_pairs={{0,14},{1,15},{2,0},{3,1},{4,2},{5,3},{6,4},{7,5},{8,6},{9,7},{10,... | collective-permute-start | bytes 147464 | tf_op jit(solution)/shard_map/cond/branch_11_fun/ppermute | solution.py:23
  13.7 1.8 %collective-permute-done.20 = bf16[1,48,512]{2,1,0:T(8,128)(2,1)S(1)} collective-permute-done((bf16[1,48,512]{2,1,0:T(8,128)(2,1)S(1)}, bf16[1,48,512]{2,1,0:T(8,128)(2,1)S(1)}, u32[]{:S(2)}, u32[]{:S(2)}) %collective-permute-start.20) | collective-permute-done | bytes 49184 | tf_op jit(solution)/shard_map/cond/branch_11_fun/ppermute | solution.py:23
  15.4 11.1 %collective-permute-done.21 = bf16[11,48,512]{2,1,0:T(8,128)(2,1)S(1)} collective-permute-done((bf16[11,48,512]{2,1,0:T(8,128)(2,1)S(1)}, bf16[11,48,512]{2,1,0:T(8,128)(2,1)S(1)}, u32[]{:S(2)}, u32[]{:S(2)}) %collective-permute-start.21) | collective-permute-done | bytes 540704 | tf_op jit(solution)/shard_map/cond/branch_11_fun/ppermute | solution.py:23
  26.5 0.1 pad_maximum_fusion.10
  26.6 10.0 %fine.1 = (bf16[48,6,512]{2,1,0:T(8,128)(2,1)}, bf16[48,6,512]{2,1,0:T(8,128)(2,1)}, bf16[144,512]{1,0:T(8,128)(2,1)}) custom-call(s32[2,3]{1,0:T(2,128)} %shift_ref.7, bf16[12,48,512]{2,1,0:T(8,128)(2,1)S(1)} %pad_maximum_fusion.11.x_ref, bf16[12,48,512]{2,1,0:T(8,128)(2,1)S(1)} %get-tuple-element.100.r_ref, f32[1,512]{1,0:T(1,128)} %bitcast.5, ...), custom_call_target="tpu_custom_call" | custom-call | tf_op jit(solution)/shard_map/fine/pallas_call | solution.py:284
  36.6 0.0 collective-permute-start.23
  37.9 0.3 collective-permute-done.23
  38.2 1.0 %broadcast_select_fusion.2.own_ref = bf16[144,512]{1,0:T(8,128)(2,1)S(1)} fusion(bf16[144,512]{1,0:T(8,128)(2,1)S(1)} %collective-permute-done.23, bf16[144,512]{1,0:T(8,128)(2,1)} %get-tuple-element.92, pred[144]{0:T(512)(128)(4,1)S(1)} %compare_and_fusion), kind=kLoop, calls=%fused_computation.14 | loop fusion | flops 73728 | bytes 442512 | tf_op jit(solution)/shard_map/jit(_where)/select_n | solution.py:362
  39.2 0.1 collective-permute-start.24
  39.2 4.7 %collective-permute-start.25 = (bf16[144,512]{1,0:T(8,128)(2,1)S(1)}, bf16[144,512]{1,0:T(8,128)(2,1)S(1)}, u32[]{:S(2)}, u32[]{:S(2)}) collective-permute-start(bf16[144,512]{1,0:T(8,128)(2,1)S(1)} %broadcast_select_fusion.2.own_ref), channel_id=1, source_target_pairs={{0,14},{1,15},{2,0},{3,1},{4,2},{5,3},{6,4},{7,5},{8,6},{9,7},{10,... | collective-permute-start | bytes 442376 | tf_op jit(solution)/shard_map/ppermute | solution.py:23
  44.0 0.0 collective-permute-start.26
  44.0 3.8 %collective-permute-start.27 = (bf16[144,512]{1,0:T(8,128)(2,1)S(1)}, bf16[144,512]{1,0:T(8,128)(2,1)S(1)}, u32[]{:S(2)}, u32[]{:S(2)}) collective-permute-start(bf16[144,512]{1,0:T(8,128)(2,1)S(1)} %broadcast_select_fusion.2.own_ref), channel_id=1, source_target_pairs={{0,12},{1,13},{2,14},{3,15},{4,0},{5,1},{6,2},{7,3},{8,4},{9,5},{1... | collective-permute-start | bytes 442376 | tf_op jit(solution)/shard_map/ppermute | solution.py:23
  47.8 1.0 %collective-permute-done.24.l1_ref = bf16[144,512]{1,0:T(8,128)(2,1)S(1)} collective-permute-done((bf16[144,512]{1,0:T(8,128)(2,1)S(1)}, bf16[144,512]{1,0:T(8,128)(2,1)S(1)}, u32[]{:S(2)}, u32[]{:S(2)}) %collective-permute-start.24) | collective-permute-done | bytes 147488 | tf_op jit(solution)/shard_map/ppermute | solution.py:23
  48.8 0.0 collective-permute-done.25.r1_ref
  48.8 3.7 %collective-permute-done.26.l2_ref = bf16[144,512]{1,0:T(8,128)(2,1)S(1)} collective-permute-done((bf16[144,512]{1,0:T(8,128)(2,1)S(1)}, bf16[144,512]{1,0:T(8,128)(2,1)S(1)}, u32[]{:S(2)}, u32[]{:S(2)}) %collective-permute-start.26) | collective-permute-done | bytes 147488 | tf_op jit(solution)/shard_map/ppermute | solution.py:23
  52.5 1.0 %collective-permute-done.27.r2_ref = bf16[144,512]{1,0:T(8,128)(2,1)S(1)} collective-permute-done((bf16[144,512]{1,0:T(8,128)(2,1)S(1)}, bf16[144,512]{1,0:T(8,128)(2,1)S(1)}, u32[]{:S(2)}, u32[]{:S(2)}) %collective-permute-start.27) | collective-permute-done | bytes 147488 | tf_op jit(solution)/shard_map/ppermute | solution.py:23
  53.6 0.6 copy-done.5
  54.2 6.0 %coarse.1.own_ref = bf16[144,512]{1,0:T(8,128)(2,1)} custom-call(s32[2,3]{1,0:T(2,128)} %shift_ref.7, bf16[144,512]{1,0:T(8,128)(2,1)} %copy-done, bf16[144,512]{1,0:T(8,128)(2,1)} %copy-done.2, bf16[144,512]{1,0:T(8,128)(2,1)} %copy-done.3, bf16[144,512]{1,0:T(8,128)(2,1)} %copy-done.4, bf16[144,512]{1,0:T(8,128)(2,1)} %copy-done.5, f32[1,512]{1,0:T(1,128)} %bitcast.6, ...), custom_call_target="tpu_custom_call" | custom-call | tf_op jit(solution)/shard_map/coarse/pallas_call | solution.py:284
  60.2 0.0 collective-permute-start.28
  60.2 1.6 %collective-permute-done.28.other_ref = bf16[144,512]{1,0:T(8,128)(2,1)S(1)} collective-permute-done((bf16[144,512]{1,0:T(8,128)(2,1)}, bf16[144,512]{1,0:T(8,128)(2,1)S(1)}, u32[]{:S(2)}, u32[]{:S(2)}) %collective-permute-start.28) | collective-permute-done | bytes 147488 | tf_op jit(solution)/shard_map/ppermute | solution.py:28
  61.7 0.7 copy-done.6
  62.4 4.3 %expand.1 = bf16[4,24,6,512]{3,2,1,0:T(8,128)(2,1)} custom-call(s32[2,3]{1,0:T(2,128)} %shift_ref.7, bf16[144,512]{1,0:T(8,128)(2,1)} %coarse.1.own_ref, bf16[144,512]{1,0:T(8,128)(2,1)} %copy-done.6, bf16[48,6,512]{2,1,0:T(8,128)(2,1)} %get-tuple-element.93.fkeep_ref, bf16[48,6,512]{2,1,0:T(8,128)(2,1)} %copy-done.1, f32[1,512]{1,0:T(1,128)} %bitcast.7, ...), custom_call_target="tpu_custom_call" | custom-call | tf_op jit(solution)/shard_map/expand/pallas_call | solution.py:284
  66.7 2.1 %copy.14 = bf16[4,24,6,512]{3,1,2,0:T(8,128)(2,1)} copy(bf16[4,24,6,512]{3,2,1,0:T(8,128)(2,1)} %expand.1) | data formatting | bytes 1179648 | tf_op jit(solution)/shard_map/expand/pallas_call | solution.py:284
  (22 shorter events, 0.1 us)
Async XLA Ops:
  0.0 5.5 %copy-start.7 = (s32[2,3]{1,0:T(2,128)S(1)}, s32[2,3]{1,0:T(2,128)}, u32[]{:S(2)}) copy-start(s32[2,3]{1,0:T(2,128)} %shift_ref.7) | copy-start | bytes 76
  0.0 4.9 %copy-start.8 = (f32[2048]{0:T(1024)S(1)}, f32[2048]{0:T(1024)}, u32[]{:S(2)}) copy-start(f32[2048]{0:T(1024)} %param.29) | copy-start | bytes 24580
  4.4 2.4 %collective-permute-start.22 = (bf16[6,48,512]{2,1,0:T(8,128)(2,1)}, bf16[6,48,512]{2,1,0:T(8,128)(2,1)S(1)}, u32[]{:S(2)}, u32[]{:S(2)}) collective-permute-start(bf16[6,48,512]{2,1,0:T(8,128)(2,1)} %get-tuple-element.91), channel_id=1, source_target_pairs={{0,1},{1,0},{2,3},{3,2},{4,5},{5,4},{6,7},{7,6},{8,9},{9,8},{10,11... | collective-permute-start | bytes 884744 | tf_op jit(solution)/shard_map/ppermute | solution.py:28
  8.0 18.5 %collective-permute-start.21 = (bf16[11,48,512]{2,1,0:T(8,128)(2,1)S(1)}, bf16[11,48,512]{2,1,0:T(8,128)(2,1)S(1)}, u32[]{:S(2)}, u32[]{:S(2)}) collective-permute-start(bf16[11,48,512]{2,1,0:T(8,128)(2,1)S(1)} %slice.65), channel_id=1, source_target_pairs={{0,2},{1,3},{2,4},{3,5},{4,6},{5,7},{6,8},{7,9},{8,10},{9,11},{10,... | collective-permute-start | bytes 1622024 | tf_op jit(solution)/shard_map/cond/branch_11_fun/ppermute | solution.py:23
  10.6 4.9 %collective-permute-start.20 = (bf16[1,48,512]{2,1,0:T(8,128)(2,1)S(1)}, bf16[1,48,512]{2,1,0:T(8,128)(2,1)S(1)}, u32[]{:S(2)}, u32[]{:S(2)}) collective-permute-start(bf16[1,48,512]{2,1,0:T(8,128)(2,1)S(1)} %slice.64), channel_id=1, source_target_pairs={{0,14},{1,15},{2,0},{3,1},{4,2},{5,3},{6,4},{7,5},{8,6},{9,7},{10,... | collective-permute-start | bytes 147464 | tf_op jit(solution)/shard_map/cond/branch_11_fun/ppermute | solution.py:23
  36.6 1.6 %collective-permute-start.23 = (bf16[144,512]{1,0:T(8,128)(2,1)}, bf16[144,512]{1,0:T(8,128)(2,1)S(1)}, u32[]{:S(2)}, u32[]{:S(2)}) collective-permute-start(bf16[144,512]{1,0:T(8,128)(2,1)} %get-tuple-element.92), channel_id=1, source_target_pairs={{0,1},{1,0},{2,3},{3,2},{4,5},{5,4},{6,7},{7,6},{8,9},{9,8},{10,11... | collective-permute-start | bytes 442376 | tf_op jit(solution)/shard_map/ppermute | solution.py:28
  39.2 14.4 %copy-start = (bf16[144,512]{1,0:T(8,128)(2,1)}, bf16[144,512]{1,0:T(8,128)(2,1)S(1)}, u32[]{:S(2)}) copy-start(bf16[144,512]{1,0:T(8,128)(2,1)S(1)} %broadcast_select_fusion.2.own_ref) | copy-start | bytes 442372
  39.2 9.6 %collective-permute-start.24 = (bf16[144,512]{1,0:T(8,128)(2,1)S(1)}, bf16[144,512]{1,0:T(8,128)(2,1)S(1)}, u32[]{:S(2)}, u32[]{:S(2)}) collective-permute-start(bf16[144,512]{1,0:T(8,128)(2,1)S(1)} %broadcast_select_fusion.2.own_ref), channel_id=1, source_target_pairs={{0,2},{1,3},{2,4},{3,5},{4,6},{5,7},{6,8},{7,9},{8,10},{9,11},{10,... | collective-permute-start | bytes 442376 | tf_op jit(solution)/shard_map/ppermute | solution.py:23
  39.2 9.6 %collective-permute-start.25 = (bf16[144,512]{1,0:T(8,128)(2,1)S(1)}, bf16[144,512]{1,0:T(8,128)(2,1)S(1)}, u32[]{:S(2)}, u32[]{:S(2)}) collective-permute-start(bf16[144,512]{1,0:T(8,128)(2,1)S(1)} %broadcast_select_fusion.2.own_ref), channel_id=1, source_target_pairs={{0,14},{1,15},{2,0},{3,1},{4,2},{5,3},{6,4},{7,5},{8,6},{9,7},{10,... | collective-permute-start | bytes 442376 | tf_op jit(solution)/shard_map/ppermute | solution.py:23
  44.0 8.6 %collective-permute-start.26 = (bf16[144,512]{1,0:T(8,128)(2,1)S(1)}, bf16[144,512]{1,0:T(8,128)(2,1)S(1)}, u32[]{:S(2)}, u32[]{:S(2)}) collective-permute-start(bf16[144,512]{1,0:T(8,128)(2,1)S(1)} %broadcast_select_fusion.2.own_ref), channel_id=1, source_target_pairs={{0,4},{1,5},{2,6},{3,7},{4,8},{5,9},{6,10},{7,11},{8,12},{9,13},{1... | collective-permute-start | bytes 442376 | tf_op jit(solution)/shard_map/ppermute | solution.py:23
  44.0 9.6 %collective-permute-start.27 = (bf16[144,512]{1,0:T(8,128)(2,1)S(1)}, bf16[144,512]{1,0:T(8,128)(2,1)S(1)}, u32[]{:S(2)}, u32[]{:S(2)}) collective-permute-start(bf16[144,512]{1,0:T(8,128)(2,1)S(1)} %broadcast_select_fusion.2.own_ref), channel_id=1, source_target_pairs={{0,12},{1,13},{2,14},{3,15},{4,0},{5,1},{6,2},{7,3},{8,4},{9,5},{1... | collective-permute-start | bytes 442376 | tf_op jit(solution)/shard_map/ppermute | solution.py:23
  47.8 12.4 %collective-permute-start.29 = (bf16[48,6,512]{2,1,0:T(8,128)(2,1)}, bf16[48,6,512]{2,1,0:T(8,128)(2,1)S(1)}, u32[]{:S(2)}, u32[]{:S(2)}) collective-permute-start(bf16[48,6,512]{2,1,0:T(8,128)(2,1)} %get-tuple-element.94), channel_id=1, source_target_pairs={{0,1},{1,0},{2,3},{3,2},{4,5},{5,4},{6,7},{7,6},{8,9},{9,8},{10,11... | collective-permute-start | bytes 884744 | tf_op jit(solution)/shard_map/ppermute | solution.py:28
  48.8 4.7 %copy-start.2 = (bf16[144,512]{1,0:T(8,128)(2,1)}, bf16[144,512]{1,0:T(8,128)(2,1)S(1)}, u32[]{:S(2)}) copy-start(bf16[144,512]{1,0:T(8,128)(2,1)S(1)} %collective-permute-done.24.l1_ref) | copy-start | bytes 442372
  48.8 4.7 %copy-start.3 = (bf16[144,512]{1,0:T(8,128)(2,1)}, bf16[144,512]{1,0:T(8,128)(2,1)S(1)}, u32[]{:S(2)}) copy-start(bf16[144,512]{1,0:T(8,128)(2,1)S(1)} %collective-permute-done.25.r1_ref) | copy-start | bytes 442372
  52.5 1.0 %copy-start.4 = (bf16[144,512]{1,0:T(8,128)(2,1)}, bf16[144,512]{1,0:T(8,128)(2,1)S(1)}, u32[]{:S(2)}) copy-start(bf16[144,512]{1,0:T(8,128)(2,1)S(1)} %collective-permute-done.26.l2_ref) | copy-start | bytes 442372
  53.5 0.7 copy-start.5
  60.2 1.6 %collective-permute-start.28 = (bf16[144,512]{1,0:T(8,128)(2,1)}, bf16[144,512]{1,0:T(8,128)(2,1)S(1)}, u32[]{:S(2)}, u32[]{:S(2)}) collective-permute-start(bf16[144,512]{1,0:T(8,128)(2,1)} %coarse.1.own_ref), channel_id=1, source_target_pairs={{0,1},{1,0},{2,3},{3,2},{4,5},{5,4},{6,7},{7,6},{8,9},{9,8},{10,11... | collective-permute-start | bytes 442376 | tf_op jit(solution)/shard_map/ppermute | solution.py:28
  60.2 1.6 %copy-start.1 = (bf16[48,6,512]{2,1,0:T(8,128)(2,1)}, bf16[48,6,512]{2,1,0:T(8,128)(2,1)S(1)}, u32[]{:S(2)}) copy-start(bf16[48,6,512]{2,1,0:T(8,128)(2,1)S(1)} %collective-permute-done.29.fother_ref) | copy-start | bytes 884740
  61.7 0.7 copy-start.6
where the time goes:
time: 69.2 us; the launch traced here: 68.8 us
  Pallas kernels  22.5 us (33%)
  waiting for transfers between devices  20.5 us (30%)
  starting transfers between devices  14.7 us (21%)
  local copies, waits for them, and re-layouts  6.92 us (10%)
  other arithmetic  2.13 us (3%)
  between operations  2.03 us (3%)
    pallas_call x4, Pallas kernels, call(): pl.pallas_call(kernel, name=name, out_shape=outs, in_specs=[SMEM_SPEC] +...  22.5 us
    ppermute x6, waiting for transfers between devices, permuted(): lax.ppermute(value, 'lon', [(s, (s + steps) % count) for s in range(count)])  18.6 us
    ppermute x6, starting transfers between devices, permuted(): lax.ppermute(value, 'lon', [(s, (s + steps) % count) for s in range(count)])  14.2 us
    unnamed x19, local copies, waits for them, and re-layouts  3.5 us
    pallas_call x1, local copies, waits for them, and re-layouts, call(): pl.pallas_call(kernel, name=name, out_shape=outs, in_specs=[SMEM_SPEC] +...  2.13 us
    ppermute x4, waiting for transfers between devices, swapped(): return lax.ppermute(value, 'lon', [(s, s ^ 1) for s in range(count)])  1.87 us
  transfers between devices with their start and end apart: 10, of which 7 were waited for; matrix products, arithmetic and copies ran while one was open for 2% of the time, Pallas kernels for 9%

commit v1 on v0

v1 whole, which is shorter than its diff:
```python
import functools

import jax
import jax.numpy as jnp
from jax import lax
from jax.experimental import pallas as pl
from jax.experimental.pallas import tpu as pltpu
from jax.sharding import PartitionSpec as P

HEADS = 8
HC = 8
WIN_LEV = 2
WIN_LAT = 6
WIN_LON = 12
EPSILON = 1e-05
NEG = -1e30
FINE_MIB = 28
COARSE_MIB = 16
EXPAND_MIB = 16
F32 = jnp.float32
BF16 = jnp.bfloat16


def permuted(value, steps):
    count = lax.axis_size("lon")
    return lax.ppermute(value, "lon", [(s, (s + steps) % count) for s in range(count)])


def swapped(value):
    count = lax.axis_size("lon")
    return lax.ppermute(value, "lon", [(s, s ^ 1) for s in range(count)])


def layer_norm(x, gain):
    center = x - jnp.mean(x, axis=-1, keepdims=True)
    spread = jnp.mean(center * center, axis=-1, keepdims=True)
    return center * lax.rsqrt(spread + EPSILON) * gain


def dot(a, b):
    return jnp.dot(a, b, preferred_element_type=F32)


def dot_t(a, b):
    return lax.dot_general(a, b, (((1,), (1,)), ((), ())), preferred_element_type=F32)


def level_of(core, slot, a):
    if slot == 0:
        return 2 * core
    return jnp.where(core == 0, 1 + 2 * a, 3 - 2 * a)


def iota(shape, axis):
    return lax.broadcasted_iota(jnp.int32, shape, axis)


def take(ref, start, count, stride=1):
    at = pl.ds(start, count, stride=stride) if stride > 1 else pl.ds(start, count)
    return jnp.concatenate([ref[k, at, :] for k in range(ref.shape[0])], axis=1)


def put(ref, start, value, stride=1):
    at = pl.ds(start, value.shape[0], stride=stride) if stride > 1 else pl.ds(start, value.shape[0])
    for k in range(ref.shape[0]):
        ref[k, at, :] = value[:, k * 128 : (k + 1) * 128]


def chunked(count, width):
    return pltpu.VMEM((width // 128, count, 128), F32)


def head_pair(q, keys, values, picks, bias, scale):
    size = q.shape[0]
    low = iota(q.shape, 1) < q.shape[1] // 2
    zero = jnp.zeros_like(q)
    q2 = jnp.concatenate([jnp.where(low, q, zero), jnp.where(low, zero, q)], axis=0)
    if picks is None:
        scores = dot_t(q2, keys[0])
    else:
        scores = jnp.where(picks, dot_t(q2, keys[0]), dot_t(q2, keys[1]))
    scores = scores + bias
    top = jnp.max(scores, axis=-1, keepdims=True)
    expo = jnp.exp((scores - top) * scale)
    total = jnp.sum(expo, axis=-1, keepdims=True)
    if picks is None:
        mixed = dot(expo.astype(BF16), values[0])
    else:
        none = jnp.zeros_like(expo)
        mixed = dot(jnp.where(picks, expo, none).astype(BF16), values[0]) + dot(
            jnp.where(picks, none, expo).astype(BF16), values[1]
        )
    mixed = mixed / total
    return jnp.where(low, mixed[:size], mixed[size:])


def fine_kernel(
    shift_ref, x_ref, r_ref, gain_ref, qkv_ref, proj_ref, mgain_ref, mw_ref,
    keep_ref, send_ref, coarse_ref,
    xs, rs, qkv, kvr, mix, fr, fu, bias,
):
    core = lax.axis_index("lon") % 2
    cols, slots, rows, feats = x_ref.shape
    unit = slots * cols
    wins = rows // WIN_LAT
    size = WIN_LAT * unit
    a, b, c = shift_ref[0, 0], shift_ref[0, 1], shift_ref[0, 2]
    for ref, scr in ((x_ref, xs), (r_ref, rs)):
        for col in range(cols):
            for slot in range(slots):
                put(scr, size + slot * cols + col, ref[col, slot].astype(F32), unit)
        put(scr, 0, take(scr, rows * unit, size))
    starts = [pl.multiple_of(((j + 1) * WIN_LAT - b) * unit, 8) for j in range(wins)]
    gain = gain_ref[...]
    for j in range(wins):
        at = pl.ds(j * size, size)
        normed = layer_norm(take(xs, starts[j], size), gain).astype(BF16)
        qkv[at, :] = dot(normed, qkv_ref[...]).astype(BF16)
        normed = layer_norm(take(rs, starts[j], size), gain).astype(BF16)
        kvr[at, :] = dot(normed, qkv_ref[:, feats:]).astype(BF16)

    def parts(index):
        return index // unit, (index // cols) % slots, index % cols

    q_row, q_slot, q_col = parts(iota((2 * size, 1), 0) % size)
    k_row, k_slot, k_col = parts(iota((1, size), 1))
    q_side = jnp.where(q_col + c >= cols, 1, 0)
    k_side = jnp.where(k_col + c >= cols, 1, 0)
    apart = jnp.where((a == 0) | (core == 1), 0, 1)
    q_slot, k_slot = q_slot * apart, k_slot * apart
    q_id = q_slot * 2 + jnp.where(q_row < b, 1, 0)
    k_id = k_slot * 2 + jnp.where(k_row < b, 1, 0)
    bias[0] = jnp.where(q_id == k_id, 0.0, NEG)
    bias[1] = jnp.where(q_slot == k_slot, 0.0, NEG)
    picks = q_side == k_side
    scale = (feats // HEADS) ** -0.5
    for j in range(wins):
        at = pl.ds(j * size, size)
        for pair in range(feats // 128):
            lanes = pl.ds(pair * 128, 128)
            k_lanes = pl.ds(feats + pair * 128, 128)
            v_lanes = pl.ds(2 * feats + pair * 128, 128)
            mix[at, lanes] = head_pair(
                qkv[at, lanes],
                (qkv[at, k_lanes], kvr[at, lanes]),
                (qkv[at, v_lanes], kvr[at, k_lanes]),
                picks,
                bias[min(j, 1)],
                scale,
            ).astype(BF16)
    half = rows // 2
    for j in range(wins):
        at = pl.ds(j * size, size)
        fine = take(xs, starts[j], size) + dot(mix[at, :], proj_ref[...])
        fine = fine.astype(BF16).astype(F32)
        for inner in range(WIN_LAT):
            source = j * WIN_LAT + inner - b
            source = jnp.where(source < 0, source + rows, source)
            put(fr, pl.multiple_of(source * unit, 8), fine[inner * unit : (inner + 1) * unit])
    own_cols = cols // 2
    for slot in range(slots):
        for col in range(own_cols):
            for target, out_ref in ((core, keep_ref), (1 - core, send_ref)):
                start = slot * cols + target * own_cols + col
                out_ref[col, slot] = take(fr, start, rows, unit).astype(BF16)
    for p in range(2):
        for slot in range(slots):
            for col in range(cols):
                first = slot * cols + col
                piece = take(fr, p * unit + first, half, 2 * unit)
                put(fu, (p * slots + slot) * half * cols + col, piece, cols)
    pieces = []
    count = half * unit // 2
    for q in range(2):
        for p in range(2):
            pieces.append(take(fu, p * half * unit + q, count, 2))
    width = 4 * feats
    mean = sum(jnp.sum(piece, axis=-1, keepdims=True) for piece in pieces) / width
    pieces = [piece - mean for piece in pieces]
    spread = sum(jnp.sum(piece * piece, axis=-1, keepdims=True) for piece in pieces) / width
    scaling = lax.rsqrt(spread + EPSILON)
    total = jnp.zeros((count, mw_ref.shape[1]), F32)
    for k, piece in enumerate(pieces):
        lanes = slice(k * feats, (k + 1) * feats)
        merged = (piece * scaling * mgain_ref[:, lanes]).astype(BF16)
        total = total + dot(merged, mw_ref[lanes, :])
    coarse_ref[...] = total.astype(BF16).reshape(coarse_ref.shape)


def coarse_kernel(
    shift_ref, own_ref, l1_ref, r1_ref, l2_ref, r2_ref, gain_ref, qkv_ref, proj_ref,
    out_ref, keys, values, bias, mix, *, own_cols,
):
    place = lax.axis_index("lon")
    core = place % 2
    chips_wide = WIN_LON // own_cols
    side = (place // 2) % chips_wide
    slots, depth, feats = own_ref.shape
    size = slots * depth
    a, b, c = shift_ref[1, 0], shift_ref[1, 1], shift_ref[1, 2]
    gain = gain_ref[...]
    refs = (own_ref, l1_ref, r1_ref, l2_ref, r2_ref)
    offsets = (0, -1, 1, -2, 2)
    queries = None
    for n, ref in enumerate(refs):
        at = pl.ds(n * size, size)
        full = ref[...].astype(F32).reshape(size, feats)
        normed = layer_norm(full, gain).astype(BF16)
        if n == 0:
            queries = dot(normed, qkv_ref[:, :feats]).astype(BF16)
        keys[at, :] = dot(normed, qkv_ref[:, feats : 2 * feats]).astype(BF16)
        values[at, :] = dot(normed, qkv_ref[:, 2 * feats :]).astype(BF16)

    def ids(index, offset):
        slot = index // depth
        row = (index // own_cols) % (depth // own_cols)
        col = (side + offset + chips_wide) * own_cols + index % own_cols
        window = (col + c) // WIN_LON
        apart = jnp.where((a == 0) | (core == 1), 0, slot)
        return (window * 8 + (row + b) // WIN_LAT) * 2 + apart

    q_id = ids(iota((2 * size, 1), 0) % size, 0)
    for n, offset in enumerate(offsets):
        k_id = ids(iota((1, size), 1), offset)
        bias[:, n * size : (n + 1) * size] = jnp.where(q_id == k_id, 0.0, NEG)
    scale = (feats // HC) ** -0.5
    for pair in range(feats // 128):
        lanes = pl.ds(pair * 128, 128)
        mix[:, lanes] = head_pair(
            queries[:, pair * 128 : (pair + 1) * 128],
            (keys[:, lanes],),
            (values[:, lanes],),
            None,
            bias[...],
            scale,
        ).astype(BF16)
    out = own_ref[...].astype(F32).reshape(size, feats) + dot(mix[...], proj_ref[...])
    out_ref[...] = out.astype(BF16).reshape(out_ref.shape)


def expand_kernel(
    shift_ref, own_ref, other_ref, fkeep_ref, fother_ref, gain_ref, weight_ref,
    out_ref, cs, ex, *, own_cols,
):
    core = lax.axis_index("lon") % 2
    slots, depth, feats = own_ref.shape
    size = slots * depth
    units = size // own_cols
    rows = 2 * units // slots
    home = own_cols // 2
    a1, a2 = shift_ref[0, 0], shift_ref[1, 0]
    put(cs.at[0], 0, own_ref[...].astype(F32).reshape(size, feats))
    put(cs.at[1], 0, other_ref[...].astype(F32).reshape(size, feats))
    blocks = []
    for which in range(2):
        for col in range(home):
            blocks.append(take(cs.at[which], core * home + col, units, own_cols))
    blocks = jnp.concatenate(blocks, axis=0).astype(BF16)
    gain = gain_ref[...]
    for q in range(2):
        for p in range(2):
            k = 2 * q + p
            piece = layer_norm(dot(blocks, weight_ref[:, k * feats : (k + 1) * feats]), gain)
            for which in range(2):
                for col in range(home):
                    first = (which * home + col) * units
                    put(ex.at[which, 2 * col + q], p, piece[first : first + units], 2)
    for which, (target, f_ref) in enumerate(((core, fkeep_ref), (1 - core, fother_ref))):
        for slot in range(slots):
            level = level_of(target, slot, a1)
            source = which if slot == 0 else jnp.where(a1 == a2, which, 1 - which)
            for col in range(2 * home):
                add = take(ex.at[source, col], slot * rows, rows)
                out_ref[level, col] = (f_ref[col, slot].astype(F32) + add).astype(BF16)


VMEM_SPEC = pl.BlockSpec(memory_space=pltpu.VMEM)
SMEM_SPEC = pl.BlockSpec(memory_space=pltpu.SMEM)


def call(kernel, name, outs, scratch, arrays, limit):
    return pl.pallas_call(
        kernel,
        name=name,
        out_shape=outs,
        in_specs=[SMEM_SPEC] + [VMEM_SPEC] * (len(arrays) - 1),
        out_specs=jax.tree.map(lambda _: VMEM_SPEC, outs),
        scratch_shapes=scratch,
        compiler_params=pltpu.CompilerParams(vmem_limit_bytes=limit << 20),
    )(*arrays)


def local(
    tokens,
    window_shift,
    fine_gain,
    fine_qkv,
    fine_proj,
    merge_gain,
    merge_weight,
    coarse_gain,
    coarse_qkv,
    coarse_proj,
    expand_weight,
    expand_gain,
):
    levels, rows, dev_cols, feats = tokens.shape
    cols = 2 * dev_cols
    slots = 2
    assert levels == 4 and cols == WIN_LON and rows % (2 * WIN_LAT) == 0
    core = lax.axis_index("lon") % 2
    sds = jax.ShapeDtypeStruct
    viewed = tokens.transpose(0, 2, 1, 3)

    def picked(target):
        levels_in = [
            lax.dynamic_index_in_dim(viewed, level_of(target, slot, window_shift[0, 0]), 0, False)
            for slot in range(slots)
        ]
        return jnp.stack(levels_in, axis=1)

    other = swapped(picked(1 - core))
    keep = picked(core)
    grid = jnp.concatenate(
        [jnp.where(core == 0, keep, other), jnp.where(core == 0, other, keep)], axis=0
    )

    def branch(c):
        def run(grid):
            if c == 0:
                return grid
            left = permuted(grid[: cols - c], -2)
            right = permuted(grid[cols - c :], 2)
            return jnp.concatenate([left, right], axis=0)

        return run

    around = lax.switch(window_shift[0, 2], [branch(c) for c in range(WIN_LON)], grid)
    unit = slots * cols
    tokens_n = rows * unit
    size = WIN_LAT * unit
    channels = merge_weight.shape[1]
    coarse_depth = rows // 2 * dev_cols
    coarse_n = slots * coarse_depth
    coarse_type = sds((slots, coarse_depth, channels), BF16)
    fine_half = sds((dev_cols, slots, rows, feats), BF16)
    fine_keep, fine_send, coarse = call(
        fine_kernel, "fine", (fine_half, fine_half, coarse_type),
        [
            chunked(tokens_n + size, feats),
            chunked(tokens_n + size, feats),
            pltpu.VMEM((tokens_n, 3 * feats), BF16),
            pltpu.VMEM((tokens_n, 2 * feats), BF16),
            pltpu.VMEM((tokens_n, feats), BF16),
            chunked(tokens_n, feats),
            chunked(tokens_n, feats),
            pltpu.VMEM((2, 2 * size, size), F32),
        ],
        (
            window_shift, grid, around, fine_gain.reshape(1, feats), fine_qkv, fine_proj,
            merge_gain.reshape(1, 4 * feats), merge_weight,
        ),
        FINE_MIB,
    )
    fine_other = swapped(fine_send)
    moved = jnp.where(window_shift[0, 0] != window_shift[1, 0], swapped(coarse[1]), coarse[1])
    coarse = jnp.stack([coarse[0], moved])
    l1, r1 = permuted(coarse, 2), permuted(coarse, -2)
    l2, r2 = permuted(coarse, 4), permuted(coarse, -4)
    coarse_out = call(
        functools.partial(coarse_kernel, own_cols=dev_cols), "coarse", coarse_type,
        [
            pltpu.VMEM((5 * coarse_n, channels), BF16),
            pltpu.VMEM((5 * coarse_n, channels), BF16),
            pltpu.VMEM((2 * coarse_n, 5 * coarse_n), F32),
            pltpu.VMEM((coarse_n, channels), BF16),
        ],
        (
            window_shift, coarse, l1, r1, l2, r2, coarse_gain.reshape(1, channels), coarse_qkv,
            coarse_proj,
        ),
        COARSE_MIB,
    )
    coarse_other = swapped(coarse_out)
    out = call(
        functools.partial(expand_kernel, own_cols=dev_cols), "expand",
        sds(viewed.shape, BF16),
        [
            pltpu.VMEM((2, channels // 128, coarse_n, 128), F32),
            pltpu.VMEM((2, dev_cols, feats // 128, slots * rows, 128), F32),
        ],
        (
            window_shift, coarse_out, coarse_other, fine_keep, fine_other,
            expand_gain.reshape(1, feats), expand_weight,
        ),
        EXPAND_MIB,
    )
    return out.transpose(0, 2, 1, 3)


def solution(mesh):
    placed = (P("groups", None, "lon", None), P(), P(), P(), P(), P(), P(), P(), P(), P(), P(), P())
    return jax.shard_map(
        local, mesh=mesh, in_specs=placed, out_specs=P("groups", None, "lon", None), check_vma=False
    )
```

time: 69.2 us -> 59.2 us (0.86)
  Pallas kernels: 22.5 us -> 15.1 us
  local copies, waits for them, and re-layouts: 6.92 us -> 4.08 us
  waiting for transfers between devices: 20.5 us -> 22.4 us
  starting transfers between devices: 14.7 us -> 13.3 us
  other arithmetic: 2.13 us -> 1.02 us
  between operations: 2.03 us -> 2.83 us
    pallas_call x4 -> x3, Pallas kernels: 22.5 us -> 15.1 us  [call(): pl.pallas_call(kernel, name=name, out_shape=outs, in_specs=[SMEM_SPEC] +...]
    pallas_call x1 -> x0, local copies, waits for them, and re-layouts: 2.13 us -> none  [call(): pl.pallas_call(kernel, name=name, out_shape=outs, in_specs=[SMEM_SPEC] +...]
    unnamed x19 -> x22, local copies, waits for them, and re-layouts: 3.5 us -> 1.46 us
    ppermute x6, waiting for transfers between devices: 18.6 us -> 20.5 us  [permuted(): lax.ppermute(value, 'lon', [(s, (s + steps) % count) for s in range(count)])]
    ppermute x6, starting transfers between devices: 14.2 us -> 12.6 us  [permuted(): lax.ppermute(value, 'lon', [(s, (s + steps) % count) for s in range(count)])]
    another operation x0 -> x1, local copies, waits for them, and re-layouts: none -> 1.17 us  [picked(): return jnp.stack(levels_in, axis=1)]
    select_n x1 -> x0, other arithmetic: 1 us -> none  [local(): coarse = jnp.where((slot[:, None] == 1) & crossed, swapped(coarse), coarse)]
    select_n x1, other arithmetic: 1.01 us -> 0.04 us  [local(): jnp.where(core == 0, keep, other)]
  transfers between devices with their start and end apart: 10 -> 10, of which waited for: 7 -> 8; matrix products, arithmetic and copies ran while one was open for 2% -> 0% of each run, Pallas kernels for 9% -> 7%
where the time goes in v1:
time: 59.2 us; the launch traced here: 58.9 us
  waiting for transfers between devices  22.4 us (38%)
  Pallas kernels  15.1 us (26%)
  starting transfers between devices  13.3 us (22%)
  local copies, waits for them, and re-layouts  4.08 us (7%)
  between operations  2.83 us (5%)
  other arithmetic  1.02 us (2%)
    ppermute x6, waiting for transfers between devices, permuted(): lax.ppermute(value, 'lon', [(s, (s + steps) % count) for s in range(count)])  20.5 us
    pallas_call x3, Pallas kernels, call(): pl.pallas_call(kernel, name=name, out_shape=outs, in_specs=[SMEM_SPEC] +...  15.1 us
    ppermute x6, starting transfers between devices, permuted(): lax.ppermute(value, 'lon', [(s, (s + steps) % count) for s in range(count)])  12.6 us
    ppermute x4, waiting for transfers between devices, swapped(): return lax.ppermute(value, 'lon', [(s, s ^ 1) for s in range(count)])  1.91 us
    unnamed x22, local copies, waits for them, and re-layouts  1.46 us
    slice x1, local copies, waits for them, and re-layouts, local(): window_shift[1, 0]  1.4 us
  transfers between devices with their start and end apart: 10, of which 8 were waited for; matrix products, arithmetic and copies ran while one was open for 0% of the time, Pallas kernels for 7%

profile of v1, /device:TPU:0, one launch (start us, length us, event | category | flops | bytes accessed | tf_op | source)
XLA Modules:
  0.0 58.9 jit_solution(948975398292189045)
XLA Ops:
  0.0 1.4 %fusion.1 = (s32[1,1]{1,0:T(1,128)}, s32[1,1]{1,0:T(1,128)}, s32[1,1]{1,0:T(1,128)}) fusion(s32[2,3]{1,0:T(2,128)} %shift_ref.5), kind=kLoop, calls=%fused_computation.24 | loop fusion | bytes 24 | tf_op jit(solution)/shard_map/slice | solution.py:366
  2.1 1.2 %dynamic-slice_bitcast_fusion.3 = (bf16[6,1,24,512]{3,2,1,0:T(8,128)(2,1)S(1)}, bf16[6,1,24,512]{3,2,1,0:T(8,128)(2,1)S(1)}, bf16[6,1,24,512]{3,2,1,0:T(8,128)(2,1)S(1)}, bf16[6,1,24,512]{3,2,1,0:T(8,128)(2,1)S(1)}) fusion(bf16[4,24,6,512]{3,1,2,0:T(8,128)(2,1)} %param.24, s32[]{:T(128)S(6)} %select_n.48, s32[]{:T(128)S(6)} %select_n.50, s32[]{:T(128)S(6)} %select_n.53, ...), kind=kLoop, calls=%fused_computation.20 | loop fusion | bytes 1179664 | tf_op jit(solution)/shard_map/stack | solution.py:320
  3.3 0.6 collective-permute-start.22
  4.5 0.6 collective-permute-done.22
  5.1 0.1 pad_maximum_fusion.11.x_ref
  5.2 0.0 copy-start.1
  5.2 0.0 copy-start.5
  5.2 0.0 copy-start.6
  5.2 0.0 copy-start.7
  5.2 0.0 copy-start.9
  5.2 19.6 %conditional.1 = (bf16[12,2,24,512]{3,2,1,0:T(8,128)(2,1)}) conditional(s32[]{:T(128)} %bitcast.10, bf16[12,2,24,512]{3,2,1,0:T(8,128)(2,1)S(1)} %pad_maximum_fusion.11.x_ref, (bf16[12,2,24,512]{3,2,1,0:T(8,128)(2,1)S(1)}, bf16[6,2,24,512]{3,2,1,0:T(8,128)(2,1)S(1)}) %tuple.41, ...), branch_computations={%region_0.1_spmd, %region_1.2_spmd, %region_2.3_spmd, %region_3.4_... | conditional | flops 294912 | bytes 4718680 | solution.py:338
  5.3 2.9 %collective-permute-start.21 = (bf16[11,2,24,512]{3,2,1,0:T(8,128)(2,1)S(1)}, bf16[11,2,24,512]{3,2,1,0:T(8,128)(2,1)S(1)}, u32[]{:S(2)}, u32[]{:S(2)}) collective-permute-start(bf16[11,2,24,512]{3,2,1,0:T(8,128)(2,1)S(1)} %slice.72), channel_id=1, source_target_pairs={{0,2},{1,3},{2,4},{3,5},{4,6},{5,7},{6,8},{7,9},{8,10},{9,11},{10,... | collective-permute-start | bytes 1622024 | tf_op jit(solution)/shard_map/cond/branch_11_fun/ppermute | solution.py:26
  8.2 3.1 %collective-permute-start.20 = (bf16[1,2,24,512]{3,2,1,0:T(8,128)(2,1)S(1)}, bf16[1,2,24,512]{3,2,1,0:T(8,128)(2,1)S(1)}, u32[]{:S(2)}, u32[]{:S(2)}) collective-permute-start(bf16[1,2,24,512]{3,2,1,0:T(8,128)(2,1)S(1)} %slice.71), channel_id=1, source_target_pairs={{0,14},{1,15},{2,0},{3,1},{4,2},{5,3},{6,4},{7,5},{8,6},{9,7},{10,... | collective-permute-start | bytes 147464 | tf_op jit(solution)/shard_map/cond/branch_11_fun/ppermute | solution.py:26
  11.3 1.8 %collective-permute-done.20 = bf16[1,2,24,512]{3,2,1,0:T(8,128)(2,1)S(1)} collective-permute-done((bf16[1,2,24,512]{3,2,1,0:T(8,128)(2,1)S(1)}, bf16[1,2,24,512]{3,2,1,0:T(8,128)(2,1)S(1)}, u32[]{:S(2)}, u32[]{:S(2)}) %collective-permute-start.20) | collective-permute-done | bytes 49184 | tf_op jit(solution)/shard_map/cond/branch_11_fun/ppermute | solution.py:26
  13.1 10.8 %collective-permute-done.21 = bf16[11,2,24,512]{3,2,1,0:T(8,128)(2,1)S(1)} collective-permute-done((bf16[11,2,24,512]{3,2,1,0:T(8,128)(2,1)S(1)}, bf16[11,2,24,512]{3,2,1,0:T(8,128)(2,1)S(1)}, u32[]{:S(2)}, u32[]{:S(2)}) %collective-permute-start.21) | collective-permute-done | bytes 540704 | tf_op jit(solution)/shard_map/cond/branch_11_fun/ppermute | solution.py:26
  23.9 0.9 %pad_maximum_fusion.10 = bf16[12,2,24,512]{3,2,1,0:T(8,128)(2,1)} fusion(bf16[11,2,24,512]{3,2,1,0:T(8,128)(2,1)S(1)} %collective-permute-done.21, bf16[1,2,24,512]{3,2,1,0:T(8,128)(2,1)S(1)} %collective-permute-done.20), kind=kLoop, calls=%fused_computation.10 | loop fusion | flops 294912 | bytes 1179648 | tf_op jit(solution)/shard_map/cond/branch_11_fun/concatenate | solution.py:334
  24.8 0.0 copy-start.3
  24.8 1.4 %copy-done.3 = bf16[512,1536]{1,0:T(8,128)(2,1)S(1)} copy-done((bf16[512,1536]{1,0:T(8,128)(2,1)S(1)}, bf16[512,1536]{1,0:T(8,128)(2,1)}, u32[]{:S(2)}) %copy-start.3) | copy-done | bytes 1572888
  26.2 9.0 %fine.1 = (bf16[6,2,24,512]{3,2,1,0:T(8,128)(2,1)S(1)}, bf16[6,2,24,512]{3,2,1,0:T(8,128)(2,1)S(1)}, bf16[2,72,512]{2,1,0:T(8,128)(2,1)S(1)}) custom-call(s32[2,3]{1,0:T(2,128)S(1)} %copy-done.6, bf16[12,2,24,512]{3,2,1,0:T(8,128)(2,1)S(1)} %pad_maximum_fusion.11.x_ref, bf16[12,2,24,512]{3,2,1,0:T(8,128)(2,1)} %get-tuple-element.102.r_ref, ...), custom_call_target="tpu_custom_call" | custom-call | tf_op jit(solution)/shard_map/fine/pallas_call | solution.py:282
  35.2 0.0 copy-start
  35.3 0.0 copy-start.8
  35.3 0.1 collective-permute-start.23
  36.7 2.8 %collective-permute-start.27 = (bf16[2,72,512]{2,1,0:T(8,128)(2,1)S(1)}, bf16[2,72,512]{2,1,0:T(8,128)(2,1)S(1)}, u32[]{:S(2)}, u32[]{:S(2)}) collective-permute-start(bf16[2,72,512]{2,1,0:T(8,128)(2,1)S(1)} %pad_maximum_fusion.14.own_ref), channel_id=1, source_target_pairs={{0,12},{1,13},{2,14},{3,15},{4,0},{5,1},{6,2},{7,3},{8,4},{9,5},{1... | collective-permute-start | bytes 442376 | tf_op jit(solution)/shard_map/ppermute | solution.py:26
  39.5 3.8 %collective-permute-start.25 = (bf16[2,72,512]{2,1,0:T(8,128)(2,1)S(1)}, bf16[2,72,512]{2,1,0:T(8,128)(2,1)S(1)}, u32[]{:S(2)}, u32[]{:S(2)}) collective-permute-start(bf16[2,72,512]{2,1,0:T(8,128)(2,1)S(1)} %pad_maximum_fusion.14.own_ref), channel_id=1, source_target_pairs={{0,14},{1,15},{2,0},{3,1},{4,2},{5,3},{6,4},{7,5},{8,6},{9,7},{10,... | collective-permute-start | bytes 442376 | tf_op jit(solution)/shard_map/ppermute | solution.py:26
  43.4 0.4 collective-permute-done.27.r2_ref
  43.8 4.3 %collective-permute-done.26.l2_ref = bf16[2,72,512]{2,1,0:T(8,128)(2,1)S(1)} collective-permute-done((bf16[2,72,512]{2,1,0:T(8,128)(2,1)S(1)}, bf16[2,72,512]{2,1,0:T(8,128)(2,1)S(1)}, u32[]{:S(2)}, u32[]{:S(2)}) %collective-permute-start.26) | collective-permute-done | bytes 147488 | tf_op jit(solution)/shard_map/ppermute | solution.py:26
  48.1 1.5 %collective-permute-done.25.r1_ref = bf16[2,72,512]{2,1,0:T(8,128)(2,1)S(1)} collective-permute-done((bf16[2,72,512]{2,1,0:T(8,128)(2,1)S(1)}, bf16[2,72,512]{2,1,0:T(8,128)(2,1)S(1)}, u32[]{:S(2)}, u32[]{:S(2)}) %collective-permute-start.25) | collective-permute-done | bytes 147488 | tf_op jit(solution)/shard_map/ppermute | solution.py:26
  49.5 1.8 %collective-permute-done.24.l1_ref = bf16[2,72,512]{2,1,0:T(8,128)(2,1)S(1)} collective-permute-done((bf16[2,72,512]{2,1,0:T(8,128)(2,1)S(1)}, bf16[2,72,512]{2,1,0:T(8,128)(2,1)S(1)}, u32[]{:S(2)}, u32[]{:S(2)}) %collective-permute-start.24) | collective-permute-done | bytes 147488 | tf_op jit(solution)/shard_map/ppermute | solution.py:26
  51.3 3.9 %coarse.1.own_ref = bf16[2,72,512]{2,1,0:T(8,128)(2,1)S(1)} custom-call(s32[2,3]{1,0:T(2,128)S(1)} %copy-done.6, bf16[2,72,512]{2,1,0:T(8,128)(2,1)S(1)} %pad_maximum_fusion.14.own_ref, bf16[2,72,512]{2,1,0:T(8,128)(2,1)S(1)} %collective-permute-done.24.l1_ref, bf16[2,72,512]{2,1,0:T(8,128)(2,1)S(1)} %collective-permute-done.25.r1_ref, ...), custom_call_target="tpu_custom_call" | custom-call | tf_op jit(solution)/shard_map/coarse/pallas_call | solution.py:282
  55.2 0.1 collective-permute-start.28
  55.3 1.3 %collective-permute-done.28.other_ref = bf16[2,72,512]{2,1,0:T(8,128)(2,1)S(1)} collective-permute-done((bf16[2,72,512]{2,1,0:T(8,128)(2,1)S(1)}, bf16[2,72,512]{2,1,0:T(8,128)(2,1)S(1)}, u32[]{:S(2)}, u32[]{:S(2)}) %collective-permute-start.28) | collective-permute-done | bytes 147488 | tf_op jit(solution)/shard_map/ppermute | solution.py:31
  56.6 2.3 %expand.1 = bf16[4,6,24,512]{3,2,1,0:T(8,128)(2,1)} custom-call(s32[2,3]{1,0:T(2,128)S(1)} %copy-done.6, bf16[2,72,512]{2,1,0:T(8,128)(2,1)S(1)} %coarse.1.own_ref, bf16[2,72,512]{2,1,0:T(8,128)(2,1)S(1)} %collective-permute-done.28.other_ref, bf16[6,2,24,512]{3,2,1,0:T(8,128)(2,1)S(1)} %get-tuple-element.89.fkeep_ref, ...), custom_call_target="tpu_custom_call" | custom-call | tf_op jit(solution)/shard_map/expand/pallas_call | solution.py:282
  (25 shorter events, 0.2 us)
Async XLA Ops:
  3.3 1.8 %collective-permute-start.22 = (bf16[6,2,24,512]{3,2,1,0:T(8,128)(2,1)S(1)}, bf16[6,2,24,512]{3,2,1,0:T(8,128)(2,1)S(1)}, u32[]{:S(2)}, u32[]{:S(2)}) collective-permute-start(bf16[6,2,24,512]{3,2,1,0:T(8,128)(2,1)S(1)} %pad_maximum_fusion.13), channel_id=1, source_target_pairs={{0,1},{1,0},{2,3},{3,2},{4,5},{5,4},{6,7},{7,6},{8,9},{9,8},{10,11... | collective-permute-start | bytes 884744 | tf_op jit(solution)/shard_map/ppermute | solution.py:31
  5.2 19.6 %copy-start.1 = (bf16[2048,512]{1,0:T(8,128)(2,1)S(1)}, bf16[2048,512]{1,0:T(8,128)(2,1)}, u32[]{:S(2)}) copy-start(bf16[2048,512]{1,0:T(8,128)(2,1)} %mw_ref.1) | copy-start | bytes 6291460
  5.2 19.6 %copy-start.5 = (bf16[512,512]{1,0:T(8,128)(2,1)S(1)}, bf16[512,512]{1,0:T(8,128)(2,1)}, u32[]{:S(2)}) copy-start(bf16[512,512]{1,0:T(8,128)(2,1)} %proj_ref.2) | copy-start | bytes 1572868
  5.2 19.6 %copy-start.6 = (s32[2,3]{1,0:T(2,128)S(1)}, s32[2,3]{1,0:T(2,128)}, u32[]{:S(2)}) copy-start(s32[2,3]{1,0:T(2,128)} %shift_ref.5) | copy-start | bytes 76
  5.2 19.6 %copy-start.7 = (f32[2048]{0:T(1024)S(1)}, f32[2048]{0:T(1024)}, u32[]{:S(2)}) copy-start(f32[2048]{0:T(1024)} %param.29) | copy-start | bytes 24580
  5.2 19.6 %copy-start.9 = (f32[512]{0:T(512)S(1)}, f32[512]{0:T(512)}, u32[]{:S(2)}) copy-start(f32[512]{0:T(512)} %param.26) | copy-start | bytes 6148
  5.3 18.6 %collective-permute-start.21 = (bf16[11,2,24,512]{3,2,1,0:T(8,128)(2,1)S(1)}, bf16[11,2,24,512]{3,2,1,0:T(8,128)(2,1)S(1)}, u32[]{:S(2)}, u32[]{:S(2)}) collective-permute-start(bf16[11,2,24,512]{3,2,1,0:T(8,128)(2,1)S(1)} %slice.72), channel_id=1, source_target_pairs={{0,2},{1,3},{2,4},{3,5},{4,6},{5,7},{6,8},{7,9},{8,10},{9,11},{10,... | collective-permute-start | bytes 1622024 | tf_op jit(solution)/shard_map/cond/branch_11_fun/ppermute | solution.py:26
  8.2 4.9 %collective-permute-start.20 = (bf16[1,2,24,512]{3,2,1,0:T(8,128)(2,1)S(1)}, bf16[1,2,24,512]{3,2,1,0:T(8,128)(2,1)S(1)}, u32[]{:S(2)}, u32[]{:S(2)}) collective-permute-start(bf16[1,2,24,512]{3,2,1,0:T(8,128)(2,1)S(1)} %slice.71), channel_id=1, source_target_pairs={{0,14},{1,15},{2,0},{3,1},{4,2},{5,3},{6,4},{7,5},{8,6},{9,7},{10,... | collective-permute-start | bytes 147464 | tf_op jit(solution)/shard_map/cond/branch_11_fun/ppermute | solution.py:26
  24.8 1.4 %copy-start.3 = (bf16[512,1536]{1,0:T(8,128)(2,1)S(1)}, bf16[512,1536]{1,0:T(8,128)(2,1)}, u32[]{:S(2)}) copy-start(bf16[512,1536]{1,0:T(8,128)(2,1)} %qkv_ref.2) | copy-start | bytes 4718596
  26.2 25.1 %copy-start.2 = (bf16[512,1536]{1,0:T(8,128)(2,1)S(1)}, bf16[512,1536]{1,0:T(8,128)(2,1)}, u32[]{:S(2)}) copy-start(bf16[512,1536]{1,0:T(8,128)(2,1)} %qkv_ref.3) | copy-start | bytes 4718596
  26.2 25.1 %copy-start.4 = (bf16[512,512]{1,0:T(8,128)(2,1)S(1)}, bf16[512,512]{1,0:T(8,128)(2,1)}, u32[]{:S(2)}) copy-start(bf16[512,512]{1,0:T(8,128)(2,1)} %proj_ref.3) | copy-start | bytes 1572868
  26.2 25.1 %copy-start.10 = (f32[512]{0:T(512)S(1)}, f32[512]{0:T(512)}, u32[]{:S(2)}) copy-start(f32[512]{0:T(512)} %param.31) | copy-start | bytes 6148
  35.2 21.4 %copy-start = (bf16[512,2048]{1,0:T(8,128)(2,1)S(1)}, bf16[512,2048]{1,0:T(8,128)(2,1)}, u32[]{:S(2)}) copy-start(bf16[512,2048]{1,0:T(8,128)(2,1)} %weight_ref.1) | copy-start | bytes 6291460
  35.3 21.4 %copy-start.8 = (f32[512]{0:T(512)S(1)}, f32[512]{0:T(512)}, u32[]{:S(2)}) copy-start(f32[512]{0:T(512)} %param.35) | copy-start | bytes 6148
  35.3 1.4 %collective-permute-start.23 = (bf16[72,512]{1,0:T(8,128)(2,1)S(1)}, bf16[72,512]{1,0:T(8,128)(2,1)S(1)}, u32[]{:S(2)}, u32[]{:S(2)}) collective-permute-start(bf16[72,512]{1,0:T(8,128)(2,1)S(1)} %get-tuple-element.98), channel_id=1, source_target_pairs={{0,1},{1,0},{2,3},{3,2},{4,5},{5,4},{6,7},{7,6},{8,9},{9,8},{10,11... | collective-permute-start | bytes 221192 | tf_op jit(solution)/shard_map/ppermute | solution.py:31
  36.7 7.0 %collective-permute-start.27 = (bf16[2,72,512]{2,1,0:T(8,128)(2,1)S(1)}, bf16[2,72,512]{2,1,0:T(8,128)(2,1)S(1)}, u32[]{:S(2)}, u32[]{:S(2)}) collective-permute-start(bf16[2,72,512]{2,1,0:T(8,128)(2,1)S(1)} %pad_maximum_fusion.14.own_ref), channel_id=1, source_target_pairs={{0,12},{1,13},{2,14},{3,15},{4,0},{5,1},{6,2},{7,3},{8,4},{9,5},{1... | collective-permute-start | bytes 442376 | tf_op jit(solution)/shard_map/ppermute | solution.py:26
  39.5 8.6 %collective-permute-start.26 = (bf16[2,72,512]{2,1,0:T(8,128)(2,1)S(1)}, bf16[2,72,512]{2,1,0:T(8,128)(2,1)S(1)}, u32[]{:S(2)}, u32[]{:S(2)}) collective-permute-start(bf16[2,72,512]{2,1,0:T(8,128)(2,1)S(1)} %pad_maximum_fusion.14.own_ref), channel_id=1, source_target_pairs={{0,4},{1,5},{2,6},{3,7},{4,8},{5,9},{6,10},{7,11},{8,12},{9,13},{1... | collective-permute-start | bytes 442376 | tf_op jit(solution)/shard_map/ppermute | solution.py:26
  39.5 10.0 %collective-permute-start.25 = (bf16[2,72,512]{2,1,0:T(8,128)(2,1)S(1)}, bf16[2,72,512]{2,1,0:T(8,128)(2,1)S(1)}, u32[]{:S(2)}, u32[]{:S(2)}) collective-permute-start(bf16[2,72,512]{2,1,0:T(8,128)(2,1)S(1)} %pad_maximum_fusion.14.own_ref), channel_id=1, source_target_pairs={{0,14},{1,15},{2,0},{3,1},{4,2},{5,3},{6,4},{7,5},{8,6},{9,7},{10,... | collective-permute-start | bytes 442376 | tf_op jit(solution)/shard_map/ppermute | solution.py:26
  43.3 8.0 %collective-permute-start.24 = (bf16[2,72,512]{2,1,0:T(8,128)(2,1)S(1)}, bf16[2,72,512]{2,1,0:T(8,128)(2,1)S(1)}, u32[]{:S(2)}, u32[]{:S(2)}) collective-permute-start(bf16[2,72,512]{2,1,0:T(8,128)(2,1)S(1)} %pad_maximum_fusion.14.own_ref), channel_id=1, source_target_pairs={{0,2},{1,3},{2,4},{3,5},{4,6},{5,7},{6,8},{7,9},{8,10},{9,11},{10,... | collective-permute-start | bytes 442376 | tf_op jit(solution)/shard_map/ppermute | solution.py:26
  43.3 11.9 %collective-permute-start.29 = (bf16[6,2,24,512]{3,2,1,0:T(8,128)(2,1)S(1)}, bf16[6,2,24,512]{3,2,1,0:T(8,128)(2,1)S(1)}, u32[]{:S(2)}, u32[]{:S(2)}) collective-permute-start(bf16[6,2,24,512]{3,2,1,0:T(8,128)(2,1)S(1)} %get-tuple-element.90), channel_id=1, source_target_pairs={{0,1},{1,0},{2,3},{3,2},{4,5},{5,4},{6,7},{7,6},{8,9},{9,8},{10,11... | collective-permute-start | bytes 884744 | tf_op jit(solution)/shard_map/ppermute | solution.py:31
  55.2 1.4 %collective-permute-start.28 = (bf16[2,72,512]{2,1,0:T(8,128)(2,1)S(1)}, bf16[2,72,512]{2,1,0:T(8,128)(2,1)S(1)}, u32[]{:S(2)}, u32[]{:S(2)}) collective-permute-start(bf16[2,72,512]{2,1,0:T(8,128)(2,1)S(1)} %coarse.1.own_ref), channel_id=1, source_target_pairs={{0,1},{1,0},{2,3},{3,2},{4,5},{5,4},{6,7},{7,6},{8,9},{9,8},{10,11... | collective-permute-start | bytes 442376 | tf_op jit(solution)/shard_map/ppermute | solution.py:31

commit v2 on v1

--- a/solution.py
+++ b/solution.py
@@ -14,7 +14,8 @@
 WIN_LON = 12
 EPSILON = 1e-05
 NEG = -1e30
-FINE_MIB = 28
+OWN_MIB = 8
+FINE_MIB = 24
 COARSE_MIB = 16
 EXPAND_MIB = 16
 F32 = jnp.float32
@@ -94,31 +95,87 @@
     return jnp.where(low, mixed[:size], mixed[size:])
 
 
+def split_kernel(shift_ref, tok_ref, keep_ref, send_ref, branch_ref, sems):
+    core = lax.axis_index("lon") % 2
+    a = shift_ref[0, 0]
+    copies = []
+    for n, (target, out_ref) in enumerate(((1 - core, send_ref), (core, keep_ref))):
+        for slot in range(2):
+            copies.append(
+                pltpu.make_async_copy(
+                    tok_ref.at[level_of(target, slot, a)], out_ref.at[:, slot], sems.at[n, slot]
+                )
+            )
+    for copy in copies:
+        copy.start()
+    branch_ref[0] = shift_ref[0, 2]
+    branch_ref[1] = jnp.where(a == shift_ref[1, 0], 0, 1)
+    for copy in copies:
+        copy.wait()
+
+
+def by_window(columns, scr):
+    cols, slots = len(columns), 2
+    unit = slots * cols
+    size = WIN_LAT * unit
+    for col, read in enumerate(columns):
+        for slot in range(slots):
+            put(scr, size + slot * cols + col, read(slot), unit)
+    put(scr, 0, take(scr, scr.shape[1] - size, size))
+
+
+def reader(ref, col):
+    return lambda slot: ref[col, slot].astype(F32)
+
+
+def own_kernel(shift_ref, x_ref, gain_ref, qkv_ref, xw_ref, out_ref, xs):
+    cols, slots, rows, feats = x_ref.shape
+    unit = slots * cols
+    size = WIN_LAT * unit
+    b = shift_ref[0, 1]
+    by_window([reader(x_ref, col) for col in range(cols)], xs)
+    gain = gain_ref[...]
+
+    @pl.loop(0, rows // WIN_LAT)
+    def _(j):
+        at = pl.ds(pl.multiple_of(j * size, size), size)
+        tokens = take(xs, pl.multiple_of(((j + 1) * WIN_LAT - b) * unit, 8), size)
+        xw_ref[at, :] = tokens.astype(BF16)
+        normed = layer_norm(tokens, gain).astype(BF16)
+        out_ref[at, :] = dot(normed, qkv_ref[...]).astype(BF16)
+
+
 def fine_kernel(
-    shift_ref, x_ref, r_ref, gain_ref, qkv_ref, proj_ref, mgain_ref, mw_ref,
+    shift_ref, r_ref, xw_ref, qkv, gain_ref, qkv_hbm, proj_hbm, mgain_ref, mw_hbm,
     keep_ref, send_ref, coarse_ref,
-    xs, rs, qkv, kvr, mix, fr, fu, bias,
+    rs, kvr, mix, fr, fu, bias, kv_w, proj_ref, mw_ref, sems,
 ):
     core = lax.axis_index("lon") % 2
-    cols, slots, rows, feats = x_ref.shape
+    cols, slots, rows, feats = r_ref.shape
+    own_cols = cols // 2
     unit = slots * cols
     wins = rows // WIN_LAT
     size = WIN_LAT * unit
     a, b, c = shift_ref[0, 0], shift_ref[0, 1], shift_ref[0, 2]
-    for ref, scr in ((x_ref, xs), (r_ref, rs)):
-        for col in range(cols):
-            for slot in range(slots):
-                put(scr, size + slot * cols + col, ref[col, slot].astype(F32), unit)
-        put(scr, 0, take(scr, rows * unit, size))
-    starts = [pl.multiple_of(((j + 1) * WIN_LAT - b) * unit, 8) for j in range(wins)]
+    loads = [
+        pltpu.make_async_copy(source, target, sems.at[n])
+        for n, (source, target) in enumerate(
+            (
+                (qkv_hbm.at[:, pl.ds(feats, 2 * feats)], kv_w),
+                (proj_hbm, proj_ref),
+                (mw_hbm, mw_ref),
+            )
+        )
+    ]
+    for load in loads:
+        load.start()
+    by_window([reader(r_ref, col) for col in range(cols)], rs)
     gain = gain_ref[...]
+    loads[0].wait()
     for j in range(wins):
-        at = pl.ds(j * size, size)
-        normed = layer_norm(take(xs, starts[j], size), gain).astype(BF16)
-        qkv[at, :] = dot(normed, qkv_ref[...]).astype(BF16)
-        normed = layer_norm(take(rs, starts[j], size), gain).astype(BF16)
-        kvr[at, :] = dot(normed, qkv_ref[:, feats:]).astype(BF16)
-
+        tokens = take(rs, pl.multiple_of(((j + 1) * WIN_LAT - b) * unit, 8), size)
+        normed = layer_norm(tokens, gain).astype(BF16)
+        kvr[pl.ds(j * size, size), :] = dot(normed, kv_w[...]).astype(BF16)
     def parts(index):
         return index // unit, (index // cols) % slots, index % cols
 
@@ -132,10 +189,12 @@
     k_id = k_slot * 2 + jnp.where(k_row < b, 1, 0)
     bias[0] = jnp.where(q_id == k_id, 0.0, NEG)
     bias[1] = jnp.where(q_slot == k_slot, 0.0, NEG)
-    picks = q_side == k_side
     scale = (feats // HEADS) ** -0.5
+
     for j in range(wins):
         at = pl.ds(j * size, size)
+        masked = bias[min(j, 1)]
+        picks = q_side == k_side
         for pair in range(feats // 128):
             lanes = pl.ds(pair * 128, 128)
             k_lanes = pl.ds(feats + pair * 128, 128)
@@ -145,46 +204,49 @@
                 (qkv[at, k_lanes], kvr[at, lanes]),
                 (qkv[at, v_lanes], kvr[at, k_lanes]),
                 picks,
-                bias[min(j, 1)],
+                masked,
                 scale,
             ).astype(BF16)
+
     half = rows // 2
+    loads[1].wait()
     for j in range(wins):
         at = pl.ds(j * size, size)
-        fine = take(xs, starts[j], size) + dot(mix[at, :], proj_ref[...])
+        fine = xw_ref[at, :].astype(F32) + dot(mix[at, :], proj_ref[...])
         fine = fine.astype(BF16).astype(F32)
         for inner in range(WIN_LAT):
             source = j * WIN_LAT + inner - b
             source = jnp.where(source < 0, source + rows, source)
             put(fr, pl.multiple_of(source * unit, 8), fine[inner * unit : (inner + 1) * unit])
-    own_cols = cols // 2
-    for slot in range(slots):
-        for col in range(own_cols):
-            for target, out_ref in ((core, keep_ref), (1 - core, send_ref)):
-                start = slot * cols + target * own_cols + col
-                out_ref[col, slot] = take(fr, start, rows, unit).astype(BF16)
+
     for p in range(2):
         for slot in range(slots):
             for col in range(cols):
                 first = slot * cols + col
                 piece = take(fr, p * unit + first, half, 2 * unit)
                 put(fu, (p * slots + slot) * half * cols + col, piece, cols)
-    pieces = []
+    loads[2].wait()
+    groups = []
     count = half * unit // 2
     for q in range(2):
         for p in range(2):
-            pieces.append(take(fu, p * half * unit + q, count, 2))
+            groups.append(take(fu, p * half * unit + q, count, 2))
     width = 4 * feats
-    mean = sum(jnp.sum(piece, axis=-1, keepdims=True) for piece in pieces) / width
-    pieces = [piece - mean for piece in pieces]
-    spread = sum(jnp.sum(piece * piece, axis=-1, keepdims=True) for piece in pieces) / width
+    mean = sum(jnp.sum(piece, axis=-1, keepdims=True) for piece in groups) / width
+    groups = [piece - mean for piece in groups]
+    spread = sum(jnp.sum(piece * piece, axis=-1, keepdims=True) for piece in groups) / width
     scaling = lax.rsqrt(spread + EPSILON)
     total = jnp.zeros((count, mw_ref.shape[1]), F32)
-    for k, piece in enumerate(pieces):
+    for k, piece in enumerate(groups):
         lanes = slice(k * feats, (k + 1) * feats)
         merged = (piece * scaling * mgain_ref[:, lanes]).astype(BF16)
         total = total + dot(merged, mw_ref[lanes, :])
     coarse_ref[...] = total.astype(BF16).reshape(coarse_ref.shape)
+    for slot in range(slots):
+        for col in range(own_cols):
+            for target, out_ref in ((core, keep_ref), (1 - core, send_ref)):
+                start = slot * cols + target * own_cols + col
+                out_ref[col, slot] = take(fr, start, rows, unit).astype(BF16)
 
 
 def coarse_kernel(
@@ -278,15 +340,24 @@
 SMEM_SPEC = pl.BlockSpec(memory_space=pltpu.SMEM)
 
 
-def call(kernel, name, outs, scratch, arrays, limit):
+HBM_SPEC = pl.BlockSpec(memory_space=pltpu.HBM)
+
+
+def call(kernel, name, outs, scratch, arrays, limit, cost=None, hbm=()):
+    specs = [SMEM_SPEC] + [VMEM_SPEC] * (len(arrays) - 1)
+    arrays = list(arrays)
+    for n in hbm:
+        specs[n] = HBM_SPEC
+        arrays[n] = pltpu.with_memory_space_constraint(arrays[n], pltpu.HBM)
     return pl.pallas_call(
         kernel,
         name=name,
         out_shape=outs,
-        in_specs=[SMEM_SPEC] + [VMEM_SPEC] * (len(arrays) - 1),
+        in_specs=specs,
         out_specs=jax.tree.map(lambda _: VMEM_SPEC, outs),
         scratch_shapes=scratch,
         compiler_params=pltpu.CompilerParams(vmem_limit_bytes=limit << 20),
+        cost_estimate=cost,
     )(*arrays)
 
 
@@ -312,58 +383,79 @@
     sds = jax.ShapeDtypeStruct
     viewed = tokens.transpose(0, 2, 1, 3)
 
-    def picked(target):
-        levels_in = [
-            lax.dynamic_index_in_dim(viewed, level_of(target, slot, window_shift[0, 0]), 0, False)
-            for slot in range(slots)
-        ]
-        return jnp.stack(levels_in, axis=1)
-
-    other = swapped(picked(1 - core))
-    keep = picked(core)
+    half = sds((dev_cols, slots, rows, feats), BF16)
+    vhalf = pltpu.VMEM(half.shape, BF16)
+    keep, send, index = pl.pallas_call(
+        split_kernel,
+        name="split",
+        out_shape=(vhalf, vhalf, sds((2,), jnp.int32)),
+        in_specs=[SMEM_SPEC, HBM_SPEC],
+        out_specs=(VMEM_SPEC, VMEM_SPEC, SMEM_SPEC),
+        scratch_shapes=[pltpu.SemaphoreType.DMA((2, slots))],
+        compiler_params=pltpu.CompilerParams(vmem_limit_bytes=4 << 20),
+    )(window_shift, pltpu.with_memory_space_constraint(viewed, pltpu.HBM))
+    other = swapped(send)
     grid = jnp.concatenate(
         [jnp.where(core == 0, keep, other), jnp.where(core == 0, other, keep)], axis=0
     )
-
-    def branch(c):
-        def run(grid):
-            if c == 0:
-                return grid
-            left = permuted(grid[: cols - c], -2)
-            right = permuted(grid[cols - c :], 2)
-            return jnp.concatenate([left, right], axis=0)
-
-        return run
-
-    around = lax.switch(window_shift[0, 2], [branch(c) for c in range(WIN_LON)], grid)
     unit = slots * cols
     tokens_n = rows * unit
     size = WIN_LAT * unit
+    gain = fine_gain.reshape(1, feats)
+
     channels = merge_weight.shape[1]
     coarse_depth = rows // 2 * dev_cols
     coarse_n = slots * coarse_depth
     coarse_type = sds((slots, coarse_depth, channels), BF16)
-    fine_half = sds((dev_cols, slots, rows, feats), BF16)
+
+    def branch(c):
+        def run(grid):
+            around = grid
+            if c > 0:
+                left = permuted(grid[: cols - c], -2)
+                right = permuted(grid[cols - c :], 2)
+                around = jnp.concatenate([left, right], axis=0)
+            own = call(
+                own_kernel, "own",
+                (pltpu.VMEM((tokens_n, feats), BF16), pltpu.VMEM((tokens_n, 3 * feats), BF16)),
+                [chunked(tokens_n + size, feats)],
+                (window_shift, grid, gain, fine_qkv),
+                OWN_MIB,
+                pl.CostEstimate(
+                    flops=tokens_n * feats * feats * 6,
+                    bytes_accessed=10 * tokens_n * feats,
+                    transcendentals=0,
+                ),
+            )
+            return around, *own
+
+        return run
+
+    branches = [branch(c) for c in range(WIN_LON)]
+    around, xw, qkv = lax.switch(index[0], branches, grid)
     fine_keep, fine_send, coarse = call(
-        fine_kernel, "fine", (fine_half, fine_half, coarse_type),
+        fine_kernel, "fine", (half, half, coarse_type),
         [
             chunked(tokens_n + size, feats),
-            chunked(tokens_n + size, feats),
-            pltpu.VMEM((tokens_n, 3 * feats), BF16),
             pltpu.VMEM((tokens_n, 2 * feats), BF16),
             pltpu.VMEM((tokens_n, feats), BF16),
             chunked(tokens_n, feats),
             chunked(tokens_n, feats),
             pltpu.VMEM((2, 2 * size, size), F32),
+            pltpu.VMEM((feats, 2 * feats), BF16),
+            pltpu.VMEM(fine_proj.shape, BF16),
+            pltpu.VMEM(merge_weight.shape, BF16),
+            pltpu.SemaphoreType.DMA((3,)),
         ],
         (
-            window_shift, grid, around, fine_gain.reshape(1, feats), fine_qkv, fine_proj,
+            window_shift, around, xw, qkv, gain, fine_qkv, fine_proj,
             merge_gain.reshape(1, 4 * feats), merge_weight,
         ),
         FINE_MIB,
+        hbm=(5, 6, 8),
     )
     fine_other = swapped(fine_send)
-    moved = jnp.where(window_shift[0, 0] != window_shift[1, 0], swapped(coarse[1]), coarse[1])
+    moved = jnp.where(index[1] == 1, swapped(coarse[1]), coarse[1])
     coarse = jnp.stack([coarse[0], moved])
     l1, r1 = permuted(coarse, 2), permuted(coarse, -2)
     l2, r2 = permuted(coarse, 4), permuted(coarse, -4)

time: 59.2 us -> 55.3 us (0.934)
  Pallas kernels: 15.1 us -> 19.9 us
  waiting for transfers between devices: 22.4 us -> 18.7 us
  local copies, waits for them, and re-layouts: 4.08 us -> 0.68 us
  between operations: 2.83 us -> 1.65 us
  other arithmetic: 1.02 us -> 0.21 us
    pallas_call x3 -> x5, Pallas kernels: 15.1 us -> 19.9 us  [the longest x4 17.3 us: call(): pl.pallas_call(kernel, name=name, out_shape=outs, in_specs=specs, out_spe...]
    ppermute x6, waiting for transfers between devices: 20.5 us -> 16.9 us  [permuted(): lax.ppermute(value, 'lon', [(s, (s + steps) % count) for s in range(count)])]
    unnamed x22 -> x18, local copies, waits for them, and re-layouts: 1.46 us -> 0.05 us
    another operation x1 -> x0, local copies, waits for them, and re-layouts: 1.17 us -> none  [picked(): return jnp.stack(levels_in, axis=1)]
    slice x1, local copies, waits for them, and re-layouts: 1.4 us -> 0.58 us  [local(): moved = jnp.where(index[1] == 1, swapped(coarse[1]), coarse[1])]
    concatenate x1, other arithmetic: 0.87 us -> 0.05 us  [run(): around = jnp.concatenate([left, right], axis=0)]
  transfers between devices with their start and end apart: 10 -> 10, of which waited for: 8 -> 7; matrix products, arithmetic and copies ran while one was open for 0% -> 1% of each run, Pallas kernels for 7% -> 13%
where the time goes in v2:
time: 55.3 us; the launch traced here: 55.2 us
  Pallas kernels  19.9 us (36%)
  waiting for transfers between devices  18.7 us (34%)
  starting transfers between devices  13.8 us (25%)
  between operations  1.65 us (3%)
  local copies, waits for them, and re-layouts  0.68 us (1%)
    pallas_call x4, Pallas kernels, call(): pl.pallas_call(kernel, name=name, out_shape=outs, in_specs=specs, out_spe...  17.3 us
    ppermute x6, waiting for transfers between devices, permuted(): lax.ppermute(value, 'lon', [(s, (s + steps) % count) for s in range(count)])  16.9 us
    ppermute x6, starting transfers between devices, permuted(): lax.ppermute(value, 'lon', [(s, (s + steps) % count) for s in range(count)])  13.1 us
    pallas_call x1, Pallas kernels, local(): pl.pallas_call(split_kernel, name='split', out_shape=(vhalf, vhalf, sds((...  2.58 us
    ppermute x4, waiting for transfers between devices, swapped(): return lax.ppermute(value, 'lon', [(s, s ^ 1) for s in range(count)])  1.83 us
  transfers between devices with their start and end apart: 10, of which 7 were waited for; matrix products, arithmetic and copies ran while one was open for 1% of the time, Pallas kernels for 13%

profile of v2, /device:TPU:0, one launch (start us, length us, event | category | flops | bytes accessed | tf_op | source)
XLA Modules:
  0.0 55.2 jit_solution(17504935161868958208)
XLA Ops:
  0.0 2.6 %split.1 = (bf16[6,2,24,512]{3,2,1,0:T(8,128)(2,1)S(1)}, bf16[6,2,24,512]{3,2,1,0:T(8,128)(2,1)S(1)}, s32[2]{0:T(128)S(1)}) custom-call(s32[2,3]{1,0:T(2,128)} %shift_ref.7, bf16[4,6,24,512]{3,2,1,0:T(8,128)(2,1)} %bitcast.17), custom_call_target="tpu_custom_call" | custom-call | tf_op jit(solution)/shard_map/split/pallas_call | solution.py:388
  2.6 0.6 %collective-permute-start.22 = (bf16[6,2,24,512]{3,2,1,0:T(8,128)(2,1)S(1)}, bf16[6,2,24,512]{3,2,1,0:T(8,128)(2,1)S(1)}, u32[]{:S(2)}, u32[]{:S(2)}) collective-permute-start(bf16[6,2,24,512]{3,2,1,0:T(8,128)(2,1)S(1)} %get-tuple-element.220), channel_id=1, source_target_pairs={{0,1},{1,0},{2,3},{3,2},{4,5},{5,4},{6,7},{7,6},{8,9},{9,8},{10,11... | collective-permute-start | bytes 884744 | tf_op jit(solution)/shard_map/ppermute | solution.py:32
  3.2 0.6 %fusion.1 = (s32[1]{0:T(128)}, s32[1]{0:T(128)}) fusion(s32[2]{0:T(128)S(1)} %get-tuple-element.218), kind=kLoop, calls=%fused_computation.18 | loop fusion | bytes 16 | tf_op jit(solution)/shard_map/slice | solution.py:458
  4.4 0.1 broadcast_select_fusion.1
  4.5 0.1 pad_maximum_fusion.11
  4.6 0.0 copy-start.3
  4.6 18.4 %conditional.1 = (bf16[12,2,24,512]{3,2,1,0:T(8,128)(2,1)S(1)}, bf16[576,512]{1,0:T(8,128)(2,1)S(1)}, bf16[576,1536]{1,0:T(8,128)(2,1)S(1)}) conditional(s32[]{:T(128)} %bitcast.1, (s32[2,3]{1,0:T(2,128)S(1)}, bf16[12,2,24,512]{3,2,1,0:T(8,128)(2,1)S(1)}, f32[1,512]{1,0:T(1,128)S(1)}, ...), branch_computations={%region_0.1_spmd, %region_1.2_spmd, %region_2.3_spmd, %region_3.4_... | conditional | flops 906264576 | bytes 7667816 | solution.py:435
  4.7 2.8 %collective-permute-start.15 = (bf16[8,2,24,512]{3,2,1,0:T(8,128)(2,1)S(1)}, bf16[8,2,24,512]{3,2,1,0:T(8,128)(2,1)S(1)}, u32[]{:S(2)}, u32[]{:S(2)}) collective-permute-start(bf16[8,2,24,512]{3,2,1,0:T(8,128)(2,1)S(1)} %slice.62), channel_id=1, source_target_pairs={{0,2},{1,3},{2,4},{3,5},{4,6},{5,7},{6,8},{7,9},{8,10},{9,11},{10,... | collective-permute-start | bytes 1179656 | tf_op jit(solution)/shard_map/cond/branch_8_fun/ppermute | solution.py:27
  7.5 3.1 %collective-permute-start.14 = (bf16[4,2,24,512]{3,2,1,0:T(8,128)(2,1)S(1)}, bf16[4,2,24,512]{3,2,1,0:T(8,128)(2,1)S(1)}, u32[]{:S(2)}, u32[]{:S(2)}) collective-permute-start(bf16[4,2,24,512]{3,2,1,0:T(8,128)(2,1)S(1)} %slice.61), channel_id=1, source_target_pairs={{0,14},{1,15},{2,0},{3,1},{4,2},{5,3},{6,4},{7,5},{8,6},{9,7},{10,... | collective-permute-start | bytes 589832 | tf_op jit(solution)/shard_map/cond/branch_8_fun/ppermute | solution.py:27
  10.7 3.1 %own.20 = (bf16[576,512]{1,0:T(8,128)(2,1)S(1)}, bf16[576,1536]{1,0:T(8,128)(2,1)S(1)}) custom-call(s32[2,3]{1,0:T(2,128)S(1)} %get-tuple-element.183.shift_ref, bf16[12,2,24,512]{3,2,1,0:T(8,128)(2,1)S(1)} %get-tuple-element.182.x_ref, f32[1,512]{1,0:T(1,128)S(1)} %get-tuple-element.184.gain_ref, bf16[512,1536]{1,0:T(8,128)(2,1)S(1)} %get-tuple-element.185.qkv_ref), custom_call_target="tpu_custom_call" | custom-call | flops 905969664 | bytes 2949120 | tf_op jit(solution)/shard_map/cond/branch_8_fun/own/pallas_call | solution.py:352
  13.7 9.0 %collective-permute-done.14 = bf16[4,2,24,512]{3,2,1,0:T(8,128)(2,1)S(1)} collective-permute-done((bf16[4,2,24,512]{3,2,1,0:T(8,128)(2,1)S(1)}, bf16[4,2,24,512]{3,2,1,0:T(8,128)(2,1)S(1)}, u32[]{:S(2)}, u32[]{:S(2)}) %collective-permute-start.14) | collective-permute-done | bytes 196640 | tf_op jit(solution)/shard_map/cond/branch_8_fun/ppermute | solution.py:27
  22.8 0.1 pad_maximum_fusion.7
  23.0 0.0 copy-start.1
  23.0 0.0 copy-start.2
  23.0 0.0 copy-start.5
  23.1 8.1 %fine.1 = (bf16[6,2,24,512]{3,2,1,0:T(8,128)(2,1)S(1)}, bf16[6,2,24,512]{3,2,1,0:T(8,128)(2,1)S(1)}, bf16[2,72,512]{2,1,0:T(8,128)(2,1)S(1)}) custom-call(s32[2,3]{1,0:T(2,128)S(1)} %copy-done.7, bf16[12,2,24,512]{3,2,1,0:T(8,128)(2,1)S(1)} %get-tuple-element.221.r_ref, bf16[576,512]{1,0:T(8,128)(2,1)S(1)} %get-tuple-element.222.xw_ref, ...), custom_call_target="tpu_custom_call" | custom-call | tf_op jit(solution)/shard_map/fine/pallas_call | solution.py:352
  31.2 0.0 copy-start
  31.2 0.0 copy-start.4
  31.2 0.1 collective-permute-start.23
  32.1 0.5 collective-permute-done.23
  32.6 3.3 %collective-permute-start.27 = (bf16[2,72,512]{2,1,0:T(8,128)(2,1)S(1)}, bf16[2,72,512]{2,1,0:T(8,128)(2,1)S(1)}, u32[]{:S(2)}, u32[]{:S(2)}) collective-permute-start(bf16[2,72,512]{2,1,0:T(8,128)(2,1)S(1)} %pad_maximum_fusion.12.own_ref), channel_id=1, source_target_pairs={{0,12},{1,13},{2,14},{3,15},{4,0},{5,1},{6,2},{7,3},{8,4},{9,5},{1... | collective-permute-start | bytes 442376 | tf_op jit(solution)/shard_map/ppermute | solution.py:27
  35.9 0.0 collective-permute-start.26
  35.9 3.8 %collective-permute-start.25 = (bf16[2,72,512]{2,1,0:T(8,128)(2,1)S(1)}, bf16[2,72,512]{2,1,0:T(8,128)(2,1)S(1)}, u32[]{:S(2)}, u32[]{:S(2)}) collective-permute-start(bf16[2,72,512]{2,1,0:T(8,128)(2,1)S(1)} %pad_maximum_fusion.12.own_ref), channel_id=1, source_target_pairs={{0,14},{1,15},{2,0},{3,1},{4,2},{5,3},{6,4},{7,5},{8,6},{9,7},{10,... | collective-permute-start | bytes 442376 | tf_op jit(solution)/shard_map/ppermute | solution.py:27
  39.7 0.0 collective-permute-start.24
  39.7 0.4 collective-permute-done.27.r2_ref
  40.2 4.3 %collective-permute-done.26.l2_ref = bf16[2,72,512]{2,1,0:T(8,128)(2,1)S(1)} collective-permute-done((bf16[2,72,512]{2,1,0:T(8,128)(2,1)S(1)}, bf16[2,72,512]{2,1,0:T(8,128)(2,1)S(1)}, u32[]{:S(2)}, u32[]{:S(2)}) %collective-permute-start.26) | collective-permute-done | bytes 147488 | tf_op jit(solution)/shard_map/ppermute | solution.py:27
  44.4 1.2 %collective-permute-done.25.r1_ref = bf16[2,72,512]{2,1,0:T(8,128)(2,1)S(1)} collective-permute-done((bf16[2,72,512]{2,1,0:T(8,128)(2,1)S(1)}, bf16[2,72,512]{2,1,0:T(8,128)(2,1)S(1)}, u32[]{:S(2)}, u32[]{:S(2)}) %collective-permute-start.25) | collective-permute-done | bytes 147488 | tf_op jit(solution)/shard_map/ppermute | solution.py:27
  45.7 1.9 %collective-permute-done.24.l1_ref = bf16[2,72,512]{2,1,0:T(8,128)(2,1)S(1)} collective-permute-done((bf16[2,72,512]{2,1,0:T(8,128)(2,1)S(1)}, bf16[2,72,512]{2,1,0:T(8,128)(2,1)S(1)}, u32[]{:S(2)}, u32[]{:S(2)}) %collective-permute-start.24) | collective-permute-done | bytes 147488 | tf_op jit(solution)/shard_map/ppermute | solution.py:27
  47.6 3.9 %coarse.1.own_ref = bf16[2,72,512]{2,1,0:T(8,128)(2,1)S(1)} custom-call(s32[2,3]{1,0:T(2,128)S(1)} %copy-done.7, bf16[2,72,512]{2,1,0:T(8,128)(2,1)S(1)} %pad_maximum_fusion.12.own_ref, bf16[2,72,512]{2,1,0:T(8,128)(2,1)S(1)} %collective-permute-done.24.l1_ref, bf16[2,72,512]{2,1,0:T(8,128)(2,1)S(1)} %collective-permute-done.25.r1_ref, ...), custom_call_target="tpu_custom_call" | custom-call | tf_op jit(solution)/shard_map/coarse/pallas_call | solution.py:352
  51.4 0.1 collective-permute-start.28
  51.5 1.3 %collective-permute-done.28.other_ref = bf16[2,72,512]{2,1,0:T(8,128)(2,1)S(1)} collective-permute-done((bf16[2,72,512]{2,1,0:T(8,128)(2,1)S(1)}, bf16[2,72,512]{2,1,0:T(8,128)(2,1)S(1)}, u32[]{:S(2)}, u32[]{:S(2)}) %collective-permute-start.28) | collective-permute-done | bytes 147488 | tf_op jit(solution)/shard_map/ppermute | solution.py:32
  52.9 2.3 %expand.1 = bf16[4,6,24,512]{3,2,1,0:T(8,128)(2,1)} custom-call(s32[2,3]{1,0:T(2,128)S(1)} %copy-done.7, bf16[2,72,512]{2,1,0:T(8,128)(2,1)S(1)} %coarse.1.own_ref, bf16[2,72,512]{2,1,0:T(8,128)(2,1)S(1)} %collective-permute-done.28.other_ref, bf16[6,2,24,512]{3,2,1,0:T(8,128)(2,1)S(1)} %get-tuple-element.225.fkeep_ref, ...), custom_call_target="tpu_custom_call" | custom-call | tf_op jit(solution)/shard_map/expand/pallas_call | solution.py:352
  (21 shorter events, 0.1 us)
Async XLA Ops:
  0.0 4.6 %copy-start.7 = (s32[2,3]{1,0:T(2,128)S(1)}, s32[2,3]{1,0:T(2,128)}, u32[]{:S(2)}) copy-start(s32[2,3]{1,0:T(2,128)} %shift_ref.7) | copy-start | bytes 76
  0.0 4.6 %copy-start.8 = (f32[512]{0:T(512)S(1)}, f32[512]{0:T(512)}, u32[]{:S(2)}) copy-start(f32[512]{0:T(512)} %param.26) | copy-start | bytes 6148
  2.6 1.8 %collective-permute-start.22 = (bf16[6,2,24,512]{3,2,1,0:T(8,128)(2,1)S(1)}, bf16[6,2,24,512]{3,2,1,0:T(8,128)(2,1)S(1)}, u32[]{:S(2)}, u32[]{:S(2)}) collective-permute-start(bf16[6,2,24,512]{3,2,1,0:T(8,128)(2,1)S(1)} %get-tuple-element.220), channel_id=1, source_target_pairs={{0,1},{1,0},{2,3},{3,2},{4,5},{5,4},{6,7},{7,6},{8,9},{9,8},{10,11... | collective-permute-start | bytes 884744 | tf_op jit(solution)/shard_map/ppermute | solution.py:32
  3.2 1.4 %copy-start.6 = (bf16[512,1536]{1,0:T(8,128)(2,1)S(1)}, bf16[512,1536]{1,0:T(8,128)(2,1)}, u32[]{:S(2)}) copy-start(bf16[512,1536]{1,0:T(8,128)(2,1)} %qkv_hbm.1) | copy-start | bytes 4718596
  4.6 18.4 %copy-start.3 = (f32[2048]{0:T(1024)S(1)}, f32[2048]{0:T(1024)}, u32[]{:S(2)}) copy-start(f32[2048]{0:T(1024)} %param.29) | copy-start | bytes 24580
  4.7 18.1 %collective-permute-start.15 = (bf16[8,2,24,512]{3,2,1,0:T(8,128)(2,1)S(1)}, bf16[8,2,24,512]{3,2,1,0:T(8,128)(2,1)S(1)}, u32[]{:S(2)}, u32[]{:S(2)}) collective-permute-start(bf16[8,2,24,512]{3,2,1,0:T(8,128)(2,1)S(1)} %slice.62), channel_id=1, source_target_pairs={{0,2},{1,3},{2,4},{3,5},{4,6},{5,7},{6,8},{7,9},{8,10},{9,11},{10,... | collective-permute-start | bytes 1179656 | tf_op jit(solution)/shard_map/cond/branch_8_fun/ppermute | solution.py:27
  7.5 15.2 %collective-permute-start.14 = (bf16[4,2,24,512]{3,2,1,0:T(8,128)(2,1)S(1)}, bf16[4,2,24,512]{3,2,1,0:T(8,128)(2,1)S(1)}, u32[]{:S(2)}, u32[]{:S(2)}) collective-permute-start(bf16[4,2,24,512]{3,2,1,0:T(8,128)(2,1)S(1)} %slice.61), channel_id=1, source_target_pairs={{0,14},{1,15},{2,0},{3,1},{4,2},{5,3},{6,4},{7,5},{8,6},{9,7},{10,... | collective-permute-start | bytes 589832 | tf_op jit(solution)/shard_map/cond/branch_8_fun/ppermute | solution.py:27
  23.0 24.5 %copy-start.1 = (bf16[512,1536]{1,0:T(8,128)(2,1)S(1)}, bf16[512,1536]{1,0:T(8,128)(2,1)}, u32[]{:S(2)}) copy-start(bf16[512,1536]{1,0:T(8,128)(2,1)} %qkv_ref.1) | copy-start | bytes 4718596
  23.0 24.5 %copy-start.2 = (bf16[512,512]{1,0:T(8,128)(2,1)S(1)}, bf16[512,512]{1,0:T(8,128)(2,1)}, u32[]{:S(2)}) copy-start(bf16[512,512]{1,0:T(8,128)(2,1)} %proj_ref.1) | copy-start | bytes 1572868
  23.0 24.5 %copy-start.5 = (f32[512]{0:T(512)S(1)}, f32[512]{0:T(512)}, u32[]{:S(2)}) copy-start(f32[512]{0:T(512)} %param.31) | copy-start | bytes 6148
  31.2 21.7 %copy-start = (bf16[512,2048]{1,0:T(8,128)(2,1)S(1)}, bf16[512,2048]{1,0:T(8,128)(2,1)}, u32[]{:S(2)}) copy-start(bf16[512,2048]{1,0:T(8,128)(2,1)} %weight_ref.1) | copy-start | bytes 6291460
  31.2 21.7 %copy-start.4 = (f32[512]{0:T(512)S(1)}, f32[512]{0:T(512)}, u32[]{:S(2)}) copy-start(f32[512]{0:T(512)} %param.35) | copy-start | bytes 6148
  31.2 1.3 %collective-permute-start.23 = (bf16[72,512]{1,0:T(8,128)(2,1)S(1)}, bf16[72,512]{1,0:T(8,128)(2,1)S(1)}, u32[]{:S(2)}, u32[]{:S(2)}) collective-permute-start(bf16[72,512]{1,0:T(8,128)(2,1)S(1)} %get-tuple-element.230), channel_id=1, source_target_pairs={{0,1},{1,0},{2,3},{3,2},{4,5},{5,4},{6,7},{7,6},{8,9},{9,8},{10,11... | collective-permute-start | bytes 221192 | tf_op jit(solution)/shard_map/ppermute | solution.py:32
  32.6 7.6 %collective-permute-start.27 = (bf16[2,72,512]{2,1,0:T(8,128)(2,1)S(1)}, bf16[2,72,512]{2,1,0:T(8,128)(2,1)S(1)}, u32[]{:S(2)}, u32[]{:S(2)}) collective-permute-start(bf16[2,72,512]{2,1,0:T(8,128)(2,1)S(1)} %pad_maximum_fusion.12.own_ref), channel_id=1, source_target_pairs={{0,12},{1,13},{2,14},{3,15},{4,0},{5,1},{6,2},{7,3},{8,4},{9,5},{1... | collective-permute-start | bytes 442376 | tf_op jit(solution)/shard_map/ppermute | solution.py:27
  35.9 8.6 %collective-permute-start.26 = (bf16[2,72,512]{2,1,0:T(8,128)(2,1)S(1)}, bf16[2,72,512]{2,1,0:T(8,128)(2,1)S(1)}, u32[]{:S(2)}, u32[]{:S(2)}) collective-permute-start(bf16[2,72,512]{2,1,0:T(8,128)(2,1)S(1)} %pad_maximum_fusion.12.own_ref), channel_id=1, source_target_pairs={{0,4},{1,5},{2,6},{3,7},{4,8},{5,9},{6,10},{7,11},{8,12},{9,13},{1... | collective-permute-start | bytes 442376 | tf_op jit(solution)/shard_map/ppermute | solution.py:27
  35.9 9.8 %collective-permute-start.25 = (bf16[2,72,512]{2,1,0:T(8,128)(2,1)S(1)}, bf16[2,72,512]{2,1,0:T(8,128)(2,1)S(1)}, u32[]{:S(2)}, u32[]{:S(2)}) collective-permute-start(bf16[2,72,512]{2,1,0:T(8,128)(2,1)S(1)} %pad_maximum_fusion.12.own_ref), channel_id=1, source_target_pairs={{0,14},{1,15},{2,0},{3,1},{4,2},{5,3},{6,4},{7,5},{8,6},{9,7},{10,... | collective-permute-start | bytes 442376 | tf_op jit(solution)/shard_map/ppermute | solution.py:27
  39.7 7.8 %collective-permute-start.24 = (bf16[2,72,512]{2,1,0:T(8,128)(2,1)S(1)}, bf16[2,72,512]{2,1,0:T(8,128)(2,1)S(1)}, u32[]{:S(2)}, u32[]{:S(2)}) collective-permute-start(bf16[2,72,512]{2,1,0:T(8,128)(2,1)S(1)} %pad_maximum_fusion.12.own_ref), channel_id=1, source_target_pairs={{0,2},{1,3},{2,4},{3,5},{4,6},{5,7},{6,8},{7,9},{8,10},{9,11},{10,... | collective-permute-start | bytes 442376 | tf_op jit(solution)/shard_map/ppermute | solution.py:27
  39.7 11.8 %collective-permute-start.29 = (bf16[6,2,24,512]{3,2,1,0:T(8,128)(2,1)S(1)}, bf16[6,2,24,512]{3,2,1,0:T(8,128)(2,1)S(1)}, u32[]{:S(2)}, u32[]{:S(2)}) collective-permute-start(bf16[6,2,24,512]{3,2,1,0:T(8,128)(2,1)S(1)} %get-tuple-element.226), channel_id=1, source_target_pairs={{0,1},{1,0},{2,3},{3,2},{4,5},{5,4},{6,7},{7,6},{8,9},{9,8},{10,11... | collective-permute-start | bytes 884744 | tf_op jit(solution)/shard_map/ppermute | solution.py:32
  51.4 1.4 %collective-permute-start.28 = (bf16[2,72,512]{2,1,0:T(8,128)(2,1)S(1)}, bf16[2,72,512]{2,1,0:T(8,128)(2,1)S(1)}, u32[]{:S(2)}, u32[]{:S(2)}) collective-permute-start(bf16[2,72,512]{2,1,0:T(8,128)(2,1)S(1)} %coarse.1.own_ref), channel_id=1, source_target_pairs={{0,1},{1,0},{2,3},{3,2},{4,5},{5,4},{6,7},{7,6},{8,9},{9,8},{10,11... | collective-permute-start | bytes 442376 | tf_op jit(solution)/shard_map/ppermute | solution.py:32

commit v3 on v2

--- a/solution.py
+++ b/solution.py
@@ -1,5 +1,3 @@
-import functools
-
 import jax
 import jax.numpy as jnp
 from jax import lax
@@ -7,9 +5,9 @@
 from jax.experimental.pallas import tpu as pltpu
 from jax.sharding import PartitionSpec as P
 
+
 HEADS = 8
 HC = 8
-WIN_LEV = 2
 WIN_LAT = 6
 WIN_LON = 12
 EPSILON = 1e-05
@@ -32,6 +30,12 @@
     return lax.ppermute(value, "lon", [(s, s ^ 1) for s in range(count)])
 
 
+def paired(value, inside):
+    count = lax.axis_size("lon")
+    steps = [2 if (s // 2 % 2 == 0) == inside else -2 for s in range(count)]
+    return lax.ppermute(value, "lon", [(s, (s + steps[s]) % count) for s in range(count)])
+
+
 def layer_norm(x, gain):
     center = x - jnp.mean(x, axis=-1, keepdims=True)
     spread = jnp.mean(center * center, axis=-1, keepdims=True)
@@ -71,47 +75,44 @@
     return pltpu.VMEM((width // 128, count, 128), F32)
 
 
-def head_pair(q, keys, values, picks, bias, scale):
+def head_pair(q, k, v, bias, scale, far=None):
     size = q.shape[0]
-    low = iota(q.shape, 1) < q.shape[1] // 2
+    low = iota(q.shape, 1) < 64
     zero = jnp.zeros_like(q)
-    q2 = jnp.concatenate([jnp.where(low, q, zero), jnp.where(low, zero, q)], axis=0)
-    if picks is None:
-        scores = dot_t(q2, keys[0])
-    else:
-        scores = jnp.where(picks, dot_t(q2, keys[0]), dot_t(q2, keys[1]))
-    scores = scores + bias
+    q2 = [jnp.where(low, q, zero), jnp.where(low, zero, q)]
+    if far is not None:
+        q2 = [
+            jnp.concatenate([jnp.where(far, zero, one), jnp.where(far, one, zero)], axis=1)
+            for one in q2
+        ]
+    scores = dot_t(jnp.concatenate(q2, axis=0), k) + bias
     top = jnp.max(scores, axis=-1, keepdims=True)
     expo = jnp.exp((scores - top) * scale)
     total = jnp.sum(expo, axis=-1, keepdims=True)
-    if picks is None:
-        mixed = dot(expo.astype(BF16), values[0])
+    mixed = dot(expo.astype(BF16), v) / total
+    if far is not None:
+        mixed = [
+            jnp.where(far, part[:, 128:], part[:, :128]) for part in (mixed[:size], mixed[size:])
+        ]
     else:
-        none = jnp.zeros_like(expo)
-        mixed = dot(jnp.where(picks, expo, none).astype(BF16), values[0]) + dot(
-            jnp.where(picks, none, expo).astype(BF16), values[1]
-        )
-    mixed = mixed / total
-    return jnp.where(low, mixed[:size], mixed[size:])
-
-
-def split_kernel(shift_ref, tok_ref, keep_ref, send_ref, branch_ref, sems):
+        mixed = [mixed[:size], mixed[size:]]
+    return jnp.where(low, mixed[0], mixed[1])
+
+
+def both_ways(far, one, two):
+    return jnp.concatenate([jnp.where(far, two, one), jnp.where(far, one, two)], axis=1)
+
+
+def split_kernel(shift_ref, tok_ref, keep_ref, send_ref, branch_ref):
     core = lax.axis_index("lon") % 2
     a = shift_ref[0, 0]
-    copies = []
-    for n, (target, out_ref) in enumerate(((1 - core, send_ref), (core, keep_ref))):
-        for slot in range(2):
-            copies.append(
-                pltpu.make_async_copy(
-                    tok_ref.at[level_of(target, slot, a)], out_ref.at[:, slot], sems.at[n, slot]
-                )
-            )
-    for copy in copies:
-        copy.start()
     branch_ref[0] = shift_ref[0, 2]
     branch_ref[1] = jnp.where(a == shift_ref[1, 0], 0, 1)
-    for copy in copies:
-        copy.wait()
+    for target, out_ref in ((1 - core, send_ref), (core, keep_ref)):
+        for slot in range(2):
+            level = level_of(target, slot, a)
+            for col in range(out_ref.shape[0]):
+                out_ref[col, slot] = tok_ref[level, col]
 
 
 def by_window(columns, scr):
@@ -129,7 +130,7 @@
 
 
 def own_kernel(shift_ref, x_ref, gain_ref, qkv_ref, xw_ref, out_ref, xs):
-    cols, slots, rows, feats = x_ref.shape
+    cols, slots, rows, _ = x_ref.shape
     unit = slots * cols
     size = WIN_LAT * unit
     b = shift_ref[0, 1]
@@ -176,13 +177,13 @@
         tokens = take(rs, pl.multiple_of(((j + 1) * WIN_LAT - b) * unit, 8), size)
         normed = layer_norm(tokens, gain).astype(BF16)
         kvr[pl.ds(j * size, size), :] = dot(normed, kv_w[...]).astype(BF16)
+
     def parts(index):
         return index // unit, (index // cols) % slots, index % cols
 
-    q_row, q_slot, q_col = parts(iota((2 * size, 1), 0) % size)
-    k_row, k_slot, k_col = parts(iota((1, size), 1))
-    q_side = jnp.where(q_col + c >= cols, 1, 0)
-    k_side = jnp.where(k_col + c >= cols, 1, 0)
+    q_row, q_slot, _ = parts(iota((2 * size, 1), 0) % size)
+    k_row, k_slot, _ = parts(iota((1, size), 1))
+    far = iota((size, 128), 0) % cols + c >= cols
     apart = jnp.where((a == 0) | (core == 1), 0, 1)
     q_slot, k_slot = q_slot * apart, k_slot * apart
     q_id = q_slot * 2 + jnp.where(q_row < b, 1, 0)
@@ -194,18 +195,17 @@
     for j in range(wins):
         at = pl.ds(j * size, size)
         masked = bias[min(j, 1)]
-        picks = q_side == k_side
         for pair in range(feats // 128):
             lanes = pl.ds(pair * 128, 128)
             k_lanes = pl.ds(feats + pair * 128, 128)
             v_lanes = pl.ds(2 * feats + pair * 128, 128)
             mix[at, lanes] = head_pair(
                 qkv[at, lanes],
-                (qkv[at, k_lanes], kvr[at, lanes]),
-                (qkv[at, v_lanes], kvr[at, k_lanes]),
-                picks,
+                both_ways(far, qkv[at, k_lanes], kvr[at, lanes]),
+                both_ways(far, qkv[at, v_lanes], kvr[at, k_lanes]),
                 masked,
                 scale,
+                far,
             ).astype(BF16)
 
     half = rows // 2
@@ -219,18 +219,19 @@
             source = jnp.where(source < 0, source + rows, source)
             put(fr, pl.multiple_of(source * unit, 8), fine[inner * unit : (inner + 1) * unit])
 
+    block = slots * half
     for p in range(2):
         for slot in range(slots):
             for col in range(cols):
-                first = slot * cols + col
-                piece = take(fr, p * unit + first, half, 2 * unit)
-                put(fu, (p * slots + slot) * half * cols + col, piece, cols)
+                piece = take(fr, p * unit + slot * cols + col, half, 2 * unit)
+                put(fu, (p * cols + col) * block + slot * half, piece)
     loads[2].wait()
     groups = []
     count = half * unit // 2
     for q in range(2):
         for p in range(2):
-            groups.append(take(fu, p * half * unit + q, count, 2))
+            starts = [(p * cols + col) * block for col in range(q, cols, 2)]
+            groups.append(jnp.concatenate([take(fu, start, block) for start in starts], axis=0))
     width = 4 * feats
     mean = sum(jnp.sum(piece, axis=-1, keepdims=True) for piece in groups) / width
     groups = [piece - mean for piece in groups]
@@ -250,49 +251,56 @@
 
 
 def coarse_kernel(
-    shift_ref, own_ref, l1_ref, r1_ref, l2_ref, r2_ref, gain_ref, qkv_ref, proj_ref,
-    out_ref, keys, values, bias, mix, *, own_cols,
+    shift_ref, own_ref, inside_ref, outside_ref, left_ref, right_ref, gain_ref, qkv_ref, proj_ref,
+    out_ref, keys, values, bias, mix,
 ):
     place = lax.axis_index("lon")
     core = place % 2
-    chips_wide = WIN_LON // own_cols
-    side = (place // 2) % chips_wide
-    slots, depth, feats = own_ref.shape
-    size = slots * depth
+    own_cols, depth, feats = own_ref.shape
+    side = (place // 2) % (WIN_LON // own_cols)
+    size = own_cols * depth
     a, b, c = shift_ref[1, 0], shift_ref[1, 1], shift_ref[1, 2]
     gain = gain_ref[...]
-    refs = (own_ref, l1_ref, r1_ref, l2_ref, r2_ref)
-    offsets = (0, -1, 1, -2, 2)
+    near_cols = own_cols - lax.rem(c, own_cols)
+    far = [
+        jnp.where(col < near_cols, right_ref[col].astype(F32), left_ref[col].astype(F32))
+        for col in range(own_cols)
+    ]
     queries = None
-    for n, ref in enumerate(refs):
+    sets = [ref[...].astype(F32).reshape(size, feats) for ref in (own_ref, inside_ref, outside_ref)]
+    for n, full in enumerate((*sets, jnp.concatenate(far, axis=0))):
         at = pl.ds(n * size, size)
-        full = ref[...].astype(F32).reshape(size, feats)
         normed = layer_norm(full, gain).astype(BF16)
         if n == 0:
             queries = dot(normed, qkv_ref[:, :feats]).astype(BF16)
         keys[at, :] = dot(normed, qkv_ref[:, feats : 2 * feats]).astype(BF16)
         values[at, :] = dot(normed, qkv_ref[:, 2 * feats :]).astype(BF16)
 
-    def ids(index, offset):
-        slot = index // depth
-        row = (index // own_cols) % (depth // own_cols)
-        col = (side + offset + chips_wide) * own_cols + index % own_cols
-        window = (col + c) // WIN_LON
+    def ids(index, chips):
+        col = index // depth
+        slot = (index // (depth // 2)) % 2
+        row = index % (depth // 2)
+        window = ((side + chips(col) + 2) * own_cols + col + c) // WIN_LON
         apart = jnp.where((a == 0) | (core == 1), 0, slot)
         return (window * 8 + (row + b) // WIN_LAT) * 2 + apart
 
-    q_id = ids(iota((2 * size, 1), 0) % size, 0)
-    for n, offset in enumerate(offsets):
-        k_id = ids(iota((1, size), 1), offset)
+    chips_off = (
+        lambda col: 0,
+        lambda col: 1 - 2 * side,
+        lambda col: 2 * side - 1,
+        lambda col: jnp.where(col < near_cols, 2, -2),
+    )
+    q_id = ids(iota((2 * size, 1), 0) % size, chips_off[0])
+    for n, chips in enumerate(chips_off):
+        k_id = ids(iota((1, size), 1), chips)
         bias[:, n * size : (n + 1) * size] = jnp.where(q_id == k_id, 0.0, NEG)
     scale = (feats // HC) ** -0.5
     for pair in range(feats // 128):
         lanes = pl.ds(pair * 128, 128)
         mix[:, lanes] = head_pair(
             queries[:, pair * 128 : (pair + 1) * 128],
-            (keys[:, lanes],),
-            (values[:, lanes],),
-            None,
+            keys[:, lanes],
+            values[:, lanes],
             bias[...],
             scale,
         ).astype(BF16)
@@ -302,21 +310,18 @@
 
 def expand_kernel(
     shift_ref, own_ref, other_ref, fkeep_ref, fother_ref, gain_ref, weight_ref,
-    out_ref, cs, ex, *, own_cols,
+    out_ref, ex,
 ):
     core = lax.axis_index("lon") % 2
-    slots, depth, feats = own_ref.shape
-    size = slots * depth
-    units = size // own_cols
+    own_cols, units, feats = own_ref.shape
+    slots = 2
     rows = 2 * units // slots
     home = own_cols // 2
     a1, a2 = shift_ref[0, 0], shift_ref[1, 0]
-    put(cs.at[0], 0, own_ref[...].astype(F32).reshape(size, feats))
-    put(cs.at[1], 0, other_ref[...].astype(F32).reshape(size, feats))
     blocks = []
-    for which in range(2):
+    for ref in (own_ref, other_ref):
         for col in range(home):
-            blocks.append(take(cs.at[which], core * home + col, units, own_cols))
+            blocks.append(ref[core * home + col].astype(F32))
     blocks = jnp.concatenate(blocks, axis=0).astype(BF16)
     gain = gain_ref[...]
     for q in range(2):
@@ -343,7 +348,7 @@
 HBM_SPEC = pl.BlockSpec(memory_space=pltpu.HBM)
 
 
-def call(kernel, name, outs, scratch, arrays, limit, cost=None, hbm=()):
+def call(kernel, outs, scratch, arrays, limit, cost=None, hbm=()):
     specs = [SMEM_SPEC] + [VMEM_SPEC] * (len(arrays) - 1)
     arrays = list(arrays)
     for n in hbm:
@@ -351,7 +356,6 @@
         arrays[n] = pltpu.with_memory_space_constraint(arrays[n], pltpu.HBM)
     return pl.pallas_call(
         kernel,
-        name=name,
         out_shape=outs,
         in_specs=specs,
         out_specs=jax.tree.map(lambda _: VMEM_SPEC, outs),
@@ -379,6 +383,7 @@
     cols = 2 * dev_cols
     slots = 2
     assert levels == 4 and cols == WIN_LON and rows % (2 * WIN_LAT) == 0
+    assert lax.axis_size("lon") % 4 == 0 and WIN_LON == 2 * dev_cols
     core = lax.axis_index("lon") % 2
     sds = jax.ShapeDtypeStruct
     viewed = tokens.transpose(0, 2, 1, 3)
@@ -389,9 +394,8 @@
         split_kernel,
         name="split",
         out_shape=(vhalf, vhalf, sds((2,), jnp.int32)),
-        in_specs=[SMEM_SPEC, HBM_SPEC],
+        in_specs=[SMEM_SPEC, VMEM_SPEC],
         out_specs=(VMEM_SPEC, VMEM_SPEC, SMEM_SPEC),
-        scratch_shapes=[pltpu.SemaphoreType.DMA((2, slots))],
         compiler_params=pltpu.CompilerParams(vmem_limit_bytes=4 << 20),
     )(window_shift, pltpu.with_memory_space_constraint(viewed, pltpu.HBM))
     other = swapped(send)
@@ -404,9 +408,9 @@
     gain = fine_gain.reshape(1, feats)
 
     channels = merge_weight.shape[1]
-    coarse_depth = rows // 2 * dev_cols
-    coarse_n = slots * coarse_depth
-    coarse_type = sds((slots, coarse_depth, channels), BF16)
+    coarse_depth = rows // 2 * slots
+    coarse_n = dev_cols * coarse_depth
+    coarse_type = sds((dev_cols, coarse_depth, channels), BF16)
 
     def branch(c):
         def run(grid):
@@ -416,7 +420,7 @@
                 right = permuted(grid[cols - c :], 2)
                 around = jnp.concatenate([left, right], axis=0)
             own = call(
-                own_kernel, "own",
+                own_kernel,
                 (pltpu.VMEM((tokens_n, feats), BF16), pltpu.VMEM((tokens_n, 3 * feats), BF16)),
                 [chunked(tokens_n + size, feats)],
                 (window_shift, grid, gain, fine_qkv),
@@ -434,7 +438,7 @@
     branches = [branch(c) for c in range(WIN_LON)]
     around, xw, qkv = lax.switch(index[0], branches, grid)
     fine_keep, fine_send, coarse = call(
-        fine_kernel, "fine", (half, half, coarse_type),
+        fine_kernel, (half, half, coarse_type),
         [
             chunked(tokens_n + size, feats),
             pltpu.VMEM((tokens_n, 2 * feats), BF16),
@@ -455,30 +459,32 @@
         hbm=(5, 6, 8),
     )
     fine_other = swapped(fine_send)
-    moved = jnp.where(index[1] == 1, swapped(coarse[1]), coarse[1])
-    coarse = jnp.stack([coarse[0], moved])
-    l1, r1 = permuted(coarse, 2), permuted(coarse, -2)
-    l2, r2 = permuted(coarse, 4), permuted(coarse, -4)
+    upper = jnp.arange(coarse_depth, dtype=jnp.int32)[None, :, None] >= coarse_depth // 2
+    coarse = jnp.where(upper & (index[1] == 1), swapped(coarse), coarse)
+
+    right = permuted(coarse, -4)
+    outside = paired(coarse, False)
+    inside = paired(coarse, True)
+    left = permuted(coarse, 4)
     coarse_out = call(
-        functools.partial(coarse_kernel, own_cols=dev_cols), "coarse", coarse_type,
+        coarse_kernel, coarse_type,
         [
-            pltpu.VMEM((5 * coarse_n, channels), BF16),
-            pltpu.VMEM((5 * coarse_n, channels), BF16),
-            pltpu.VMEM((2 * coarse_n, 5 * coarse_n), F32),
+            pltpu.VMEM((4 * coarse_n, channels), BF16),
+            pltpu.VMEM((4 * coarse_n, channels), BF16),
+            pltpu.VMEM((2 * coarse_n, 4 * coarse_n), F32),
             pltpu.VMEM((coarse_n, channels), BF16),
         ],
         (
-            window_shift, coarse, l1, r1, l2, r2, coarse_gain.reshape(1, channels), coarse_qkv,
+            window_shift, coarse, inside, outside, left, right, coarse_gain.reshape(1, channels), coarse_qkv,
             coarse_proj,
         ),
         COARSE_MIB,
     )
     coarse_other = swapped(coarse_out)
     out = call(
-        functools.partial(expand_kernel, own_cols=dev_cols), "expand",
+        expand_kernel,
         sds(viewed.shape, BF16),
         [
-            pltpu.VMEM((2, channels // 128, coarse_n, 128), F32),
             pltpu.VMEM((2, dev_cols, feats // 128, slots * rows, 128), F32),
         ],
         (

time: 55.3 us -> 54.1 us (0.978)
  Pallas kernels: 19.9 us -> 18.2 us
  waiting for transfers between devices: 18.7 us -> 19.7 us
    ppermute x6 -> x4, starting transfers between devices: 13.1 us -> 8.77 us  [permuted(): lax.ppermute(value, 'lon', [(s, (s + steps) % count) for s in range(count)])]
    ppermute x0 -> x2, starting transfers between devices: none -> 3.85 us  [paired(): lax.ppermute(value, 'lon', [(s, (s + steps[s]) % count) for s in range(co...]
    ppermute x0 -> x2, waiting for transfers between devices: none -> 3.52 us  [paired(): lax.ppermute(value, 'lon', [(s, (s + steps[s]) % count) for s in range(co...]
    ppermute x6 -> x4, waiting for transfers between devices: 16.9 us -> 14.2 us  [permuted(): lax.ppermute(value, 'lon', [(s, (s + steps) % count) for s in range(count)])]
    pallas_call x1, Pallas kernels: 2.58 us -> 1.7 us  [local(): pl.pallas_call(split_kernel, name='split', out_shape=(vhalf, vhalf, sds((...]
    pallas_call x4, Pallas kernels: 17.3 us -> 16.5 us  [call(): pl.pallas_call(kernel, out_shape=outs, in_specs=specs, out_specs=jax.tree...]
where the time goes in v3:
time: 54.1 us; the launch traced here: 53.9 us
  waiting for transfers between devices  19.7 us (36%)
  Pallas kernels  18.2 us (34%)
  starting transfers between devices  13.3 us (25%)
  between operations  1.51 us (3%)
  local copies, waits for them, and re-layouts  0.71 us (1%)
    pallas_call x4, Pallas kernels, call(): pl.pallas_call(kernel, out_shape=outs, in_specs=specs, out_specs=jax.tree...  16.5 us
    ppermute x4, waiting for transfers between devices, permuted(): lax.ppermute(value, 'lon', [(s, (s + steps) % count) for s in range(count)])  14.2 us
    ppermute x4, starting transfers between devices, permuted(): lax.ppermute(value, 'lon', [(s, (s + steps) % count) for s in range(count)])  8.77 us
    ppermute x2, starting transfers between devices, paired(): lax.ppermute(value, 'lon', [(s, (s + steps[s]) % count) for s in range(co...  3.85 us
    ppermute x2, waiting for transfers between devices, paired(): lax.ppermute(value, 'lon', [(s, (s + steps[s]) % count) for s in range(co...  3.52 us
    ppermute x4, waiting for transfers between devices, swapped(): return lax.ppermute(value, 'lon', [(s, s ^ 1) for s in range(count)])  1.96 us
    pallas_call x1, Pallas kernels, local(): pl.pallas_call(split_kernel, name='split', out_shape=(vhalf, vhalf, sds((...  1.7 us
  transfers between devices with their start and end apart: 10, of which 7 were waited for; matrix products, arithmetic and copies ran while one was open for 1% of the time, Pallas kernels for 13%

profile of v3, /device:TPU:0, one launch (start us, length us, event | category | flops | bytes accessed | tf_op | source)
XLA Modules:
  0.0 53.9 jit_solution(4847751297787773648)
XLA Ops:
  0.0 1.7 %split.1 = (bf16[6,2,24,512]{3,2,1,0:T(8,128)(2,1)S(1)}, bf16[6,2,24,512]{3,2,1,0:T(8,128)(2,1)S(1)}, s32[2]{0:T(128)S(1)}) custom-call(s32[2,3]{1,0:T(2,128)} %shift_ref.7, bf16[4,6,24,512]{3,2,1,0:T(8,128)(2,1)} %bitcast.11), custom_call_target="tpu_custom_call" | custom-call | tf_op jit(solution)/shard_map/split/pallas_call | solution.py:393
  1.7 0.6 %collective-permute-start.22 = (bf16[6,2,24,512]{3,2,1,0:T(8,128)(2,1)S(1)}, bf16[6,2,24,512]{3,2,1,0:T(8,128)(2,1)S(1)}, u32[]{:S(2)}, u32[]{:S(2)}) collective-permute-start(bf16[6,2,24,512]{3,2,1,0:T(8,128)(2,1)S(1)} %get-tuple-element.220), channel_id=1, source_target_pairs={{0,1},{1,0},{2,3},{3,2},{4,5},{5,4},{6,7},{7,6},{8,9},{9,8},{10,11... | collective-permute-start | bytes 884744 | tf_op jit(solution)/shard_map/ppermute | solution.py:30
  2.3 0.6 %fusion = (s32[1]{0:T(128)}, s32[1]{0:T(128)}) fusion(s32[2]{0:T(128)S(1)} %get-tuple-element.218), kind=kLoop, calls=%fused_computation.16 | loop fusion | bytes 16 | tf_op jit(solution)/shard_map/slice | solution.py:463
  3.4 0.0 collective-permute-done.22
  3.5 0.1 broadcast_select_fusion.1
  3.6 0.1 pad_maximum_fusion.11
  3.6 0.0 copy-done.6
  3.7 18.9 %conditional.1 = (bf16[12,2,24,512]{3,2,1,0:T(8,128)(2,1)S(1)}, bf16[576,512]{1,0:T(8,128)(2,1)S(1)}, bf16[576,1536]{1,0:T(8,128)(2,1)S(1)}) conditional(s32[]{:T(128)} %bitcast.2, (s32[2,3]{1,0:T(2,128)S(1)}, bf16[12,2,24,512]{3,2,1,0:T(8,128)(2,1)S(1)}, f32[1,512]{1,0:T(1,128)S(1)}, ...), branch_computations={%region_0.1_spmd, %region_1.2_spmd, %region_2.3_spmd, %region_3.4_... | conditional | flops 906264576 | bytes 7667816 | solution.py:439
  3.8 2.9 %collective-permute-start.21 = (bf16[11,2,24,512]{3,2,1,0:T(8,128)(2,1)S(1)}, bf16[11,2,24,512]{3,2,1,0:T(8,128)(2,1)S(1)}, u32[]{:S(2)}, u32[]{:S(2)}) collective-permute-start(bf16[11,2,24,512]{3,2,1,0:T(8,128)(2,1)S(1)} %slice.63), channel_id=1, source_target_pairs={{0,2},{1,3},{2,4},{3,5},{4,6},{5,7},{6,8},{7,9},{8,10},{9,11},{10,... | collective-permute-start | bytes 1622024 | tf_op jit(solution)/shard_map/cond/branch_11_fun/ppermute | solution.py:25
  6.7 3.1 %collective-permute-start.20 = (bf16[1,2,24,512]{3,2,1,0:T(8,128)(2,1)S(1)}, bf16[1,2,24,512]{3,2,1,0:T(8,128)(2,1)S(1)}, u32[]{:S(2)}, u32[]{:S(2)}) collective-permute-start(bf16[1,2,24,512]{3,2,1,0:T(8,128)(2,1)S(1)} %slice.62), channel_id=1, source_target_pairs={{0,14},{1,15},{2,0},{3,1},{4,2},{5,3},{6,4},{7,5},{8,6},{9,7},{10,... | collective-permute-start | bytes 147464 | tf_op jit(solution)/shard_map/cond/branch_11_fun/ppermute | solution.py:25
  9.8 3.1 %branch_11_fun.1 = (bf16[576,512]{1,0:T(8,128)(2,1)S(1)}, bf16[576,1536]{1,0:T(8,128)(2,1)S(1)}) custom-call(s32[2,3]{1,0:T(2,128)S(1)} %get-tuple-element.204.shift_ref, bf16[12,2,24,512]{3,2,1,0:T(8,128)(2,1)S(1)} %get-tuple-element.203.x_ref, f32[1,512]{1,0:T(1,128)S(1)} %get-tuple-element.205.gain_ref, bf16[512,1536]{1,0:T(8,128)(2,1)S(1)} %get-tuple-element.206.qkv_ref), custom_call_target="tpu_custom_call" | custom-call | flops 905969664 | bytes 2949120 | tf_op jit(solution)/shard_map/cond/branch_11_fun/pallas_call | solution.py:357
  12.9 9.5 %collective-permute-done.21 = bf16[11,2,24,512]{3,2,1,0:T(8,128)(2,1)S(1)} collective-permute-done((bf16[11,2,24,512]{3,2,1,0:T(8,128)(2,1)S(1)}, bf16[11,2,24,512]{3,2,1,0:T(8,128)(2,1)S(1)}, u32[]{:S(2)}, u32[]{:S(2)}) %collective-permute-start.21) | collective-permute-done | bytes 540704 | tf_op jit(solution)/shard_map/cond/branch_11_fun/ppermute | solution.py:25
  22.3 0.1 pad_maximum_fusion.10
  22.6 0.0 copy-start.1
  22.6 0.0 copy-start.2
  22.6 0.0 copy-start.5
  22.6 7.4 %shard_map.118 = (bf16[6,2,24,512]{3,2,1,0:T(8,128)(2,1)S(1)}, bf16[6,2,24,512]{3,2,1,0:T(8,128)(2,1)S(1)}, bf16[6,24,512]{2,1,0:T(8,128)(2,1)S(1)}) custom-call(s32[2,3]{1,0:T(2,128)S(1)} %copy-done.7, bf16[12,2,24,512]{3,2,1,0:T(8,128)(2,1)S(1)} %get-tuple-element.221.r_ref, bf16[576,512]{1,0:T(8,128)(2,1)S(1)} %get-tuple-element.222.xw_ref, ...), custom_call_target="tpu_custom_call" | custom-call | tf_op jit(solution)/shard_map/pallas_call | solution.py:357
  30.1 0.0 copy-start
  30.1 0.0 copy-start.4
  30.1 0.1 collective-permute-start.23
  31.0 0.6 %collective-permute-done.23 = bf16[6,24,512]{2,1,0:T(8,128)(2,1)S(1)} collective-permute-done((bf16[6,24,512]{2,1,0:T(8,128)(2,1)S(1)}, bf16[6,24,512]{2,1,0:T(8,128)(2,1)S(1)}, u32[]{:S(2)}, u32[]{:S(2)}) %collective-permute-start.23) | collective-permute-done | bytes 147488 | tf_op jit(solution)/shard_map/ppermute | solution.py:30
  31.6 0.1 broadcast_select_fusion.2.own_ref
  31.6 2.8 %collective-permute-start.27 = (bf16[6,24,512]{2,1,0:T(8,128)(2,1)S(1)}, bf16[6,24,512]{2,1,0:T(8,128)(2,1)S(1)}, u32[]{:S(2)}, u32[]{:S(2)}) collective-permute-start(bf16[6,24,512]{2,1,0:T(8,128)(2,1)S(1)} %broadcast_select_fusion.2.own_ref), channel_id=1, source_target_pairs={{0,12},{1,13},{2,14},{3,15},{4,0},{5,1},{6,2},{7,3},{8,4},{9,5},{1... | collective-permute-start | bytes 442376 | tf_op jit(solution)/shard_map/ppermute | solution.py:25
  34.4 3.8 %collective-permute-start.25 = (bf16[6,24,512]{2,1,0:T(8,128)(2,1)S(1)}, bf16[6,24,512]{2,1,0:T(8,128)(2,1)S(1)}, u32[]{:S(2)}, u32[]{:S(2)}) collective-permute-start(bf16[6,24,512]{2,1,0:T(8,128)(2,1)S(1)} %broadcast_select_fusion.2.own_ref), channel_id=1, source_target_pairs={{0,14},{1,15},{2,4},{3,5},{4,2},{5,3},{6,8},{7,9},{8,6},{9,7},{10,... | collective-permute-start | bytes 442376 | tf_op jit(solution)/shard_map/ppermute | solution.py:36
  38.2 0.4 collective-permute-done.27.right_ref
  38.7 4.3 %collective-permute-done.26.left_ref = bf16[6,24,512]{2,1,0:T(8,128)(2,1)S(1)} collective-permute-done((bf16[6,24,512]{2,1,0:T(8,128)(2,1)S(1)}, bf16[6,24,512]{2,1,0:T(8,128)(2,1)S(1)}, u32[]{:S(2)}, u32[]{:S(2)}) %collective-permute-start.26) | collective-permute-done | bytes 147488 | tf_op jit(solution)/shard_map/ppermute | solution.py:25
  42.9 2.2 %collective-permute-done.25.outside_ref = bf16[6,24,512]{2,1,0:T(8,128)(2,1)S(1)} collective-permute-done((bf16[6,24,512]{2,1,0:T(8,128)(2,1)S(1)}, bf16[6,24,512]{2,1,0:T(8,128)(2,1)S(1)}, u32[]{:S(2)}, u32[]{:S(2)}) %collective-permute-start.25) | collective-permute-done | bytes 147488 | tf_op jit(solution)/shard_map/ppermute | solution.py:36
  45.2 1.3 %collective-permute-done.24.inside_ref = bf16[6,24,512]{2,1,0:T(8,128)(2,1)S(1)} collective-permute-done((bf16[6,24,512]{2,1,0:T(8,128)(2,1)S(1)}, bf16[6,24,512]{2,1,0:T(8,128)(2,1)S(1)}, u32[]{:S(2)}, u32[]{:S(2)}) %collective-permute-start.24) | collective-permute-done | bytes 147488 | tf_op jit(solution)/shard_map/ppermute | solution.py:36
  46.5 3.7 %shard_map.119.own_ref = bf16[6,24,512]{2,1,0:T(8,128)(2,1)S(1)} custom-call(s32[2,3]{1,0:T(2,128)S(1)} %copy-done.7, bf16[6,24,512]{2,1,0:T(8,128)(2,1)S(1)} %broadcast_select_fusion.2.own_ref, bf16[6,24,512]{2,1,0:T(8,128)(2,1)S(1)} %collective-permute-done.24.inside_ref, bf16[6,24,512]{2,1,0:T(8,128)(2,1)S(1)} %collective-permute-done.25.outside_ref, ...), custom_call_target="tpu_custom_call" | custom-call | tf_op jit(solution)/shard_map/pallas_call | solution.py:357
  50.2 0.1 collective-permute-start.28
  50.3 1.3 %collective-permute-done.28.other_ref = bf16[6,24,512]{2,1,0:T(8,128)(2,1)S(1)} collective-permute-done((bf16[6,24,512]{2,1,0:T(8,128)(2,1)S(1)}, bf16[6,24,512]{2,1,0:T(8,128)(2,1)S(1)}, u32[]{:S(2)}, u32[]{:S(2)}) %collective-permute-start.28) | collective-permute-done | bytes 147488 | tf_op jit(solution)/shard_map/ppermute | solution.py:30
  51.7 2.2 %shard_map.120 = bf16[4,6,24,512]{3,2,1,0:T(8,128)(2,1)} custom-call(s32[2,3]{1,0:T(2,128)S(1)} %copy-done.7, bf16[6,24,512]{2,1,0:T(8,128)(2,1)S(1)} %shard_map.119.own_ref, bf16[6,24,512]{2,1,0:T(8,128)(2,1)S(1)} %collective-permute-done.28.other_ref, bf16[6,2,24,512]{3,2,1,0:T(8,128)(2,1)S(1)} %get-tuple-element.225.fkeep_ref, ...), custom_call_target="tpu_custom_call" | custom-call | tf_op jit(solution)/shard_map/pallas_call | solution.py:357
  (20 shorter events, 0.1 us)
Async XLA Ops:
  0.0 3.6 %copy-start.7 = (s32[2,3]{1,0:T(2,128)S(1)}, s32[2,3]{1,0:T(2,128)}, u32[]{:S(2)}) copy-start(s32[2,3]{1,0:T(2,128)} %shift_ref.7) | copy-start | bytes 76
  0.0 3.6 %copy-start.8 = (f32[512]{0:T(512)S(1)}, f32[512]{0:T(512)}, u32[]{:S(2)}) copy-start(f32[512]{0:T(512)} %param.26) | copy-start | bytes 6148
  1.7 1.8 %collective-permute-start.22 = (bf16[6,2,24,512]{3,2,1,0:T(8,128)(2,1)S(1)}, bf16[6,2,24,512]{3,2,1,0:T(8,128)(2,1)S(1)}, u32[]{:S(2)}, u32[]{:S(2)}) collective-permute-start(bf16[6,2,24,512]{3,2,1,0:T(8,128)(2,1)S(1)} %get-tuple-element.220), channel_id=1, source_target_pairs={{0,1},{1,0},{2,3},{3,2},{4,5},{5,4},{6,7},{7,6},{8,9},{9,8},{10,11... | collective-permute-start | bytes 884744 | tf_op jit(solution)/shard_map/ppermute | solution.py:30
  2.3 1.4 %copy-start.6 = (bf16[512,1536]{1,0:T(8,128)(2,1)S(1)}, bf16[512,1536]{1,0:T(8,128)(2,1)}, u32[]{:S(2)}) copy-start(bf16[512,1536]{1,0:T(8,128)(2,1)} %qkv_hbm.1) | copy-start | bytes 4718596
  3.7 18.9 %copy-start.3 = (f32[2048]{0:T(1024)S(1)}, f32[2048]{0:T(1024)}, u32[]{:S(2)}) copy-start(f32[2048]{0:T(1024)} %param.29) | copy-start | bytes 24580
  3.8 18.6 %collective-permute-start.21 = (bf16[11,2,24,512]{3,2,1,0:T(8,128)(2,1)S(1)}, bf16[11,2,24,512]{3,2,1,0:T(8,128)(2,1)S(1)}, u32[]{:S(2)}, u32[]{:S(2)}) collective-permute-start(bf16[11,2,24,512]{3,2,1,0:T(8,128)(2,1)S(1)} %slice.63), channel_id=1, source_target_pairs={{0,2},{1,3},{2,4},{3,5},{4,6},{5,7},{6,8},{7,9},{8,10},{9,11},{10,... | collective-permute-start | bytes 1622024 | tf_op jit(solution)/shard_map/cond/branch_11_fun/ppermute | solution.py:25
  6.7 6.2 %collective-permute-start.20 = (bf16[1,2,24,512]{3,2,1,0:T(8,128)(2,1)S(1)}, bf16[1,2,24,512]{3,2,1,0:T(8,128)(2,1)S(1)}, u32[]{:S(2)}, u32[]{:S(2)}) collective-permute-start(bf16[1,2,24,512]{3,2,1,0:T(8,128)(2,1)S(1)} %slice.62), channel_id=1, source_target_pairs={{0,14},{1,15},{2,0},{3,1},{4,2},{5,3},{6,4},{7,5},{8,6},{9,7},{10,... | collective-permute-start | bytes 147464 | tf_op jit(solution)/shard_map/cond/branch_11_fun/ppermute | solution.py:25
  22.6 23.9 %copy-start.1 = (bf16[512,1536]{1,0:T(8,128)(2,1)S(1)}, bf16[512,1536]{1,0:T(8,128)(2,1)}, u32[]{:S(2)}) copy-start(bf16[512,1536]{1,0:T(8,128)(2,1)} %qkv_ref.1) | copy-start | bytes 4718596
  22.6 23.9 %copy-start.2 = (bf16[512,512]{1,0:T(8,128)(2,1)S(1)}, bf16[512,512]{1,0:T(8,128)(2,1)}, u32[]{:S(2)}) copy-start(bf16[512,512]{1,0:T(8,128)(2,1)} %proj_ref.1) | copy-start | bytes 1572868
  22.6 23.8 %copy-start.5 = (f32[512]{0:T(512)S(1)}, f32[512]{0:T(512)}, u32[]{:S(2)}) copy-start(f32[512]{0:T(512)} %param.31) | copy-start | bytes 6148
  30.1 21.6 %copy-start = (bf16[512,2048]{1,0:T(8,128)(2,1)S(1)}, bf16[512,2048]{1,0:T(8,128)(2,1)}, u32[]{:S(2)}) copy-start(bf16[512,2048]{1,0:T(8,128)(2,1)} %weight_ref.1) | copy-start | bytes 6291460
  30.1 21.6 %copy-start.4 = (f32[512]{0:T(512)S(1)}, f32[512]{0:T(512)}, u32[]{:S(2)}) copy-start(f32[512]{0:T(512)} %param.35) | copy-start | bytes 6148
  30.1 1.4 %collective-permute-start.23 = (bf16[6,24,512]{2,1,0:T(8,128)(2,1)S(1)}, bf16[6,24,512]{2,1,0:T(8,128)(2,1)S(1)}, u32[]{:S(2)}, u32[]{:S(2)}) collective-permute-start(bf16[6,24,512]{2,1,0:T(8,128)(2,1)S(1)} %get-tuple-element.224), channel_id=1, source_target_pairs={{0,1},{1,0},{2,3},{3,2},{4,5},{5,4},{6,7},{7,6},{8,9},{9,8},{10,11... | collective-permute-start | bytes 442376 | tf_op jit(solution)/shard_map/ppermute | solution.py:30
  31.6 7.0 %collective-permute-start.27 = (bf16[6,24,512]{2,1,0:T(8,128)(2,1)S(1)}, bf16[6,24,512]{2,1,0:T(8,128)(2,1)S(1)}, u32[]{:S(2)}, u32[]{:S(2)}) collective-permute-start(bf16[6,24,512]{2,1,0:T(8,128)(2,1)S(1)} %broadcast_select_fusion.2.own_ref), channel_id=1, source_target_pairs={{0,12},{1,13},{2,14},{3,15},{4,0},{5,1},{6,2},{7,3},{8,4},{9,5},{1... | collective-permute-start | bytes 442376 | tf_op jit(solution)/shard_map/ppermute | solution.py:25
  34.4 8.6 %collective-permute-start.26 = (bf16[6,24,512]{2,1,0:T(8,128)(2,1)S(1)}, bf16[6,24,512]{2,1,0:T(8,128)(2,1)S(1)}, u32[]{:S(2)}, u32[]{:S(2)}) collective-permute-start(bf16[6,24,512]{2,1,0:T(8,128)(2,1)S(1)} %broadcast_select_fusion.2.own_ref), channel_id=1, source_target_pairs={{0,4},{1,5},{2,6},{3,7},{4,8},{5,9},{6,10},{7,11},{8,12},{9,13},{1... | collective-permute-start | bytes 442376 | tf_op jit(solution)/shard_map/ppermute | solution.py:25
  34.4 10.8 %collective-permute-start.25 = (bf16[6,24,512]{2,1,0:T(8,128)(2,1)S(1)}, bf16[6,24,512]{2,1,0:T(8,128)(2,1)S(1)}, u32[]{:S(2)}, u32[]{:S(2)}) collective-permute-start(bf16[6,24,512]{2,1,0:T(8,128)(2,1)S(1)} %broadcast_select_fusion.2.own_ref), channel_id=1, source_target_pairs={{0,14},{1,15},{2,4},{3,5},{4,2},{5,3},{6,8},{7,9},{8,6},{9,7},{10,... | collective-permute-start | bytes 442376 | tf_op jit(solution)/shard_map/ppermute | solution.py:36
  38.2 8.2 %collective-permute-start.24 = (bf16[6,24,512]{2,1,0:T(8,128)(2,1)S(1)}, bf16[6,24,512]{2,1,0:T(8,128)(2,1)S(1)}, u32[]{:S(2)}, u32[]{:S(2)}) collective-permute-start(bf16[6,24,512]{2,1,0:T(8,128)(2,1)S(1)} %broadcast_select_fusion.2.own_ref), channel_id=1, source_target_pairs={{0,2},{1,3},{2,0},{3,1},{4,6},{5,7},{6,4},{7,5},{8,10},{9,11},{10,... | collective-permute-start | bytes 442376 | tf_op jit(solution)/shard_map/ppermute | solution.py:36
  38.2 12.1 %collective-permute-start.29 = (bf16[6,2,24,512]{3,2,1,0:T(8,128)(2,1)S(1)}, bf16[6,2,24,512]{3,2,1,0:T(8,128)(2,1)S(1)}, u32[]{:S(2)}, u32[]{:S(2)}) collective-permute-start(bf16[6,2,24,512]{3,2,1,0:T(8,128)(2,1)S(1)} %get-tuple-element.226), channel_id=1, source_target_pairs={{0,1},{1,0},{2,3},{3,2},{4,5},{5,4},{6,7},{7,6},{8,9},{9,8},{10,11... | collective-permute-start | bytes 884744 | tf_op jit(solution)/shard_map/ppermute | solution.py:30
  50.2 1.4 %collective-permute-start.28 = (bf16[6,24,512]{2,1,0:T(8,128)(2,1)S(1)}, bf16[6,24,512]{2,1,0:T(8,128)(2,1)S(1)}, u32[]{:S(2)}, u32[]{:S(2)}) collective-permute-start(bf16[6,24,512]{2,1,0:T(8,128)(2,1)S(1)} %shard_map.119.own_ref), channel_id=1, source_target_pairs={{0,1},{1,0},{2,3},{3,2},{4,5},{5,4},{6,7},{7,6},{8,9},{9,8},{10,11... | collective-permute-start | bytes 442376 | tf_op jit(solution)/shard_map/ppermute | solution.py:30

commit v4 on v3

--- a/solution.py
+++ b/solution.py
@@ -1,3 +1,5 @@
+import functools
+
 import jax
 import jax.numpy as jnp
 from jax import lax
@@ -12,6 +14,8 @@
 WIN_LON = 12
 EPSILON = 1e-05
 NEG = -1e30
+FEW = 3
+MERGE_MIB = 12
 OWN_MIB = 8
 FINE_MIB = 24
 COARSE_MIB = 16
@@ -20,9 +24,9 @@
 BF16 = jnp.bfloat16
 
 
-def permuted(value, steps):
+def permuted(value, steps, flip=0):
     count = lax.axis_size("lon")
-    return lax.ppermute(value, "lon", [(s, (s + steps) % count) for s in range(count)])
+    return lax.ppermute(value, "lon", [(s, (s + steps) % count ^ flip) for s in range(count)])
 
 
 def swapped(value):
@@ -54,6 +58,10 @@
     if slot == 0:
         return 2 * core
     return jnp.where(core == 0, 1 + 2 * a, 3 - 2 * a)
+
+
+def is_wide(c):
+    return (c > FEW) & (c < WIN_LON - FEW)
 
 
 def iota(shape, axis):
@@ -103,11 +111,16 @@
     return jnp.concatenate([jnp.where(far, two, one), jnp.where(far, one, two)], axis=1)
 
 
-def split_kernel(shift_ref, tok_ref, keep_ref, send_ref, branch_ref):
+def split_kernel(shift_ref, tok_ref, keep_ref, send_ref, go_ref, back_ref, table_ref):
     core = lax.axis_index("lon") % 2
     a = shift_ref[0, 0]
-    branch_ref[0] = shift_ref[0, 2]
-    branch_ref[1] = jnp.where(a == shift_ref[1, 0], 0, 1)
+    for n in range(2):
+        for m in range(3):
+            table_ref[n, m] = shift_ref[n, m]
+    c = shift_ref[0, 2]
+    go_ref[0] = c
+    few = jnp.where(is_wide(c), 0, jnp.where(c <= FEW, c, c - (WIN_LON - 2 * FEW - 1)))
+    back_ref[0] = few + jnp.where(a == shift_ref[1, 0], 0, 2 * FEW + 1)
     for target, out_ref in ((1 - core, send_ref), (core, keep_ref)):
         for slot in range(2):
             level = level_of(target, slot, a)
@@ -129,6 +142,17 @@
     return lambda slot: ref[col, slot].astype(F32)
 
 
+def ahead_kernel(weight_hbm, gain_hbm, weight_ref, gain_ref, sems):
+    loads = [
+        pltpu.make_async_copy(weight_hbm, weight_ref, sems.at[0]),
+        pltpu.make_async_copy(gain_hbm, gain_ref, sems.at[1]),
+    ]
+    for load in loads:
+        load.start()
+    for load in loads:
+        load.wait()
+
+
 def own_kernel(shift_ref, x_ref, gain_ref, qkv_ref, xw_ref, out_ref, xs):
     cols, slots, rows, _ = x_ref.shape
     unit = slots * cols
@@ -147,43 +171,43 @@
 
 
 def fine_kernel(
-    shift_ref, r_ref, xw_ref, qkv, gain_ref, qkv_hbm, proj_hbm, mgain_ref, mw_hbm,
-    keep_ref, send_ref, coarse_ref,
-    rs, kvr, mix, fr, fu, bias, kv_w, proj_ref, mw_ref, sems,
+    shift_ref, r_ref, xw_ref, qkv, gain_ref, qkv_hbm, proj_hbm,
+    out_ref,
+    rs, kvr, mix, fr, bias, kv_w, proj_ref, sems,
 ):
     core = lax.axis_index("lon") % 2
     cols, slots, rows, feats = r_ref.shape
-    own_cols = cols // 2
     unit = slots * cols
     wins = rows // WIN_LAT
     size = WIN_LAT * unit
     a, b, c = shift_ref[0, 0], shift_ref[0, 1], shift_ref[0, 2]
-    loads = [
-        pltpu.make_async_copy(source, target, sems.at[n])
-        for n, (source, target) in enumerate(
-            (
-                (qkv_hbm.at[:, pl.ds(feats, 2 * feats)], kv_w),
-                (proj_hbm, proj_ref),
-                (mw_hbm, mw_ref),
-            )
-        )
-    ]
-    for load in loads:
-        load.start()
-    by_window([reader(r_ref, col) for col in range(cols)], rs)
-    gain = gain_ref[...]
-    loads[0].wait()
-    for j in range(wins):
-        tokens = take(rs, pl.multiple_of(((j + 1) * WIN_LAT - b) * unit, 8), size)
-        normed = layer_norm(tokens, gain).astype(BF16)
-        kvr[pl.ds(j * size, size), :] = dot(normed, kv_w[...]).astype(BF16)
+    wide = is_wide(c)
+    load = pltpu.make_async_copy(proj_hbm, proj_ref, sems.at[1])
+
+    @pl.when(wide)
+    def _():
+        first = pltpu.make_async_copy(qkv_hbm.at[:, pl.ds(feats, 2 * feats)], kv_w, sems.at[0])
+        first.start()
+        by_window([reader(r_ref, col) for col in range(cols)], rs)
+        gain = gain_ref[...]
+        first.wait()
+        for j in range(wins):
+            tokens = take(rs, pl.multiple_of(((j + 1) * WIN_LAT - b) * unit, 8), size)
+            normed = layer_norm(tokens, gain).astype(BF16)
+            kvr[pl.ds(j * size, size), :] = dot(normed, kv_w[...]).astype(BF16)
+
+    @pl.when(jnp.logical_not(wide))
+    def _():
+        kvr[...] = jnp.zeros_like(kvr)
+
+    load.start()
 
     def parts(index):
         return index // unit, (index // cols) % slots, index % cols
 
     q_row, q_slot, _ = parts(iota((2 * size, 1), 0) % size)
     k_row, k_slot, _ = parts(iota((1, size), 1))
-    far = iota((size, 128), 0) % cols + c >= cols
+    far = iota((size, 128), 0) % cols + jnp.where(wide, c, 0) >= cols
     apart = jnp.where((a == 0) | (core == 1), 0, 1)
     q_slot, k_slot = q_slot * apart, k_slot * apart
     q_id = q_slot * 2 + jnp.where(q_row < b, 1, 0)
@@ -208,46 +232,51 @@
                 far,
             ).astype(BF16)
 
-    half = rows // 2
-    loads[1].wait()
+    load.wait()
     for j in range(wins):
         at = pl.ds(j * size, size)
         fine = xw_ref[at, :].astype(F32) + dot(mix[at, :], proj_ref[...])
-        fine = fine.astype(BF16).astype(F32)
         for inner in range(WIN_LAT):
             source = j * WIN_LAT + inner - b
             source = jnp.where(source < 0, source + rows, source)
             put(fr, pl.multiple_of(source * unit, 8), fine[inner * unit : (inner + 1) * unit])
-
-    block = slots * half
-    for p in range(2):
-        for slot in range(slots):
-            for col in range(cols):
-                piece = take(fr, p * unit + slot * cols + col, half, 2 * unit)
-                put(fu, (p * cols + col) * block + slot * half, piece)
-    loads[2].wait()
+    for slot in range(slots):
+        for col in range(cols):
+            out_ref[col, slot] = take(fr, slot * cols + col, rows, unit).astype(BF16)
+
+
+def merge_kernel(f_ref, mgain_ref, mw_hbm, keep_ref, send_ref, coarse_ref, fs, mw_ref, sems):
+    core = lax.axis_index("lon") % 2
+    cols, slots, rows, feats = f_ref.shape
+    loads = []
+    for k in range(4):
+        at = pl.ds(k * feats, feats)
+        loads.append(pltpu.make_async_copy(mw_hbm.at[at], mw_ref.at[at], sems.at[k]))
+        loads[k].start()
+    for col in range(cols):
+        put(fs, col * slots * rows, f_ref[col].astype(F32).reshape(slots * rows, feats))
+    own_cols = cols // 2
+    for col in range(own_cols):
+        keep_ref[col] = f_ref[core * own_cols + col]
+        send_ref[col] = f_ref[(1 - core) * own_cols + col]
     groups = []
-    count = half * unit // 2
+    block = slots * rows // 2
     for q in range(2):
         for p in range(2):
-            starts = [(p * cols + col) * block for col in range(q, cols, 2)]
-            groups.append(jnp.concatenate([take(fu, start, block) for start in starts], axis=0))
+            starts = [col * slots * rows + p for col in range(q, cols, 2)]
+            groups.append(jnp.concatenate([take(fs, start, block, 2) for start in starts], axis=0))
     width = 4 * feats
     mean = sum(jnp.sum(piece, axis=-1, keepdims=True) for piece in groups) / width
     groups = [piece - mean for piece in groups]
     spread = sum(jnp.sum(piece * piece, axis=-1, keepdims=True) for piece in groups) / width
     scaling = lax.rsqrt(spread + EPSILON)
-    total = jnp.zeros((count, mw_ref.shape[1]), F32)
+    total = jnp.zeros((own_cols * block, mw_ref.shape[1]), F32)
     for k, piece in enumerate(groups):
         lanes = slice(k * feats, (k + 1) * feats)
         merged = (piece * scaling * mgain_ref[:, lanes]).astype(BF16)
+        loads[k].wait()
         total = total + dot(merged, mw_ref[lanes, :])
     coarse_ref[...] = total.astype(BF16).reshape(coarse_ref.shape)
-    for slot in range(slots):
-        for col in range(own_cols):
-            for target, out_ref in ((core, keep_ref), (1 - core, send_ref)):
-                start = slot * cols + target * own_cols + col
-                out_ref[col, slot] = take(fr, start, rows, unit).astype(BF16)
 
 
 def coarse_kernel(
@@ -317,7 +346,6 @@
     slots = 2
     rows = 2 * units // slots
     home = own_cols // 2
-    a1, a2 = shift_ref[0, 0], shift_ref[1, 0]
     blocks = []
     for ref in (own_ref, other_ref):
         for col in range(home):
@@ -334,10 +362,9 @@
                     put(ex.at[which, 2 * col + q], p, piece[first : first + units], 2)
     for which, (target, f_ref) in enumerate(((core, fkeep_ref), (1 - core, fother_ref))):
         for slot in range(slots):
-            level = level_of(target, slot, a1)
-            source = which if slot == 0 else jnp.where(a1 == a2, which, 1 - which)
+            level = level_of(target, slot, shift_ref[1, 0])
             for col in range(2 * home):
-                add = take(ex.at[source, col], slot * rows, rows)
+                add = take(ex.at[which, col], slot * rows, rows)
                 out_ref[level, col] = (f_ref[col, slot].astype(F32) + add).astype(BF16)
 
 
@@ -349,7 +376,7 @@
 
 
 def call(kernel, outs, scratch, arrays, limit, cost=None, hbm=()):
-    specs = [SMEM_SPEC] + [VMEM_SPEC] * (len(arrays) - 1)
+    specs = [SMEM_SPEC if one.dtype == jnp.int32 else VMEM_SPEC for one in arrays]
     arrays = list(arrays)
     for n in hbm:
         specs[n] = HBM_SPEC
@@ -390,22 +417,31 @@
 
     half = sds((dev_cols, slots, rows, feats), BF16)
     vhalf = pltpu.VMEM(half.shape, BF16)
-    keep, send, index = pl.pallas_call(
+    one = sds((1,), jnp.int32)
+    in_hbm = functools.partial(pltpu.with_memory_space_constraint, memory_space=pltpu.HBM)
+    keep, send, go, back, table = pl.pallas_call(
         split_kernel,
         name="split",
-        out_shape=(vhalf, vhalf, sds((2,), jnp.int32)),
+        out_shape=(vhalf, vhalf, one, one, sds((2, 3), jnp.int32)),
         in_specs=[SMEM_SPEC, VMEM_SPEC],
-        out_specs=(VMEM_SPEC, VMEM_SPEC, SMEM_SPEC),
+        out_specs=(VMEM_SPEC, VMEM_SPEC, SMEM_SPEC, SMEM_SPEC, SMEM_SPEC),
         compiler_params=pltpu.CompilerParams(vmem_limit_bytes=4 << 20),
-    )(window_shift, pltpu.with_memory_space_constraint(viewed, pltpu.HBM))
+    )(in_hbm(window_shift), in_hbm(viewed))
     other = swapped(send)
+    own_w, gain = call(
+        ahead_kernel,
+        (pltpu.VMEM(fine_qkv.shape, BF16), pltpu.VMEM((1, feats), F32)),
+        [pltpu.SemaphoreType.DMA((2,))],
+        (fine_qkv, fine_gain.reshape(1, feats)),
+        6,
+        hbm=(0, 1),
+    )
     grid = jnp.concatenate(
         [jnp.where(core == 0, keep, other), jnp.where(core == 0, other, keep)], axis=0
     )
     unit = slots * cols
     tokens_n = rows * unit
     size = WIN_LAT * unit
-    gain = fine_gain.reshape(1, feats)
 
     channels = merge_weight.shape[1]
     coarse_depth = rows // 2 * slots
@@ -415,7 +451,11 @@
     def branch(c):
         def run(grid):
             around = grid
-            if c > 0:
+            if c > WIN_LON - 1 - FEW:
+                grid = jnp.concatenate([permuted(grid[: cols - c], -2), grid[cols - c :]], axis=0)
+            elif 0 < c <= FEW:
+                grid = jnp.concatenate([grid[: cols - c], permuted(grid[cols - c :], 2)], axis=0)
+            elif c > 0:
                 left = permuted(grid[: cols - c], -2)
                 right = permuted(grid[cols - c :], 2)
                 around = jnp.concatenate([left, right], axis=0)
@@ -423,7 +463,7 @@
                 own_kernel,
                 (pltpu.VMEM((tokens_n, feats), BF16), pltpu.VMEM((tokens_n, 3 * feats), BF16)),
                 [chunked(tokens_n + size, feats)],
-                (window_shift, grid, gain, fine_qkv),
+                (table, grid, gain, own_w),
                 OWN_MIB,
                 pl.CostEstimate(
                     flops=tokens_n * feats * feats * 6,
@@ -436,32 +476,58 @@
         return run
 
     branches = [branch(c) for c in range(WIN_LON)]
-    around, xw, qkv = lax.switch(index[0], branches, grid)
-    fine_keep, fine_send, coarse = call(
-        fine_kernel, (half, half, coarse_type),
+    around, xw, qkv = lax.switch(go.reshape(()), branches, grid)
+    fine = call(
+        fine_kernel, pltpu.VMEM(grid.shape, BF16),
         [
             chunked(tokens_n + size, feats),
             pltpu.VMEM((tokens_n, 2 * feats), BF16),
             pltpu.VMEM((tokens_n, feats), BF16),
             chunked(tokens_n, feats),
-            chunked(tokens_n, feats),
             pltpu.VMEM((2, 2 * size, size), F32),
             pltpu.VMEM((feats, 2 * feats), BF16),
             pltpu.VMEM(fine_proj.shape, BF16),
+            pltpu.SemaphoreType.DMA((2,)),
+        ],
+        (table, around, xw, qkv, gain, fine_qkv, fine_proj),
+        FINE_MIB,
+        hbm=(5, 6),
+    )
+
+    def returned(c, crossed):
+        def run(fine):
+            first, last = (cols - c, cols) if c > FEW else (0, cols - c)
+            held = fine[first:last]
+            moved = fine[:first] if c > FEW else fine[last:]
+            steps = 2 if c > FEW else -2
+            if crossed:
+                held = jnp.stack([held[:, 0], swapped(held[:, 1])], axis=1)
+            if c == 0:
+                return held
+            if crossed:
+                moved = [permuted(moved[:, 0], steps), permuted(moved[:, 1], steps, 1)]
+                moved = jnp.stack(moved, axis=1)
+            else:
+                moved = permuted(moved, steps)
+            return jnp.concatenate([moved, held] if c > FEW else [held, moved], axis=0)
+
+        return run
+
+    few = [*range(FEW + 1), *range(WIN_LON - FEW, WIN_LON)]
+    branches = [returned(c, crossed) for crossed in (False, True) for c in few]
+    fine = lax.switch(back.reshape(()), branches, fine)
+    fine_keep, fine_send, coarse = call(
+        merge_kernel, (half, half, coarse_type),
+        [
+            chunked(tokens_n, feats),
             pltpu.VMEM(merge_weight.shape, BF16),
-            pltpu.SemaphoreType.DMA((3,)),
+            pltpu.SemaphoreType.DMA((4,)),
         ],
-        (
-            window_shift, around, xw, qkv, gain, fine_qkv, fine_proj,
-            merge_gain.reshape(1, 4 * feats), merge_weight,
-        ),
-        FINE_MIB,
-        hbm=(5, 6, 8),
+        (fine, merge_gain.reshape(1, 4 * feats), merge_weight),
+        MERGE_MIB,
+        hbm=(2,),
     )
     fine_other = swapped(fine_send)
-    upper = jnp.arange(coarse_depth, dtype=jnp.int32)[None, :, None] >= coarse_depth // 2
-    coarse = jnp.where(upper & (index[1] == 1), swapped(coarse), coarse)
-
     right = permuted(coarse, -4)
     outside = paired(coarse, False)
     inside = paired(coarse, True)
@@ -475,7 +541,7 @@
             pltpu.VMEM((coarse_n, channels), BF16),
         ],
         (
-            window_shift, coarse, inside, outside, left, right, coarse_gain.reshape(1, channels), coarse_qkv,
+            table, coarse, inside, outside, left, right, coarse_gain.reshape(1, channels), coarse_qkv,
             coarse_proj,
         ),
         COARSE_MIB,
@@ -488,7 +554,7 @@
             pltpu.VMEM((2, dev_cols, feats // 128, slots * rows, 128), F32),
         ],
         (
-            window_shift, coarse_out, coarse_other, fine_keep, fine_other,
+            table, coarse_out, coarse_other, fine_keep, fine_other,
             expand_gain.reshape(1, feats), expand_weight,
         ),
         EXPAND_MIB,

time: 54.1 us -> 52.2 us (0.965)
  waiting for transfers between devices: 19.7 us -> 17.8 us
  Pallas kernels: 18.2 us -> 19.6 us
  starting transfers between devices: 13.3 us -> 12.6 us
    pallas_call x4 -> x6, Pallas kernels: 16.5 us -> 17.9 us  [call(): pl.pallas_call(kernel, out_shape=outs, in_specs=specs, out_specs=jax.tree...]
    ppermute x2, waiting for transfers between devices: 3.52 us -> 2.6 us  [paired(): lax.ppermute(value, 'lon', [(s, (s + steps[s]) % count) for s in range(co...]
    ppermute x2, starting transfers between devices: 3.85 us -> 2.94 us  [paired(): lax.ppermute(value, 'lon', [(s, (s + steps[s]) % count) for s in range(co...]
    ppermute x4, waiting for transfers between devices: 1.96 us -> 1.37 us  [swapped(): return lax.ppermute(value, 'lon', [(s, s ^ 1) for s in range(count)])]
    slice x3 -> x2, local copies, waits for them, and re-layouts: 0.62 us -> 0.04 us  [the longest x1 0.04 us: run(): grid[cols - c:]]
    ppermute x4 -> x5, waiting for transfers between devices: 14.2 us -> 13.8 us  [permuted(): lax.ppermute(value, 'lon', [(s, (s + steps) % count ^ flip) for s in rang...]
    ppermute x4 -> x5, starting transfers between devices: 8.77 us -> 8.97 us  [permuted(): lax.ppermute(value, 'lon', [(s, (s + steps) % count ^ flip) for s in rang...]
  transfers between devices with their start and end apart: 10 -> 11, of which waited for: 7 -> 7; matrix products, arithmetic and copies ran while one was open for 1% -> 0% of each run, Pallas kernels for 13% -> 10%
where the time goes in v4:
time: 52.2 us; the launch traced here: 52 us
  Pallas kernels  19.6 us (38%)
  waiting for transfers between devices  17.8 us (34%)
  starting transfers between devices  12.6 us (24%)
  between operations  1.45 us (3%)
    pallas_call x6, Pallas kernels, call(): pl.pallas_call(kernel, out_shape=outs, in_specs=specs, out_specs=jax.tree...  17.9 us
    ppermute x5, waiting for transfers between devices, permuted(): lax.ppermute(value, 'lon', [(s, (s + steps) % count ^ flip) for s in rang...  13.8 us
    ppermute x5, starting transfers between devices, permuted(): lax.ppermute(value, 'lon', [(s, (s + steps) % count ^ flip) for s in rang...  8.97 us
    ppermute x2, starting transfers between devices, paired(): lax.ppermute(value, 'lon', [(s, (s + steps[s]) % count) for s in range(co...  2.94 us
    ppermute x2, waiting for transfers between devices, paired(): lax.ppermute(value, 'lon', [(s, (s + steps[s]) % count) for s in range(co...  2.6 us
    pallas_call x1, Pallas kernels, local(): pl.pallas_call(split_kernel, name='split', out_shape=(vhalf, vhalf, one,...  1.7 us
    ppermute x4, waiting for transfers between devices, swapped(): return lax.ppermute(value, 'lon', [(s, s ^ 1) for s in range(count)])  1.37 us
  transfers between devices with their start and end apart: 11, of which 7 were waited for; matrix products, arithmetic and copies ran while one was open for 0% of the time, Pallas kernels for 10%

profile of v4, /device:TPU:0, one launch (start us, length us, event | category | flops | bytes accessed | tf_op | source)
XLA Modules:
  0.0 52.0 jit_solution(9555574552750048049)
XLA Ops:
  0.0 1.7 %split.1 = (bf16[6,2,24,512]{3,2,1,0:T(8,128)(2,1)S(1)}, bf16[6,2,24,512]{3,2,1,0:T(8,128)(2,1)S(1)}, s32[1]{0:T(128)}, s32[1]{0:T(128)}, s32[2,3]{1,0:T(2,128)S(1)}) custom-call(s32[2,3]{1,0:T(2,128)} %shift_ref.1, bf16[4,6,24,512]{3,2,1,0:T(8,128)(2,1)} %bitcast.116), custom_call_target="tpu_custom_call" | custom-call | tf_op jit(solution)/shard_map/split/pallas_call | solution.py:422
  1.7 0.6 %collective-permute-start.41 = (bf16[6,2,24,512]{3,2,1,0:T(8,128)(2,1)S(1)}, bf16[6,2,24,512]{3,2,1,0:T(8,128)(2,1)S(1)}, u32[]{:S(2)}, u32[]{:S(2)}) collective-permute-start(bf16[6,2,24,512]{3,2,1,0:T(8,128)(2,1)S(1)} %get-tuple-element.255), channel_id=1, source_target_pairs={{0,1},{1,0},{2,3},{3,2},{4,5},{5,4},{6,7},{7,6},{8,9},{9,8},{10,11... | collective-permute-start | bytes 884744 | tf_op jit(solution)/shard_map/ppermute | solution.py:34
  3.6 1.4 %shard_map.118 = (bf16[512,1536]{1,0:T(8,128)(2,1)S(1)}, f32[1,512]{1,0:T(1,128)S(1)}) custom-call(bf16[512,1536]{1,0:T(8,128)(2,1)} %qkv_hbm.1, f32[1,512]{1,0:T(1,128)} %bitcast.136), custom_call_target="tpu_custom_call" | custom-call | tf_op jit(solution)/shard_map/pallas_call | solution.py:384
  5.1 0.1 pad_maximum_fusion.18
  5.1 10.6 %conditional.2 = (bf16[12,2,24,512]{3,2,1,0:T(8,128)(2,1)S(1)}, bf16[576,512]{1,0:T(8,128)(2,1)S(1)}, bf16[576,1536]{1,0:T(8,128)(2,1)S(1)}) conditional(s32[]{:T(128)} %bitcast.40, (s32[2,3]{1,0:T(2,128)S(1)}, bf16[12,2,24,512]{3,2,1,0:T(8,128)(2,1)S(1)}, f32[1,512]{1,0:T(1,128)S(1)}, ...), branch_computations={%region_0.1_spmd, %region_1.2_spmd, %region_2.3_spmd, %region_3.4_... | conditional | flops 906264576 | bytes 7667816 | solution.py:479
  5.2 5.6 %collective-permute-start.15 = (bf16[1,2,24,512]{3,2,1,0:T(8,128)(2,1)S(1)}, bf16[1,2,24,512]{3,2,1,0:T(8,128)(2,1)S(1)}, u32[]{:S(2)}, u32[]{:S(2)}) collective-permute-start(bf16[1,2,24,512]{3,2,1,0:T(8,128)(2,1)S(1)} %slice.170), channel_id=1, source_target_pairs={{0,14},{1,15},{2,0},{3,1},{4,2},{5,3},{6,4},{7,5},{8,6},{9,7},{10,... | collective-permute-start | bytes 147464 | tf_op jit(solution)/shard_map/cond/branch_11_fun/ppermute | solution.py:29
  10.8 1.7 %collective-permute-done.15 = bf16[1,2,24,512]{3,2,1,0:T(8,128)(2,1)S(1)} collective-permute-done((bf16[1,2,24,512]{3,2,1,0:T(8,128)(2,1)S(1)}, bf16[1,2,24,512]{3,2,1,0:T(8,128)(2,1)S(1)}, u32[]{:S(2)}, u32[]{:S(2)}) %collective-permute-start.15) | collective-permute-done | bytes 49184 | tf_op jit(solution)/shard_map/cond/branch_11_fun/ppermute | solution.py:29
  12.5 0.1 pad_maximum_fusion.10.x_ref
  12.6 3.1 %branch_11_fun.1 = (bf16[576,512]{1,0:T(8,128)(2,1)S(1)}, bf16[576,1536]{1,0:T(8,128)(2,1)S(1)}) custom-call(s32[2,3]{1,0:T(2,128)S(1)} %get-tuple-element.232.shift_ref, bf16[12,2,24,512]{3,2,1,0:T(8,128)(2,1)S(1)} %pad_maximum_fusion.10.x_ref, f32[1,512]{1,0:T(1,128)S(1)} %get-tuple-element.234.gain_ref, bf16[512,1536]{1,0:T(8,128)(2,1)S(1)} %get-tuple-element.235.qkv_ref), custom_call_target="tpu_custom_call" | custom-call | flops 905969664 | bytes 2949120 | tf_op jit(solution)/shard_map/cond/branch_11_fun/pallas_call | solution.py:384
  15.7 5.3 %shard_map.119 = bf16[12,2,24,512]{3,2,1,0:T(8,128)(2,1)S(1)} custom-call(s32[2,3]{1,0:T(2,128)S(1)} %get-tuple-element.251.shift_ref, bf16[12,2,24,512]{3,2,1,0:T(8,128)(2,1)S(1)} %get-tuple-element.258.r_ref, bf16[576,512]{1,0:T(8,128)(2,1)S(1)} %get-tuple-element.259.xw_ref, bf16[576,1536]{1,0:T(8,128)(2,1)S(1)} %get-tuple-element.260.qkv, ...), custom_call_target="tpu_custom_call" | custom-call | tf_op jit(solution)/shard_map/pallas_call | solution.py:384
  21.0 0.0 copy-start.3
  21.0 7.5 %conditional.3 = (bf16[12,2,24,512]{3,2,1,0:T(8,128)(2,1)S(1)}) conditional(s32[]{:T(128)} %bitcast.39, bf16[12,2,24,512]{3,2,1,0:T(8,128)(2,1)S(1)} %shard_map.119, bf16[12,2,24,512]{3,2,1,0:T(8,128)(2,1)S(1)} %shard_map.119, bf16[12,2,24,512]{3,2,1,0:T(8,128)(2,1)S(1)} %shard_map.119, ...), branch_computations={%region_12.13_spmd, %region_13.14_spmd, %region_14.15_spmd, %regio... | conditional | flops 1179648 | bytes 5013632 | solution.py:518
  21.1 0.1 collective-permute-start.34
  21.2 0.3 collective-permute-start.32
  21.5 0.4 collective-permute-start.33
  21.9 6.5 %collective-permute-done.32 = bf16[1,24,512]{2,1,0:T(8,128)(2,1)S(1)} collective-permute-done((bf16[1,24,512]{2,1,0:T(8,128)(2,1)S(1)}, bf16[1,24,512]{2,1,0:T(8,128)(2,1)S(1)}, u32[]{:S(2)}, u32[]{:S(2)}) %collective-permute-start.32) | collective-permute-done | bytes 24608 | tf_op jit(solution)/shard_map/cond/branch_13_fun/ppermute | solution.py:29
  28.4 0.0 collective-permute-done.33
  28.4 0.1 maximum_maximum_fusion.5
  28.5 0.1 copy.56
  28.5 0.0 copy-start.1
  28.6 0.0 copy-start.2
  28.6 2.0 %shard_map.120 = (bf16[6,2,24,512]{3,2,1,0:T(8,128)(2,1)S(1)}, bf16[6,2,24,512]{3,2,1,0:T(8,128)(2,1)S(1)}, bf16[6,24,512]{2,1,0:T(8,128)(2,1)S(1)}) custom-call(bf16[12,2,24,512]{3,2,1,0:T(8,128)(2,1)S(1)} %get-tuple-element.264.f_ref, f32[1,2048]{1,0:T(1,128)S(1)} %bitcast.113, bf16[2048,512]{1,0:T(8,128)(2,1)} %mw_hbm.1), custom_call_target="tpu_custom_call" | custom-call | tf_op jit(solution)/shard_map/pallas_call | solution.py:384
  30.6 2.7 %collective-permute-start.45 = (bf16[6,24,512]{2,1,0:T(8,128)(2,1)S(1)}, bf16[6,24,512]{2,1,0:T(8,128)(2,1)S(1)}, u32[]{:S(2)}, u32[]{:S(2)}) collective-permute-start(bf16[6,24,512]{2,1,0:T(8,128)(2,1)S(1)} %get-tuple-element.261.own_ref), channel_id=1, source_target_pairs={{0,12},{1,13},{2,14},{3,15},{4,0},{5,1},{6,2},{7,3},{8,4},{9,5},{1... | collective-permute-start | bytes 442376 | tf_op jit(solution)/shard_map/ppermute | solution.py:29
  33.3 2.9 %collective-permute-start.43 = (bf16[6,24,512]{2,1,0:T(8,128)(2,1)S(1)}, bf16[6,24,512]{2,1,0:T(8,128)(2,1)S(1)}, u32[]{:S(2)}, u32[]{:S(2)}) collective-permute-start(bf16[6,24,512]{2,1,0:T(8,128)(2,1)S(1)} %get-tuple-element.261.own_ref), channel_id=1, source_target_pairs={{0,14},{1,15},{2,4},{3,5},{4,2},{5,3},{6,8},{7,9},{8,6},{9,7},{10,... | collective-permute-start | bytes 442376 | tf_op jit(solution)/shard_map/ppermute | solution.py:40
  36.3 1.3 %collective-permute-done.45.right_ref = bf16[6,24,512]{2,1,0:T(8,128)(2,1)S(1)} collective-permute-done((bf16[6,24,512]{2,1,0:T(8,128)(2,1)S(1)}, bf16[6,24,512]{2,1,0:T(8,128)(2,1)S(1)}, u32[]{:S(2)}, u32[]{:S(2)}) %collective-permute-start.45) | collective-permute-done | bytes 147488 | tf_op jit(solution)/shard_map/ppermute | solution.py:29
  37.6 4.2 %collective-permute-done.44.left_ref = bf16[6,24,512]{2,1,0:T(8,128)(2,1)S(1)} collective-permute-done((bf16[6,24,512]{2,1,0:T(8,128)(2,1)S(1)}, bf16[6,24,512]{2,1,0:T(8,128)(2,1)S(1)}, u32[]{:S(2)}, u32[]{:S(2)}) %collective-permute-start.44) | collective-permute-done | bytes 147488 | tf_op jit(solution)/shard_map/ppermute | solution.py:29
  41.8 1.5 %collective-permute-done.43.outside_ref = bf16[6,24,512]{2,1,0:T(8,128)(2,1)S(1)} collective-permute-done((bf16[6,24,512]{2,1,0:T(8,128)(2,1)S(1)}, bf16[6,24,512]{2,1,0:T(8,128)(2,1)S(1)}, u32[]{:S(2)}, u32[]{:S(2)}) %collective-permute-start.43) | collective-permute-done | bytes 147488 | tf_op jit(solution)/shard_map/ppermute | solution.py:40
  43.3 1.1 %collective-permute-done.42.inside_ref = bf16[6,24,512]{2,1,0:T(8,128)(2,1)S(1)} collective-permute-done((bf16[6,24,512]{2,1,0:T(8,128)(2,1)S(1)}, bf16[6,24,512]{2,1,0:T(8,128)(2,1)S(1)}, u32[]{:S(2)}, u32[]{:S(2)}) %collective-permute-start.42) | collective-permute-done | bytes 147488 | tf_op jit(solution)/shard_map/ppermute | solution.py:40
  44.5 3.9 %shard_map.121.own_ref = bf16[6,24,512]{2,1,0:T(8,128)(2,1)S(1)} custom-call(s32[2,3]{1,0:T(2,128)S(1)} %get-tuple-element.251.shift_ref, bf16[6,24,512]{2,1,0:T(8,128)(2,1)S(1)} %get-tuple-element.261.own_ref, bf16[6,24,512]{2,1,0:T(8,128)(2,1)S(1)} %collective-permute-done.42.inside_ref, bf16[6,24,512]{2,1,0:T(8,128)(2,1)S(1)} %collective-permute-done.43.outside_ref, ...), custom_call_target="tpu_custom_call" | custom-call | tf_op jit(solution)/shard_map/pallas_call | solution.py:384
  48.4 0.1 collective-permute-start.46
  48.4 1.4 %collective-permute-done.46.other_ref = bf16[6,24,512]{2,1,0:T(8,128)(2,1)S(1)} collective-permute-done((bf16[6,24,512]{2,1,0:T(8,128)(2,1)S(1)}, bf16[6,24,512]{2,1,0:T(8,128)(2,1)S(1)}, u32[]{:S(2)}, u32[]{:S(2)}) %collective-permute-start.46) | collective-permute-done | bytes 147488 | tf_op jit(solution)/shard_map/ppermute | solution.py:34
  49.8 2.2 %shard_map.122 = bf16[4,6,24,512]{3,2,1,0:T(8,128)(2,1)} custom-call(s32[2,3]{1,0:T(2,128)S(1)} %get-tuple-element.251.shift_ref, bf16[6,24,512]{2,1,0:T(8,128)(2,1)S(1)} %shard_map.121.own_ref, bf16[6,24,512]{2,1,0:T(8,128)(2,1)S(1)} %collective-permute-done.46.other_ref, bf16[6,2,24,512]{3,2,1,0:T(8,128)(2,1)S(1)} %get-tuple-element.262.fkeep_ref, ...), custom_call_target="tpu_custom_call" | custom-call | tf_op jit(solution)/shard_map/pallas_call | solution.py:384
  (20 shorter events, 0.2 us)
Async XLA Ops:
  1.7 3.3 %collective-permute-start.41 = (bf16[6,2,24,512]{3,2,1,0:T(8,128)(2,1)S(1)}, bf16[6,2,24,512]{3,2,1,0:T(8,128)(2,1)S(1)}, u32[]{:S(2)}, u32[]{:S(2)}) collective-permute-start(bf16[6,2,24,512]{3,2,1,0:T(8,128)(2,1)S(1)} %get-tuple-element.255), channel_id=1, source_target_pairs={{0,1},{1,0},{2,3},{3,2},{4,5},{5,4},{6,7},{7,6},{8,9},{9,8},{10,11... | collective-permute-start | bytes 884744 | tf_op jit(solution)/shard_map/ppermute | solution.py:34
  5.2 7.3 %collective-permute-start.15 = (bf16[1,2,24,512]{3,2,1,0:T(8,128)(2,1)S(1)}, bf16[1,2,24,512]{3,2,1,0:T(8,128)(2,1)S(1)}, u32[]{:S(2)}, u32[]{:S(2)}) collective-permute-start(bf16[1,2,24,512]{3,2,1,0:T(8,128)(2,1)S(1)} %slice.170), channel_id=1, source_target_pairs={{0,14},{1,15},{2,0},{3,1},{4,2},{5,3},{6,4},{7,5},{8,6},{9,7},{10,... | collective-permute-start | bytes 147464 | tf_op jit(solution)/shard_map/cond/branch_11_fun/ppermute | solution.py:29
  21.0 7.6 %copy-start.3 = (f32[2048]{0:T(1024)S(1)}, f32[2048]{0:T(1024)}, u32[]{:S(2)}) copy-start(f32[2048]{0:T(1024)} %param.43) | copy-start | bytes 24580
  21.1 7.3 %collective-permute-start.34 = (bf16[11,24,512]{2,1,0:T(8,128)(2,1)S(1)}, bf16[11,24,512]{2,1,0:T(8,128)(2,1)S(1)}, u32[]{:S(2)}, u32[]{:S(2)}) collective-permute-start(bf16[11,24,512]{2,1,0:T(8,128)(2,1)S(1)} %get-tuple-element.290), channel_id=1, source_target_pairs={{0,1},{1,0},{2,3},{3,2},{4,5},{5,4},{6,7},{7,6},{8,9},{9,8},{10,11... | collective-permute-start | bytes 811016 | tf_op jit(solution)/shard_map/cond/branch_13_fun/ppermute | solution.py:34
  21.2 7.2 %collective-permute-start.32 = (bf16[1,24,512]{2,1,0:T(8,128)(2,1)S(1)}, bf16[1,24,512]{2,1,0:T(8,128)(2,1)S(1)}, u32[]{:S(2)}, u32[]{:S(2)}) collective-permute-start(bf16[1,24,512]{2,1,0:T(8,128)(2,1)S(1)} %get-tuple-element.287), channel_id=1, source_target_pairs={{0,2},{1,3},{2,4},{3,5},{4,6},{5,7},{6,8},{7,9},{8,10},{9,11},{10,... | collective-permute-start | bytes 73736 | tf_op jit(solution)/shard_map/cond/branch_13_fun/ppermute | solution.py:29
  21.5 6.9 %collective-permute-start.33 = (bf16[1,24,512]{2,1,0:T(8,128)(2,1)S(1)}, bf16[1,24,512]{2,1,0:T(8,128)(2,1)S(1)}, u32[]{:S(2)}, u32[]{:S(2)}) collective-permute-start(bf16[1,24,512]{2,1,0:T(8,128)(2,1)S(1)} %get-tuple-element.288), channel_id=1, source_target_pairs={{0,3},{1,2},{2,5},{3,4},{4,7},{5,6},{6,9},{7,8},{8,11},{9,10},{10,... | collective-permute-start | bytes 73736 | tf_op jit(solution)/shard_map/cond/branch_13_fun/ppermute | solution.py:29
  28.5 15.9 %copy-start.1 = (bf16[512,1536]{1,0:T(8,128)(2,1)S(1)}, bf16[512,1536]{1,0:T(8,128)(2,1)}, u32[]{:S(2)}) copy-start(bf16[512,1536]{1,0:T(8,128)(2,1)} %qkv_ref.1) | copy-start | bytes 4718596
  28.6 15.9 %copy-start.2 = (bf16[512,512]{1,0:T(8,128)(2,1)S(1)}, bf16[512,512]{1,0:T(8,128)(2,1)}, u32[]{:S(2)}) copy-start(bf16[512,512]{1,0:T(8,128)(2,1)} %proj_ref.1) | copy-start | bytes 1572868
  28.6 15.9 %copy-start.5 = (f32[512]{0:T(512)S(1)}, f32[512]{0:T(512)}, u32[]{:S(2)}) copy-start(f32[512]{0:T(512)} %param.45) | copy-start | bytes 6148
  30.6 19.2 %copy-start = (bf16[512,2048]{1,0:T(8,128)(2,1)S(1)}, bf16[512,2048]{1,0:T(8,128)(2,1)}, u32[]{:S(2)}) copy-start(bf16[512,2048]{1,0:T(8,128)(2,1)} %weight_ref.1) | copy-start | bytes 6291460
  30.6 19.2 %copy-start.4 = (f32[512]{0:T(512)S(1)}, f32[512]{0:T(512)}, u32[]{:S(2)}) copy-start(f32[512]{0:T(512)} %param.49) | copy-start | bytes 6148
  30.6 7.0 %collective-permute-start.45 = (bf16[6,24,512]{2,1,0:T(8,128)(2,1)S(1)}, bf16[6,24,512]{2,1,0:T(8,128)(2,1)S(1)}, u32[]{:S(2)}, u32[]{:S(2)}) collective-permute-start(bf16[6,24,512]{2,1,0:T(8,128)(2,1)S(1)} %get-tuple-element.261.own_ref), channel_id=1, source_target_pairs={{0,12},{1,13},{2,14},{3,15},{4,0},{5,1},{6,2},{7,3},{8,4},{9,5},{1... | collective-permute-start | bytes 442376 | tf_op jit(solution)/shard_map/ppermute | solution.py:29
  33.3 8.5 %collective-permute-start.44 = (bf16[6,24,512]{2,1,0:T(8,128)(2,1)S(1)}, bf16[6,24,512]{2,1,0:T(8,128)(2,1)S(1)}, u32[]{:S(2)}, u32[]{:S(2)}) collective-permute-start(bf16[6,24,512]{2,1,0:T(8,128)(2,1)S(1)} %get-tuple-element.261.own_ref), channel_id=1, source_target_pairs={{0,4},{1,5},{2,6},{3,7},{4,8},{5,9},{6,10},{7,11},{8,12},{9,13},{1... | collective-permute-start | bytes 442376 | tf_op jit(solution)/shard_map/ppermute | solution.py:29
  33.3 10.0 %collective-permute-start.43 = (bf16[6,24,512]{2,1,0:T(8,128)(2,1)S(1)}, bf16[6,24,512]{2,1,0:T(8,128)(2,1)S(1)}, u32[]{:S(2)}, u32[]{:S(2)}) collective-permute-start(bf16[6,24,512]{2,1,0:T(8,128)(2,1)S(1)} %get-tuple-element.261.own_ref), channel_id=1, source_target_pairs={{0,14},{1,15},{2,4},{3,5},{4,2},{5,3},{6,8},{7,9},{8,6},{9,7},{10,... | collective-permute-start | bytes 442376 | tf_op jit(solution)/shard_map/ppermute | solution.py:40
  36.3 8.2 %collective-permute-start.42 = (bf16[6,24,512]{2,1,0:T(8,128)(2,1)S(1)}, bf16[6,24,512]{2,1,0:T(8,128)(2,1)S(1)}, u32[]{:S(2)}, u32[]{:S(2)}) collective-permute-start(bf16[6,24,512]{2,1,0:T(8,128)(2,1)S(1)} %get-tuple-element.261.own_ref), channel_id=1, source_target_pairs={{0,2},{1,3},{2,0},{3,1},{4,6},{5,7},{6,4},{7,5},{8,10},{9,11},{10,... | collective-permute-start | bytes 442376 | tf_op jit(solution)/shard_map/ppermute | solution.py:40
  36.3 13.5 %collective-permute-start.47 = (bf16[6,2,24,512]{3,2,1,0:T(8,128)(2,1)S(1)}, bf16[6,2,24,512]{3,2,1,0:T(8,128)(2,1)S(1)}, u32[]{:S(2)}, u32[]{:S(2)}) collective-permute-start(bf16[6,2,24,512]{3,2,1,0:T(8,128)(2,1)S(1)} %get-tuple-element.263), channel_id=1, source_target_pairs={{0,1},{1,0},{2,3},{3,2},{4,5},{5,4},{6,7},{7,6},{8,9},{9,8},{10,11... | collective-permute-start | bytes 884744 | tf_op jit(solution)/shard_map/ppermute | solution.py:34
  48.4 1.4 %collective-permute-start.46 = (bf16[6,24,512]{2,1,0:T(8,128)(2,1)S(1)}, bf16[6,24,512]{2,1,0:T(8,128)(2,1)S(1)}, u32[]{:S(2)}, u32[]{:S(2)}) collective-permute-start(bf16[6,24,512]{2,1,0:T(8,128)(2,1)S(1)} %shard_map.121.own_ref), channel_id=1, source_target_pairs={{0,1},{1,0},{2,3},{3,2},{4,5},{5,4},{6,7},{7,6},{8,9},{9,8},{10,11... | collective-permute-start | bytes 442376 | tf_op jit(solution)/shard_map/ppermute | solution.py:34

commit v5 on v4

--- a/solution.py
+++ b/solution.py
@@ -24,9 +24,9 @@
 BF16 = jnp.bfloat16
 
 
-def permuted(value, steps, flip=0):
+def permuted(value, steps):
     count = lax.axis_size("lon")
-    return lax.ppermute(value, "lon", [(s, (s + steps) % count ^ flip) for s in range(count)])
+    return lax.ppermute(value, "lon", [(s, (s + steps) % count) for s in range(count)])
 
 
 def swapped(value):
@@ -153,7 +153,7 @@
         load.wait()
 
 
-def own_kernel(shift_ref, x_ref, gain_ref, qkv_ref, xw_ref, out_ref, xs):
+def own_kernel(shift_ref, x_ref, gain_ref, qkv_ref, xw_ref, out_ref, xs, *, unroll):
     cols, slots, rows, _ = x_ref.shape
     unit = slots * cols
     size = WIN_LAT * unit
@@ -161,7 +161,7 @@
     by_window([reader(x_ref, col) for col in range(cols)], xs)
     gain = gain_ref[...]
 
-    @pl.loop(0, rows // WIN_LAT)
+    @pl.loop(0, rows // WIN_LAT, unroll=unroll)
     def _(j):
         at = pl.ds(pl.multiple_of(j * size, size), size)
         tokens = take(xs, pl.multiple_of(((j + 1) * WIN_LAT - b) * unit, 8), size)
@@ -460,7 +460,7 @@
                 right = permuted(grid[cols - c :], 2)
                 around = jnp.concatenate([left, right], axis=0)
             own = call(
-                own_kernel,
+                functools.partial(own_kernel, unroll=not FEW < c < WIN_LON - FEW),
                 (pltpu.VMEM((tokens_n, feats), BF16), pltpu.VMEM((tokens_n, 3 * feats), BF16)),
                 [chunked(tokens_n + size, feats)],
                 (table, grid, gain, own_w),
@@ -496,20 +496,13 @@
 
     def returned(c, crossed):
         def run(fine):
-            first, last = (cols - c, cols) if c > FEW else (0, cols - c)
-            held = fine[first:last]
-            moved = fine[:first] if c > FEW else fine[last:]
-            steps = 2 if c > FEW else -2
+            if c > FEW:
+                fine = jnp.concatenate([permuted(fine[: cols - c], 2), fine[cols - c :]], axis=0)
+            elif c > 0:
+                fine = jnp.concatenate([fine[: cols - c], permuted(fine[cols - c :], -2)], axis=0)
             if crossed:
-                held = jnp.stack([held[:, 0], swapped(held[:, 1])], axis=1)
-            if c == 0:
-                return held
-            if crossed:
-                moved = [permuted(moved[:, 0], steps), permuted(moved[:, 1], steps, 1)]
-                moved = jnp.stack(moved, axis=1)
-            else:
-                moved = permuted(moved, steps)
-            return jnp.concatenate([moved, held] if c > FEW else [held, moved], axis=0)
+                fine = jnp.stack([fine[:, 0], swapped(fine[:, 1])], axis=1)
+            return fine
 
         return run
 

time: 52.2 us -> 53.2 us (1.019)
  waiting for transfers between devices: 17.8 us -> 19.8 us
  Pallas kernels: 19.6 us -> 18.5 us
    ppermute x2, waiting for transfers between devices: 2.6 us -> 4.18 us  [paired(): lax.ppermute(value, 'lon', [(s, (s + steps[s]) % count) for s in range(co...]
    ppermute x4, waiting for transfers between devices: 1.37 us -> 2.93 us  [swapped(): return lax.ppermute(value, 'lon', [(s, s ^ 1) for s in range(count)])]
    ppermute x5 -> x4, waiting for transfers between devices: 13.8 us -> 12.6 us  [permuted(): lax.ppermute(value, 'lon', [(s, (s + steps) % count) for s in range(count)])]
    pallas_call x6, Pallas kernels: 17.9 us -> 16.8 us  [call(): pl.pallas_call(kernel, out_shape=outs, in_specs=specs, out_specs=jax.tree...]
    ppermute x5 -> x4, starting transfers between devices: 8.97 us -> 7.97 us  [permuted(): lax.ppermute(value, 'lon', [(s, (s + steps) % count) for s in range(count)])]
    ppermute x2, starting transfers between devices: 2.94 us -> 3.82 us  [paired(): lax.ppermute(value, 'lon', [(s, (s + steps[s]) % count) for s in range(co...]
  transfers between devices with their start and end apart: 11 -> 10, of which waited for: 7 -> 7; matrix products, arithmetic and copies ran while one was open for 0% -> 0% of each run, Pallas kernels for 10% -> 10%
where the time goes in v5:
time: 53.2 us; the launch traced here: 53 us
  waiting for transfers between devices  19.8 us (37%)
  Pallas kernels  18.5 us (35%)
  starting transfers between devices  12.5 us (23%)
  between operations  1.5 us (3%)
    pallas_call x6, Pallas kernels, call(): pl.pallas_call(kernel, out_shape=outs, in_specs=specs, out_specs=jax.tree...  16.8 us
    ppermute x4, waiting for transfers between devices, permuted(): lax.ppermute(value, 'lon', [(s, (s + steps) % count) for s in range(count)])  12.6 us
    ppermute x4, starting transfers between devices, permuted(): lax.ppermute(value, 'lon', [(s, (s + steps) % count) for s in range(count)])  7.97 us
    ppermute x2, waiting for transfers between devices, paired(): lax.ppermute(value, 'lon', [(s, (s + steps[s]) % count) for s in range(co...  4.18 us
    ppermute x2, starting transfers between devices, paired(): lax.ppermute(value, 'lon', [(s, (s + steps[s]) % count) for s in range(co...  3.82 us
    ppermute x4, waiting for transfers between devices, swapped(): return lax.ppermute(value, 'lon', [(s, s ^ 1) for s in range(count)])  2.93 us
    pallas_call x1, Pallas kernels, local(): pl.pallas_call(split_kernel, name='split', out_shape=(vhalf, vhalf, one,...  1.7 us
  transfers between devices with their start and end apart: 10, of which 7 were waited for; matrix products, arithmetic and copies ran while one was open for 0% of the time, Pallas kernels for 10%

profile of v5, /device:TPU:0, one launch (start us, length us, event | category | flops | bytes accessed | tf_op | source)
XLA Modules:
  0.0 53.0 jit_solution(685282959952141778)
XLA Ops:
  0.0 1.7 %split.1 = (bf16[6,2,24,512]{3,2,1,0:T(8,128)(2,1)S(1)}, bf16[6,2,24,512]{3,2,1,0:T(8,128)(2,1)S(1)}, s32[1]{0:T(128)}, s32[1]{0:T(128)}, s32[2,3]{1,0:T(2,128)S(1)}) custom-call(s32[2,3]{1,0:T(2,128)} %shift_ref.1, bf16[4,6,24,512]{3,2,1,0:T(8,128)(2,1)} %bitcast.44), custom_call_target="tpu_custom_call" | custom-call | tf_op jit(solution)/shard_map/split/pallas_call | solution.py:422
  1.7 0.6 %collective-permute-start.35 = (bf16[6,2,24,512]{3,2,1,0:T(8,128)(2,1)S(1)}, bf16[6,2,24,512]{3,2,1,0:T(8,128)(2,1)S(1)}, u32[]{:S(2)}, u32[]{:S(2)}) collective-permute-start(bf16[6,2,24,512]{3,2,1,0:T(8,128)(2,1)S(1)} %get-tuple-element.255), channel_id=1, source_target_pairs={{0,1},{1,0},{2,3},{3,2},{4,5},{5,4},{6,7},{7,6},{8,9},{9,8},{10,11... | collective-permute-start | bytes 884744 | tf_op jit(solution)/shard_map/ppermute | solution.py:34
  3.6 1.4 %shard_map.118 = (bf16[512,1536]{1,0:T(8,128)(2,1)S(1)}, f32[1,512]{1,0:T(1,128)S(1)}) custom-call(bf16[512,1536]{1,0:T(8,128)(2,1)} %qkv_hbm.1, f32[1,512]{1,0:T(1,128)} %bitcast.52), custom_call_target="tpu_custom_call" | custom-call | tf_op jit(solution)/shard_map/pallas_call | solution.py:384
  5.1 0.1 pad_maximum_fusion.24
  5.2 9.8 %conditional.2 = (bf16[12,2,24,512]{3,2,1,0:T(8,128)(2,1)S(1)}, bf16[576,512]{1,0:T(8,128)(2,1)S(1)}, bf16[576,1536]{1,0:T(8,128)(2,1)S(1)}) conditional(s32[]{:T(128)} %bitcast.16, (s32[2,3]{1,0:T(2,128)S(1)}, bf16[12,2,24,512]{3,2,1,0:T(8,128)(2,1)S(1)}, f32[1,512]{1,0:T(1,128)S(1)}, ...), branch_computations={%region_0.1_spmd, %region_1.2_spmd, %region_2.3_spmd, %region_3.4_... | conditional | flops 906264576 | bytes 7667816 | solution.py:479
  5.2 5.6 %collective-permute-start.15 = (bf16[1,2,24,512]{3,2,1,0:T(8,128)(2,1)S(1)}, bf16[1,2,24,512]{3,2,1,0:T(8,128)(2,1)S(1)}, u32[]{:S(2)}, u32[]{:S(2)}) collective-permute-start(bf16[1,2,24,512]{3,2,1,0:T(8,128)(2,1)S(1)} %slice.134), channel_id=1, source_target_pairs={{0,14},{1,15},{2,0},{3,1},{4,2},{5,3},{6,4},{7,5},{8,6},{9,7},{10,... | collective-permute-start | bytes 147464 | tf_op jit(solution)/shard_map/cond/branch_11_fun/ppermute | solution.py:29
  10.9 1.7 %collective-permute-done.15 = bf16[1,2,24,512]{3,2,1,0:T(8,128)(2,1)S(1)} collective-permute-done((bf16[1,2,24,512]{3,2,1,0:T(8,128)(2,1)S(1)}, bf16[1,2,24,512]{3,2,1,0:T(8,128)(2,1)S(1)}, u32[]{:S(2)}, u32[]{:S(2)}) %collective-permute-start.15) | collective-permute-done | bytes 49184 | tf_op jit(solution)/shard_map/cond/branch_11_fun/ppermute | solution.py:29
  12.6 0.1 pad_maximum_fusion.10.x_ref
  12.6 2.2 %branch_11_fun.1 = (bf16[576,512]{1,0:T(8,128)(2,1)S(1)}, bf16[576,1536]{1,0:T(8,128)(2,1)S(1)}) custom-call(s32[2,3]{1,0:T(2,128)S(1)} %get-tuple-element.232.shift_ref, bf16[12,2,24,512]{3,2,1,0:T(8,128)(2,1)S(1)} %pad_maximum_fusion.10.x_ref, f32[1,512]{1,0:T(1,128)S(1)} %get-tuple-element.234.gain_ref, bf16[512,1536]{1,0:T(8,128)(2,1)S(1)} %get-tuple-element.235.qkv_ref), custom_call_target="tpu_custom_call" | custom-call | flops 905969664 | bytes 2949120 | tf_op jit(solution)/shard_map/cond/branch_11_fun/pallas_call | solution.py:384
  15.0 5.1 %shard_map.119 = bf16[12,2,24,512]{3,2,1,0:T(8,128)(2,1)S(1)} custom-call(s32[2,3]{1,0:T(2,128)S(1)} %get-tuple-element.251.shift_ref, bf16[12,2,24,512]{3,2,1,0:T(8,128)(2,1)S(1)} %get-tuple-element.258.r_ref, bf16[576,512]{1,0:T(8,128)(2,1)S(1)} %get-tuple-element.259.xw_ref, bf16[576,1536]{1,0:T(8,128)(2,1)S(1)} %get-tuple-element.260.qkv, ...), custom_call_target="tpu_custom_call" | custom-call | tf_op jit(solution)/shard_map/pallas_call | solution.py:384
  20.1 0.0 copy-start.3
  20.1 9.1 %conditional.3 = (bf16[12,2,24,512]{3,2,1,0:T(8,128)(2,1)S(1)}) conditional(s32[]{:T(128)} %bitcast.15, bf16[12,2,24,512]{3,2,1,0:T(8,128)(2,1)S(1)} %shard_map.119, bf16[12,2,24,512]{3,2,1,0:T(8,128)(2,1)S(1)} %shard_map.119, bf16[12,2,24,512]{3,2,1,0:T(8,128)(2,1)S(1)} %shard_map.119, ...), branch_computations={%region_12.13_spmd, %region_13.14_spmd, %region_14.15_spmd, %regio... | conditional | flops 1179648 | bytes 7077976 | solution.py:511
  20.2 0.3 collective-permute-start.33
  20.5 6.9 %collective-permute-done.33 = bf16[1,2,24,512]{3,2,0,1:T(8,128)(2,1)S(1)} collective-permute-done((bf16[1,2,24,512]{3,2,0,1:T(8,128)(2,1)S(1)}, bf16[1,2,24,512]{3,2,0,1:T(8,128)(2,1)S(1)}, u32[]{:S(2)}, u32[]{:S(2)}) %collective-permute-start.33) | collective-permute-done | bytes 49184 | tf_op jit(solution)/shard_map/cond/branch_13_fun/ppermute | solution.py:29
  27.5 0.1 collective-permute-start.34
  27.6 1.6 %collective-permute-done.34 = bf16[12,24,512]{2,1,0:T(8,128)(2,1)S(1)} collective-permute-done((bf16[12,24,512]{2,1,0:T(8,128)(2,1)S(1)}, bf16[12,24,512]{2,1,0:T(8,128)(2,1)S(1)}, u32[]{:S(2)}, u32[]{:S(2)}) %collective-permute-start.34) | collective-permute-done | bytes 294944 | tf_op jit(solution)/shard_map/cond/branch_13_fun/ppermute | solution.py:34
  29.2 0.1 pad_maximum_fusion.23
  29.2 0.1 copy.48
  29.3 0.0 copy-start.1
  29.3 0.0 copy-start.2
  29.3 0.0 copy-start.5
  29.3 2.0 %shard_map.120 = (bf16[6,2,24,512]{3,2,1,0:T(8,128)(2,1)S(1)}, bf16[6,2,24,512]{3,2,1,0:T(8,128)(2,1)S(1)}, bf16[6,24,512]{2,1,0:T(8,128)(2,1)S(1)}) custom-call(bf16[12,2,24,512]{3,2,1,0:T(8,128)(2,1)S(1)} %get-tuple-element.264.f_ref, f32[1,2048]{1,0:T(1,128)S(1)} %bitcast.41, bf16[2048,512]{1,0:T(8,128)(2,1)} %mw_hbm.1), custom_call_target="tpu_custom_call" | custom-call | tf_op jit(solution)/shard_map/pallas_call | solution.py:384
  31.4 0.3 collective-permute-start.39
  31.7 1.8 %collective-permute-start.38 = (bf16[6,24,512]{2,1,0:T(8,128)(2,1)S(1)}, bf16[6,24,512]{2,1,0:T(8,128)(2,1)S(1)}, u32[]{:S(2)}, u32[]{:S(2)}) collective-permute-start(bf16[6,24,512]{2,1,0:T(8,128)(2,1)S(1)} %get-tuple-element.261.own_ref), channel_id=1, source_target_pairs={{0,4},{1,5},{2,6},{3,7},{4,8},{5,9},{6,10},{7,11},{8,12},{9,13},{1... | collective-permute-start | bytes 442376 | tf_op jit(solution)/shard_map/ppermute | solution.py:29
  33.4 3.8 %collective-permute-start.37 = (bf16[6,24,512]{2,1,0:T(8,128)(2,1)S(1)}, bf16[6,24,512]{2,1,0:T(8,128)(2,1)S(1)}, u32[]{:S(2)}, u32[]{:S(2)}) collective-permute-start(bf16[6,24,512]{2,1,0:T(8,128)(2,1)S(1)} %get-tuple-element.261.own_ref), channel_id=1, source_target_pairs={{0,14},{1,15},{2,4},{3,5},{4,2},{5,3},{6,8},{7,9},{8,6},{9,7},{10,... | collective-permute-start | bytes 442376 | tf_op jit(solution)/shard_map/ppermute | solution.py:40
  37.3 4.0 %collective-permute-done.39.right_ref = bf16[6,24,512]{2,1,0:T(8,128)(2,1)S(1)} collective-permute-done((bf16[6,24,512]{2,1,0:T(8,128)(2,1)S(1)}, bf16[6,24,512]{2,1,0:T(8,128)(2,1)S(1)}, u32[]{:S(2)}, u32[]{:S(2)}) %collective-permute-start.39) | collective-permute-done | bytes 147488 | tf_op jit(solution)/shard_map/ppermute | solution.py:29
  41.3 2.8 %collective-permute-done.37.outside_ref = bf16[6,24,512]{2,1,0:T(8,128)(2,1)S(1)} collective-permute-done((bf16[6,24,512]{2,1,0:T(8,128)(2,1)S(1)}, bf16[6,24,512]{2,1,0:T(8,128)(2,1)S(1)}, u32[]{:S(2)}, u32[]{:S(2)}) %collective-permute-start.37) | collective-permute-done | bytes 147488 | tf_op jit(solution)/shard_map/ppermute | solution.py:40
  44.1 1.4 %collective-permute-done.36.inside_ref = bf16[6,24,512]{2,1,0:T(8,128)(2,1)S(1)} collective-permute-done((bf16[6,24,512]{2,1,0:T(8,128)(2,1)S(1)}, bf16[6,24,512]{2,1,0:T(8,128)(2,1)S(1)}, u32[]{:S(2)}, u32[]{:S(2)}) %collective-permute-start.36) | collective-permute-done | bytes 147488 | tf_op jit(solution)/shard_map/ppermute | solution.py:40
  45.5 3.9 %shard_map.121.own_ref = bf16[6,24,512]{2,1,0:T(8,128)(2,1)S(1)} custom-call(s32[2,3]{1,0:T(2,128)S(1)} %get-tuple-element.251.shift_ref, bf16[6,24,512]{2,1,0:T(8,128)(2,1)S(1)} %get-tuple-element.261.own_ref, bf16[6,24,512]{2,1,0:T(8,128)(2,1)S(1)} %collective-permute-done.36.inside_ref, bf16[6,24,512]{2,1,0:T(8,128)(2,1)S(1)} %collective-permute-done.37.outside_ref, ...), custom_call_target="tpu_custom_call" | custom-call | tf_op jit(solution)/shard_map/pallas_call | solution.py:384
  49.4 0.1 collective-permute-start.40
  49.5 1.4 %collective-permute-done.40.other_ref = bf16[6,24,512]{2,1,0:T(8,128)(2,1)S(1)} collective-permute-done((bf16[6,24,512]{2,1,0:T(8,128)(2,1)S(1)}, bf16[6,24,512]{2,1,0:T(8,128)(2,1)S(1)}, u32[]{:S(2)}, u32[]{:S(2)}) %collective-permute-start.40) | collective-permute-done | bytes 147488 | tf_op jit(solution)/shard_map/ppermute | solution.py:34
  50.8 2.2 %shard_map.122 = bf16[4,6,24,512]{3,2,1,0:T(8,128)(2,1)} custom-call(s32[2,3]{1,0:T(2,128)S(1)} %get-tuple-element.251.shift_ref, bf16[6,24,512]{2,1,0:T(8,128)(2,1)S(1)} %shard_map.121.own_ref, bf16[6,24,512]{2,1,0:T(8,128)(2,1)S(1)} %collective-permute-done.40.other_ref, bf16[6,2,24,512]{3,2,1,0:T(8,128)(2,1)S(1)} %get-tuple-element.262.fkeep_ref, ...), custom_call_target="tpu_custom_call" | custom-call | tf_op jit(solution)/shard_map/pallas_call | solution.py:384
  (20 shorter events, 0.2 us)
Async XLA Ops:
  1.7 3.3 %collective-permute-start.35 = (bf16[6,2,24,512]{3,2,1,0:T(8,128)(2,1)S(1)}, bf16[6,2,24,512]{3,2,1,0:T(8,128)(2,1)S(1)}, u32[]{:S(2)}, u32[]{:S(2)}) collective-permute-start(bf16[6,2,24,512]{3,2,1,0:T(8,128)(2,1)S(1)} %get-tuple-element.255), channel_id=1, source_target_pairs={{0,1},{1,0},{2,3},{3,2},{4,5},{5,4},{6,7},{7,6},{8,9},{9,8},{10,11... | collective-permute-start | bytes 884744 | tf_op jit(solution)/shard_map/ppermute | solution.py:34
  5.2 7.3 %collective-permute-start.15 = (bf16[1,2,24,512]{3,2,1,0:T(8,128)(2,1)S(1)}, bf16[1,2,24,512]{3,2,1,0:T(8,128)(2,1)S(1)}, u32[]{:S(2)}, u32[]{:S(2)}) collective-permute-start(bf16[1,2,24,512]{3,2,1,0:T(8,128)(2,1)S(1)} %slice.134), channel_id=1, source_target_pairs={{0,14},{1,15},{2,0},{3,1},{4,2},{5,3},{6,4},{7,5},{8,6},{9,7},{10,... | collective-permute-start | bytes 147464 | tf_op jit(solution)/shard_map/cond/branch_11_fun/ppermute | solution.py:29
  20.1 9.2 %copy-start.3 = (f32[2048]{0:T(1024)S(1)}, f32[2048]{0:T(1024)}, u32[]{:S(2)}) copy-start(f32[2048]{0:T(1024)} %param.43) | copy-start | bytes 24580
  20.2 7.2 %collective-permute-start.33 = (bf16[1,2,24,512]{3,2,0,1:T(8,128)(2,1)S(1)}, bf16[1,2,24,512]{3,2,0,1:T(8,128)(2,1)S(1)}, u32[]{:S(2)}, u32[]{:S(2)}) collective-permute-start(bf16[1,2,24,512]{3,2,0,1:T(8,128)(2,1)S(1)} %slice_bitcast_fusion.11), channel_id=1, source_target_pairs={{0,2},{1,3},{2,4},{3,5},{4,6},{5,7},{6,8},{7,9},{8,10},{9,11},{10,... | collective-permute-start | bytes 147464 | tf_op jit(solution)/shard_map/cond/branch_13_fun/ppermute | solution.py:29
  27.5 1.6 %collective-permute-start.34 = (bf16[12,24,512]{2,1,0:T(8,128)(2,1)S(1)}, bf16[12,24,512]{2,1,0:T(8,128)(2,1)S(1)}, u32[]{:S(2)}, u32[]{:S(2)}) collective-permute-start(bf16[12,24,512]{2,1,0:T(8,128)(2,1)S(1)} %get-tuple-element.278), channel_id=1, source_target_pairs={{0,1},{1,0},{2,3},{3,2},{4,5},{5,4},{6,7},{7,6},{8,9},{9,8},{10,11... | collective-permute-start | bytes 884744 | tf_op jit(solution)/shard_map/cond/branch_13_fun/ppermute | solution.py:34
  29.3 16.2 %copy-start.1 = (bf16[512,1536]{1,0:T(8,128)(2,1)S(1)}, bf16[512,1536]{1,0:T(8,128)(2,1)}, u32[]{:S(2)}) copy-start(bf16[512,1536]{1,0:T(8,128)(2,1)} %qkv_ref.1) | copy-start | bytes 4718596
  29.3 16.2 %copy-start.2 = (bf16[512,512]{1,0:T(8,128)(2,1)S(1)}, bf16[512,512]{1,0:T(8,128)(2,1)}, u32[]{:S(2)}) copy-start(bf16[512,512]{1,0:T(8,128)(2,1)} %proj_ref.1) | copy-start | bytes 1572868
  29.3 16.2 %copy-start.5 = (f32[512]{0:T(512)S(1)}, f32[512]{0:T(512)}, u32[]{:S(2)}) copy-start(f32[512]{0:T(512)} %param.45) | copy-start | bytes 6148
  31.3 19.5 %copy-start = (bf16[512,2048]{1,0:T(8,128)(2,1)S(1)}, bf16[512,2048]{1,0:T(8,128)(2,1)}, u32[]{:S(2)}) copy-start(bf16[512,2048]{1,0:T(8,128)(2,1)} %weight_ref.1) | copy-start | bytes 6291460
  31.4 19.5 %copy-start.4 = (f32[512]{0:T(512)S(1)}, f32[512]{0:T(512)}, u32[]{:S(2)}) copy-start(f32[512]{0:T(512)} %param.49) | copy-start | bytes 6148
  31.4 9.9 %collective-permute-start.39 = (bf16[6,24,512]{2,1,0:T(8,128)(2,1)S(1)}, bf16[6,24,512]{2,1,0:T(8,128)(2,1)S(1)}, u32[]{:S(2)}, u32[]{:S(2)}) collective-permute-start(bf16[6,24,512]{2,1,0:T(8,128)(2,1)S(1)} %get-tuple-element.261.own_ref), channel_id=1, source_target_pairs={{0,12},{1,13},{2,14},{3,15},{4,0},{5,1},{6,2},{7,3},{8,4},{9,5},{1... | collective-permute-start | bytes 442376 | tf_op jit(solution)/shard_map/ppermute | solution.py:29
  31.7 9.6 %collective-permute-start.38 = (bf16[6,24,512]{2,1,0:T(8,128)(2,1)S(1)}, bf16[6,24,512]{2,1,0:T(8,128)(2,1)S(1)}, u32[]{:S(2)}, u32[]{:S(2)}) collective-permute-start(bf16[6,24,512]{2,1,0:T(8,128)(2,1)S(1)} %get-tuple-element.261.own_ref), channel_id=1, source_target_pairs={{0,4},{1,5},{2,6},{3,7},{4,8},{5,9},{6,10},{7,11},{8,12},{9,13},{1... | collective-permute-start | bytes 442376 | tf_op jit(solution)/shard_map/ppermute | solution.py:29
  33.4 10.7 %collective-permute-start.37 = (bf16[6,24,512]{2,1,0:T(8,128)(2,1)S(1)}, bf16[6,24,512]{2,1,0:T(8,128)(2,1)S(1)}, u32[]{:S(2)}, u32[]{:S(2)}) collective-permute-start(bf16[6,24,512]{2,1,0:T(8,128)(2,1)S(1)} %get-tuple-element.261.own_ref), channel_id=1, source_target_pairs={{0,14},{1,15},{2,4},{3,5},{4,2},{5,3},{6,8},{7,9},{8,6},{9,7},{10,... | collective-permute-start | bytes 442376 | tf_op jit(solution)/shard_map/ppermute | solution.py:40
  37.3 8.2 %collective-permute-start.36 = (bf16[6,24,512]{2,1,0:T(8,128)(2,1)S(1)}, bf16[6,24,512]{2,1,0:T(8,128)(2,1)S(1)}, u32[]{:S(2)}, u32[]{:S(2)}) collective-permute-start(bf16[6,24,512]{2,1,0:T(8,128)(2,1)S(1)} %get-tuple-element.261.own_ref), channel_id=1, source_target_pairs={{0,2},{1,3},{2,0},{3,1},{4,6},{5,7},{6,4},{7,5},{8,10},{9,11},{10,... | collective-permute-start | bytes 442376 | tf_op jit(solution)/shard_map/ppermute | solution.py:40
  37.3 13.5 %collective-permute-start.41 = (bf16[6,2,24,512]{3,2,1,0:T(8,128)(2,1)S(1)}, bf16[6,2,24,512]{3,2,1,0:T(8,128)(2,1)S(1)}, u32[]{:S(2)}, u32[]{:S(2)}) collective-permute-start(bf16[6,2,24,512]{3,2,1,0:T(8,128)(2,1)S(1)} %get-tuple-element.263), channel_id=1, source_target_pairs={{0,1},{1,0},{2,3},{3,2},{4,5},{5,4},{6,7},{7,6},{8,9},{9,8},{10,11... | collective-permute-start | bytes 884744 | tf_op jit(solution)/shard_map/ppermute | solution.py:34
  49.4 1.4 %collective-permute-start.40 = (bf16[6,24,512]{2,1,0:T(8,128)(2,1)S(1)}, bf16[6,24,512]{2,1,0:T(8,128)(2,1)S(1)}, u32[]{:S(2)}, u32[]{:S(2)}) collective-permute-start(bf16[6,24,512]{2,1,0:T(8,128)(2,1)S(1)} %shard_map.121.own_ref), channel_id=1, source_target_pairs={{0,1},{1,0},{2,3},{3,2},{4,5},{5,4},{6,7},{7,6},{8,9},{9,8},{10,11... | collective-permute-start | bytes 442376 | tf_op jit(solution)/shard_map/ppermute | solution.py:34
